TPU v7x, 32 devices: a whole 2x2x4 slice. The times are simulated.
32 devices in a mesh: dp: 8 (over y, x, core), fsdp: 4 (over z).
Axes of the slice: x: 2, y: 2, z: 4, core: 2. Of those that a mesh axis runs over, the one named last changes fastest.
Arguments:
- rows_in: bfloat16 [256, 32, 1024], P(None, ('dp', 'fsdp')), may hold values from -6 to 6
- cotangent: bfloat16 [256, 32, 1024], P(None, ('dp', 'fsdp')), may hold values from -6 to 6
- lengths: int32 [64], replicated, may hold values from 65 to 191, as said below
- deal_order: int32 [64], replicated, may hold values from 0 to 63, as said below
- w_qkv: bfloat16 [1024, 3072], P(('dp', 'fsdp')), may hold values from -0.25 to 0.25
- b_query: bfloat16 [1024], P(('dp', 'fsdp')), may hold values from -3 to 3
- b_value: bfloat16 [1024], P(('dp', 'fsdp')), may hold values from -3 to 3
- w_out: bfloat16 [1024, 1024], P(('dp', 'fsdp')), may hold values from -0.5 to 0.5
- b_out: bfloat16 [1024], P(('dp', 'fsdp')), may hold values from -3 to 3
- gain_one: bfloat16 [1024], P(('dp', 'fsdp')), may hold values from 0.5 to 1.5
- shift_one: bfloat16 [1024], P(('dp', 'fsdp')), may hold values from -2 to 2
- w_up: bfloat16 [1024, 4096], P(('dp', 'fsdp')), may hold values from -0.1875 to 0.1875
- b_up: bfloat16 [4096], P(('dp', 'fsdp')), may hold values from -3 to 3
- w_down: bfloat16 [4096, 1024], P(('dp', 'fsdp')), may hold values from -0.125 to 0.125
- b_down: bfloat16 [1024], P(('dp', 'fsdp')), may hold values from -3 to 3
- gain_two: bfloat16 [1024], P(('dp', 'fsdp')), may hold values from 0.5 to 1.5
- shift_two: bfloat16 [1024], P(('dp', 'fsdp')), may hold values from -2 to 2
Outputs:
- rows_out: bfloat16 [256, 32, 1024], P(None, ('dp', 'fsdp'))
- grad_rows: bfloat16 [256, 32, 1024], P(None, ('dp', 'fsdp'))
- grad_w_qkv: float32 [1024, 3072], P(('dp', 'fsdp'))
- grad_b_query: float32 [1024], P(('dp', 'fsdp'))
- grad_b_value: float32 [1024], P(('dp', 'fsdp'))
- grad_w_out: float32 [1024, 1024], P(('dp', 'fsdp'))
- grad_b_out: float32 [1024], P(('dp', 'fsdp'))
- grad_gain_one: float32 [1024], P(('dp', 'fsdp'))
- grad_shift_one: float32 [1024], P(('dp', 'fsdp'))
- grad_w_up: float32 [1024, 4096], P(('dp', 'fsdp'))
- grad_b_up: float32 [4096], P(('dp', 'fsdp'))
- grad_w_down: float32 [4096, 1024], P(('dp', 'fsdp'))
- grad_b_down: float32 [1024], P(('dp', 'fsdp'))
- grad_gain_two: float32 [1024], P(('dp', 'fsdp'))
- grad_shift_two: float32 [1024], P(('dp', 'fsdp'))
Inputs may be any that keep to these rules, and one draw needn't show every extreme that they name: `lengths`: they sum to 8192; sequences deal_order[2 i] and deal_order[2 i + 1] hold 256 tokens together for every i, so at most 9 rows of one device belong to the two sequences of another. `deal_order`: A permutation of the sequences.
All inputs are finite; a program needn't handle non-finite values.
Results may differ from a plain program's by a relative error of at most 0.014.
Values may be sent and summed in bfloat16 or wider, within the bound.
No kernel may reach another device: no remote copies, remote signals or barrier semaphores. Data moves between devices by JAX's collectives and lax.ppermute only.
A program may use at most 192 MiB of HBM per device.

v0:
```python
from functools import partial

import jax
import jax.numpy as jnp
from jax import lax
from jax.sharding import PartitionSpec as P

HEADS = 16
HEAD_DIM = 64


EPSILON = 1e-05


def layer_norm(values, gain_row, shift_row):
    row_mean = jnp.mean(values, axis=-1, keepdims=True)
    centered = values - row_mean
    spread = jnp.mean(centered * centered, axis=-1, keepdims=True)
    return centered * lax.rsqrt(spread + EPSILON) * gain_row + shift_row


def lookup(small_table, index_rows):
    matches = index_rows[:, None] == jnp.arange(small_table.shape[0], dtype=jnp.int32)[None, :]
    return jnp.sum(jnp.where(matches, small_table[None, :], 0), axis=1)


def rank_among(group_label, order_key):
    earlier = (group_label[None, :] == group_label[:, None]) & (
        order_key[None, :] < order_key[:, None]
    )
    return jnp.sum(earlier.astype(jnp.int32), axis=1)


def routing(lengths, deal_order, devices, row_count, device):
    slot_count = deal_order.shape[0]
    slot_ids = jnp.arange(slot_count, dtype=jnp.int32)
    starts = jnp.cumsum(lengths) - lengths
    slot_of = jnp.sum(
        jnp.where(deal_order[None, :] == slot_ids[:, None], slot_ids[None, :], 0), axis=1
    )
    slot_lengths = lookup(lengths, deal_order)
    slot_rows = row_count // devices + 1
    local_rows = jnp.arange(row_count, dtype=jnp.int32)
    token_index = local_rows * devices + device
    sequence = jnp.sum((starts[None, :] <= token_index[:, None]).astype(jnp.int32), axis=1) - 1
    slot_index = lookup(slot_of, sequence)
    target = slot_index // 2
    send_at = target * slot_rows + rank_among(target, local_rows)
    first_len = lax.dynamic_index_in_dim(slot_lengths, 2 * device, 0, False)
    second = local_rows >= first_len
    first_seq = lax.dynamic_index_in_dim(deal_order, 2 * device, 0, False)
    second_seq = lax.dynamic_index_in_dim(deal_order, 2 * device + 1, 0, False)
    sequence_here = jnp.where(second, second_seq, first_seq)
    position = local_rows - jnp.where(second, first_len, 0)
    source_token = lookup(starts, sequence_here) + position
    source = source_token % devices
    take_at = source * slot_rows + rank_among(source, source_token)
    return (send_at, take_at, second.astype(jnp.int32), position, slot_rows)


def outer_sum(left, right):
    return lax.dot_general(
        left, right, (((0,), (0,)), ((), ())), preferred_element_type=jnp.float32
    )


def back_dot(grad_rows, weight):
    return lax.dot_general(
        grad_rows, weight, (((1,), (1,)), ((), ())), preferred_element_type=jnp.float32
    )


def masked_scores(query_b, key_b, allowed, scale_factor):
    raw_scores = (
        jnp.einsum("qhd,khd->hqk", query_b, key_b, preferred_element_type=jnp.float32)
        * scale_factor
    )
    return jnp.where(allowed[None, :, :], raw_scores, -1000000000.0)


def on_device(
    rows_in,
    cotangent,
    lengths,
    deal_order,
    w_qkv,
    b_query,
    b_value,
    w_out,
    b_out,
    gain_one,
    shift_one,
    w_up,
    b_up,
    w_down,
    b_down,
    gain_two,
    shift_two,
):
    devices = lax.axis_size(("dp", "fsdp"))
    device = lax.axis_index(("dp", "fsdp"))
    row_count = rows_in.shape[0]
    model_width = rows_in.shape[2]
    send_at, take_at, segment, position, slot_rows = routing(
        lengths, deal_order, devices, row_count, device
    )
    blank_rows = jnp.zeros((devices * slot_rows, model_width), jnp.bfloat16)
    flat_in = rows_in.reshape(row_count, model_width)
    flat_cot = cotangent.reshape(row_count, model_width)
    arrived_rows, arrived_cot = (
        lax.all_to_all(
            blank_rows.at[send_at].set(flat_in),
            ("dp", "fsdp"),
            split_axis=0,
            concat_axis=0,
            tiled=True,
        ),
        lax.all_to_all(
            blank_rows.at[send_at].set(flat_cot),
            ("dp", "fsdp"),
            split_axis=0,
            concat_axis=0,
            tiled=True,
        ),
    )
    inputs = arrived_rows[take_at].astype(jnp.float32)
    grad_out = arrived_cot[take_at].astype(jnp.float32)
    attn_full = (
        lax.all_gather(w_qkv, ("dp", "fsdp"), axis=0, tiled=True),
        lax.all_gather(w_out, ("dp", "fsdp"), axis=0, tiled=True),
        lax.all_gather(b_query, ("dp", "fsdp"), axis=0, tiled=True),
        lax.all_gather(b_value, ("dp", "fsdp"), axis=0, tiled=True),
        lax.all_gather(b_out, ("dp", "fsdp"), axis=0, tiled=True),
        lax.all_gather(gain_one, ("dp", "fsdp"), axis=0, tiled=True),
        lax.all_gather(shift_one, ("dp", "fsdp"), axis=0, tiled=True),
    )
    mlp_full = (
        lax.all_gather(w_up, ("dp", "fsdp"), axis=0, tiled=True),
        lax.all_gather(w_down, ("dp", "fsdp"), axis=0, tiled=True),
        lax.all_gather(b_up, ("dp", "fsdp"), axis=0, tiled=True),
        lax.all_gather(b_down, ("dp", "fsdp"), axis=0, tiled=True),
        lax.all_gather(gain_two, ("dp", "fsdp"), axis=0, tiled=True),
        lax.all_gather(shift_two, ("dp", "fsdp"), axis=0, tiled=True),
    )
    full_qkv, full_out, full_bq, full_bv, full_bo, full_g1, full_s1 = attn_full
    full_up, full_down, full_bu, full_bd, full_g2, full_s2 = mlp_full
    gain_one_f = full_g1.astype(jnp.float32)
    shift_one_f = full_s1.astype(jnp.float32)
    gain_two_f = full_g2.astype(jnp.float32)
    shift_two_f = full_s2.astype(jnp.float32)
    normed_one_b = layer_norm(inputs, gain_one_f, shift_one_f).astype(jnp.bfloat16)
    mixed = jnp.dot(normed_one_b, full_qkv, preferred_element_type=jnp.float32)
    head_shape = (row_count, HEADS, HEAD_DIM)
    query_b = (
        (mixed[:, :model_width] + full_bq.astype(jnp.float32))
        .astype(jnp.bfloat16)
        .reshape(head_shape)
    )
    key_b = mixed[:, model_width : 2 * model_width].astype(jnp.bfloat16).reshape(head_shape)
    value_b = (
        (mixed[:, 2 * model_width :] + full_bv.astype(jnp.float32))
        .astype(jnp.bfloat16)
        .reshape(head_shape)
    )
    allowed = (segment[:, None] == segment[None, :]) & (position[None, :] <= position[:, None])
    scale_factor = HEAD_DIM ** (-0.5)
    masked = masked_scores(query_b, key_b, allowed, scale_factor)
    row_max = jnp.max(masked, axis=-1, keepdims=True)
    exps = jnp.exp(masked - row_max)
    row_total = jnp.sum(exps, axis=-1, keepdims=True)
    log_total = row_max + jnp.log(row_total)
    softmax_b = (exps / row_total).astype(jnp.bfloat16)
    attended_b = jnp.einsum("hqk,khd->qhd", softmax_b, value_b, preferred_element_type=jnp.float32)
    attended_b = attended_b.reshape(row_count, model_width).astype(jnp.bfloat16)
    hidden_one = (
        inputs
        + jnp.dot(attended_b, full_out, preferred_element_type=jnp.float32)
        + full_bo.astype(jnp.float32)
    )
    normed_two_b = layer_norm(hidden_one, gain_two_f, shift_two_f).astype(jnp.bfloat16)
    pre_act = jnp.dot(normed_two_b, full_up, preferred_element_type=jnp.float32) + full_bu.astype(
        jnp.float32
    )
    activation_b = jax.nn.gelu(pre_act, approximate=False).astype(jnp.bfloat16)
    result_rows = (
        hidden_one
        + jnp.dot(activation_b, full_down, preferred_element_type=jnp.float32)
        + full_bd.astype(jnp.float32)
    )
    returned = lax.all_to_all(
        blank_rows.at[take_at].set(result_rows.astype(jnp.bfloat16)),
        ("dp", "fsdp"),
        split_axis=0,
        concat_axis=0,
        tiled=True,
    )
    rows_out = returned[send_at].reshape(row_count, 1, model_width)
    mlp_back = (
        lax.all_gather(w_up, ("dp", "fsdp"), axis=0, tiled=True),
        lax.all_gather(w_down, ("dp", "fsdp"), axis=0, tiled=True),
        lax.all_gather(b_up, ("dp", "fsdp"), axis=0, tiled=True),
        lax.all_gather(b_down, ("dp", "fsdp"), axis=0, tiled=True),
        lax.all_gather(gain_two, ("dp", "fsdp"), axis=0, tiled=True),
        lax.all_gather(shift_two, ("dp", "fsdp"), axis=0, tiled=True),
    )
    back_up, back_down = (mlp_back[0], mlp_back[1])
    back_g2 = mlp_back[4].astype(jnp.float32)
    grad_m_b = grad_out.astype(jnp.bfloat16)
    term_w_down = outer_sum(activation_b, grad_m_b)
    term_b_down = jnp.sum(grad_m_b.astype(jnp.float32), axis=0)
    grad_w_down, grad_b_down = (
        lax.psum_scatter(term_w_down, ("dp", "fsdp"), scatter_dimension=0, tiled=True),
        lax.psum_scatter(term_b_down, ("dp", "fsdp"), scatter_dimension=0, tiled=True),
    )
    grad_act = back_dot(grad_m_b, back_down)
    gelu_pull = jax.vjp(partial(jax.nn.gelu, approximate=False), pre_act)[1]
    grad_pre_b = gelu_pull(grad_act)[0].astype(jnp.bfloat16)
    grad_normed_two = back_dot(grad_pre_b, back_up)
    norm_two_pull = jax.vjp(layer_norm, hidden_one, back_g2, shift_two_f)[1]
    grad_hidden_ln, grad_g2_rows, grad_s2_rows = norm_two_pull(grad_normed_two)
    term_w_up = outer_sum(normed_two_b, grad_pre_b)
    term_b_up = jnp.sum(grad_pre_b.astype(jnp.float32), axis=0)
    grad_w_up, grad_b_up, grad_gain_two, grad_shift_two = (
        lax.psum_scatter(term_w_up, ("dp", "fsdp"), scatter_dimension=0, tiled=True),
        lax.psum_scatter(term_b_up, ("dp", "fsdp"), scatter_dimension=0, tiled=True),
        lax.psum_scatter(grad_g2_rows, ("dp", "fsdp"), scatter_dimension=0, tiled=True),
        lax.psum_scatter(grad_s2_rows, ("dp", "fsdp"), scatter_dimension=0, tiled=True),
    )
    grad_hidden = grad_out + grad_hidden_ln
    grad_branch_b = grad_hidden.astype(jnp.bfloat16)
    attn_back = (
        lax.all_gather(w_qkv, ("dp", "fsdp"), axis=0, tiled=True),
        lax.all_gather(w_out, ("dp", "fsdp"), axis=0, tiled=True),
        lax.all_gather(b_query, ("dp", "fsdp"), axis=0, tiled=True),
        lax.all_gather(b_value, ("dp", "fsdp"), axis=0, tiled=True),
        lax.all_gather(b_out, ("dp", "fsdp"), axis=0, tiled=True),
        lax.all_gather(gain_one, ("dp", "fsdp"), axis=0, tiled=True),
        lax.all_gather(shift_one, ("dp", "fsdp"), axis=0, tiled=True),
    )
    back_qkv, back_out = (attn_back[0], attn_back[1])
    back_g1 = attn_back[5].astype(jnp.float32)
    grad_att_b = back_dot(grad_branch_b, back_out).astype(jnp.bfloat16).reshape(head_shape)
    masked_again = masked_scores(query_b, key_b, allowed, scale_factor)
    softmax_f = jnp.exp(masked_again - log_total)
    softmax_again_b = softmax_f.astype(jnp.bfloat16)
    grad_probs = jnp.einsum("qhd,khd->hqk", grad_att_b, value_b, preferred_element_type=jnp.float32)
    grad_scores_b = (
        softmax_f * (grad_probs - jnp.sum(softmax_f * grad_probs, axis=-1, keepdims=True))
    ).astype(jnp.bfloat16)
    grad_query_b = (
        jnp.einsum("hqk,khd->qhd", grad_scores_b, key_b, preferred_element_type=jnp.float32)
        * scale_factor
    ).astype(jnp.bfloat16)
    grad_key_b = (
        jnp.einsum("hqk,qhd->khd", grad_scores_b, query_b, preferred_element_type=jnp.float32)
        * scale_factor
    ).astype(jnp.bfloat16)
    grad_value_b = jnp.einsum(
        "hqk,qhd->khd", softmax_again_b, grad_att_b, preferred_element_type=jnp.float32
    ).astype(jnp.bfloat16)
    grad_mixed_b = jnp.concatenate(
        [
            grad_query_b.reshape(row_count, model_width),
            grad_key_b.reshape(row_count, model_width),
            grad_value_b.reshape(row_count, model_width),
        ],
        axis=1,
    )
    grad_normed_one = back_dot(grad_mixed_b, back_qkv)
    norm_one_pull = jax.vjp(layer_norm, inputs, back_g1, shift_one_f)[1]
    grad_input_ln, grad_g1_rows, grad_s1_rows = norm_one_pull(grad_normed_one)
    term_w_qkv = outer_sum(normed_one_b, grad_mixed_b)
    term_b_query = jnp.sum(grad_query_b.reshape(row_count, model_width).astype(jnp.float32), axis=0)
    term_b_value = jnp.sum(grad_value_b.reshape(row_count, model_width).astype(jnp.float32), axis=0)
    term_w_out = outer_sum(attended_b, grad_branch_b)
    term_b_out = jnp.sum(grad_branch_b.astype(jnp.float32), axis=0)
    (
        grad_w_qkv,
        grad_b_query,
        grad_b_value,
        grad_w_out,
        grad_b_out,
        grad_gain_one,
        grad_shift_one,
    ) = (
        lax.psum_scatter(term_w_qkv, ("dp", "fsdp"), scatter_dimension=0, tiled=True),
        lax.psum_scatter(term_b_query, ("dp", "fsdp"), scatter_dimension=0, tiled=True),
        lax.psum_scatter(term_b_value, ("dp", "fsdp"), scatter_dimension=0, tiled=True),
        lax.psum_scatter(term_w_out, ("dp", "fsdp"), scatter_dimension=0, tiled=True),
        lax.psum_scatter(term_b_out, ("dp", "fsdp"), scatter_dimension=0, tiled=True),
        lax.psum_scatter(grad_g1_rows, ("dp", "fsdp"), scatter_dimension=0, tiled=True),
        lax.psum_scatter(grad_s1_rows, ("dp", "fsdp"), scatter_dimension=0, tiled=True),
    )
    grad_input_b = (grad_hidden + grad_input_ln).astype(jnp.bfloat16)
    returned_grads = lax.all_to_all(
        blank_rows.at[take_at].set(grad_input_b),
        ("dp", "fsdp"),
        split_axis=0,
        concat_axis=0,
        tiled=True,
    )
    grad_rows = returned_grads[send_at].reshape(row_count, 1, model_width)
    return (
        rows_out,
        grad_rows,
        grad_w_qkv,
        grad_b_query,
        grad_b_value,
        grad_w_out,
        grad_b_out,
        grad_gain_one,
        grad_shift_one,
        grad_w_up,
        grad_b_up,
        grad_w_down,
        grad_b_down,
        grad_gain_two,
        grad_shift_two,
    )


def solution(mesh):
    placed = (
        P(None, ("dp", "fsdp"), None),
        P(None, ("dp", "fsdp"), None),
        P(),
        P(),
        P(("dp", "fsdp"), None),
        P(("dp", "fsdp")),
        P(("dp", "fsdp")),
        P(("dp", "fsdp"), None),
        P(("dp", "fsdp")),
        P(("dp", "fsdp")),
        P(("dp", "fsdp")),
        P(("dp", "fsdp"), None),
        P(("dp", "fsdp")),
        P(("dp", "fsdp"), None),
        P(("dp", "fsdp")),
        P(("dp", "fsdp")),
        P(("dp", "fsdp")),
    )
    return jax.shard_map(
        on_device,
        mesh=mesh,
        in_specs=placed,
        out_specs=(
            P(None, ("dp", "fsdp"), None),
            P(None, ("dp", "fsdp"), None),
            P(("dp", "fsdp"), None),
            P(("dp", "fsdp")),
            P(("dp", "fsdp")),
            P(("dp", "fsdp"), None),
            P(("dp", "fsdp")),
            P(("dp", "fsdp")),
            P(("dp", "fsdp")),
            P(("dp", "fsdp"), None),
            P(("dp", "fsdp")),
            P(("dp", "fsdp"), None),
            P(("dp", "fsdp")),
            P(("dp", "fsdp")),
            P(("dp", "fsdp")),
        ),
        check_vma=False,
    )
```

profile of v0, /device:TPU:0, one launch (start us, length us, event | category | flops | bytes accessed | tf_op | source)
XLA Modules:
  0.0 1406.5 jit_solution(18386425301885242166)
XLA Ops:
  20.0 7.3 all-to-all-start.2
  30.4 32.2 %all-to-all-done.2 = bf16[32,9,1024]{2,1,0:T(8,128)(2,1)S(1)} async-done(((bf16[32,9,1024]{2,1,0:T(8,128)(2,1)}), bf16[32,9,1024]{2,1,0:T(8,128)(2,1)S(1)}, u32[]{:S(2)}, u32[]{:S(2)}) %all-to-all-start.2) | async-done | bytes 589856 | tf_op jit(solution)/shard_map/all_to_all | solution.py:118
  62.6 4.3 all-to-all-start
  68.9 59.0 %all-reduce.18 = (bf16[1024]{0:T(1024)(128)(2,1)S(1)}, bf16[1024]{0:T(1024)(128)(2,1)S(1)}, bf16[1024]{0:T(1024)(128)(2,1)S(1)}, bf16[1024]{0:T(1024)(128)(2,1)S...) all-reduce(bf16[1024]{0:T(1024)(128)(2,1)S(1)} %dynamic-update-slic, ...), channel_id=1, replica_groups=mesh['dp'=8,'fsdp'=4] {'dp','fsdp'}, use_global_device_ids=true, to_apply=%add.1 | all-reduce | flops 8192 | bytes 32768
  127.9 66.0 %all-gather = bf16[32,1,128]{2,1,0:T(2,128)(2,1)S(1)} all-gather(bf16[1,1,128]{2,1,0:T(2,128)(2,1)S(1)} %bitcast.100), channel_id=1, replica_groups=mesh['dp'=8,'fsdp'=4] {'dp','fsdp'}, dimensions={0}, use_global_device_ids=true | all-gather | bytes 8448 | tf_op jit(solution)/shard_map/all_gather | solution.py:140
  199.7 4.7 fusion.64
  214.1 29.6 %all-gather.10.cloned.1.call-done = bf16[1024,4096]{1,0:T(8,128)(2,1)} async-done(((bf16[32,4096]{1,0:T(8,128)(2,1)}), bf16[1024,4096]{1,0:T(8,128)(2,1)}) %all-gather.10.cloned.1.call-update) | async-done | bytes 8388624 | tf_op jit(solution)/shard_map/all_gather | solution.py:138
  243.7 7.7 convolution_add_fusion
  251.4 71.0 %all-gather.12.cloned.1.call-done = bf16[4096,1024]{1,0:T(8,128)(2,1)} async-done(((bf16[128,1024]{1,0:T(8,128)(2,1)}), bf16[4096,1024]{1,0:T(8,128)(2,1)}) %all-gather.12.cloned.1.call-update) | async-done | bytes 8388624 | tf_op jit(solution)/shard_map/all_gather | solution.py:139
  322.5 16.2 %convert_reduce_fusion = (f32[4096]{0:T(1024)S(1)}, bf16[256,4096]{1,0:T(8,128)(2,1)S(1)}, f32[256,4096]{1,0:T(8,128)}) fusion(f32[256,4096]{1,0:T(8,128)} %convolution_add_fusion, bf16[256,1024]{1,0:T(8,128)(2,1)S(1)} %gather_fusion.2, bf16[4096,1024]{1,0:T(8,128)(2,1)} %all-gather.12.cloned.1.call-done), kind=kOutput, calls=%fused_computation.11 | convolution fusion | flops 2225074176 | bytes 19415040 | tf_op jit(solution)/shard_map/dot_general | solution.py:68
  351.6 3.7 multiply_reduce_fusion
  359.4 6.6 fusion.35
  366.1 9.8 fusion.67
  376.1 4.2 multiply_convert_fusion.1
  381.7 8.1 fusion.77
  389.8 7.2 fusion.18
  400.6 3.4 all-to-all-start.1
  404.0 5.3 fusion.68
  414.9 32.5 %all-to-all-done.1 = bf16[32,9,1024]{2,1,0:T(8,128)(2,1)} async-done(((bf16[32,9,1024]{2,1,0:T(8,128)(2,1)}), bf16[32,9,1024]{2,1,0:T(8,128)(2,1)}, u32[]{:S(2)}, u32[]{:S(2)}) %all-to-all-start.1) | async-done | bytes 589856 | tf_op jit(solution)/shard_map/all_to_all | solution.py:190
  447.4 6.8 all-to-all-start.3
  454.4 70.0 %all-reduce.17 = (f32[1024]{0:T(1024)S(1)}, f32[1024]{0:T(1024)S(1)}, f32[1024]{0:T(1024)S(1)}, f32[1024]{0:T(1024)S(1)}, f32[1024]{0:T(1024)S(1)}, /*index=5*/f...) all-reduce(f32[1024]{0:T(1024)S(1)} %reduce_sum.316, ...), channel_id=3, replica_groups=mesh['dp'=8,'fsdp'=4] {'dp','fsdp'}, use_global_device_ids=true, to_apply=%region_25.26.clone | all-reduce | flops 12288 | bytes 98304
  535.4 132.6 %reduce-scatter.5.cloned.1.call-done = f32[32,3072]{1,0:T(8,128)} async-done(((f32[1024,3072]{1,0:T(8,128)}), f32[32,3072]{1,0:T(8,128)}) %reduce-scatter.5.cloned.1.call-update) | async-done | bytes 393232 | tf_op jit(solution)/shard_map/reduce_scatter | solution.py:286
  668.0 366.3 %reduce-scatter.9.cloned.1.call-done = f32[32,4096]{1,0:T(8,128)} async-done(((f32[1024,4096]{1,0:T(8,128)}), f32[32,4096]{1,0:T(8,128)}) %reduce-scatter.9.cloned.1.call-update) | async-done | bytes 524304 | tf_op jit(solution)/shard_map/reduce_scatter | solution.py:224
  1034.3 365.2 %reduce-scatter.11.cloned.1.call-done = f32[128,1024]{1,0:T(8,128)} async-done(((f32[4096,1024]{1,0:T(8,128)}), f32[128,1024]{1,0:T(8,128)}) %reduce-scatter.11.cloned.1.call-update) | async-done | bytes 524304 | tf_op jit(solution)/shard_map/reduce_scatter | solution.py:212
  (185 shorter events, 71.7 us)
Async XLA Ops:
  7.2 20.1 %copy-start.18 = (bf16[256,1,1024]{2,0,1:T(8,128)(2,1)S(1)}, bf16[256,1,1024]{2,0,1:T(8,128)(2,1)}, u32[]{:S(2)}) copy-start(bf16[256,1,1024]{2,0,1:T(8,128)(2,1)} %param.17) | copy-start | bytes 1572868
  7.2 192.5 %all-gather.6.cloned.1.call-start = ((), (), s32[]{:S(2)}) async-start(), calls=%async_computation.8 | async-start | bytes 6488064 | tf_op jit(solution)/shard_map/all_gather | solution.py:129
  7.9 203.2 %all-gather.8.cloned.1.call-start = ((), (), s32[]{:S(2)}) async-start(), calls=%async_computation.9 | async-start | bytes 2162688 | tf_op jit(solution)/shard_map/all_gather | solution.py:130
  8.7 235.0 %all-gather.10.cloned.1.call-start = ((), (), s32[]{:S(2)}) async-start(), calls=%async_computation.10 | async-start | bytes 8650752 | tf_op jit(solution)/shard_map/all_gather | solution.py:138
  9.4 313.0 %all-gather.12.cloned.1.call-start = ((), (), s32[]{:S(2)}) async-start(), calls=%async_computation.11 | async-start | bytes 8650752 | tf_op jit(solution)/shard_map/all_gather | solution.py:139
  18.7 48.4 %copy-start.21 = (bf16[32]{0:T(256)(128)(2,1)S(1)}, bf16[32]{0:T(256)(128)(2,1)}, u32[]{:S(2)}) copy-start(bf16[32]{0:T(256)(128)(2,1)} %param.32) | copy-start | bytes 196
  18.7 48.6 %copy-start.22 = (bf16[32]{0:T(256)(128)(2,1)S(1)}, bf16[32]{0:T(256)(128)(2,1)}, u32[]{:S(2)}) copy-start(bf16[32]{0:T(256)(128)(2,1)} %param.33) | copy-start | bytes 196
  18.7 48.8 %copy-start.23 = (bf16[32]{0:T(256)(128)(2,1)S(1)}, bf16[32]{0:T(256)(128)(2,1)}, u32[]{:S(2)}) copy-start(bf16[32]{0:T(256)(128)(2,1)} %param.25) | copy-start | bytes 196
  18.7 49.0 %copy-start.24 = (bf16[32]{0:T(256)(128)(2,1)S(1)}, bf16[32]{0:T(256)(128)(2,1)}, u32[]{:S(2)}) copy-start(bf16[32]{0:T(256)(128)(2,1)} %param.22) | copy-start | bytes 196
  18.7 49.3 %copy-start.25 = (bf16[32]{0:T(256)(128)(2,1)S(1)}, bf16[32]{0:T(256)(128)(2,1)}, u32[]{:S(2)}) copy-start(bf16[32]{0:T(256)(128)(2,1)} %param.23) | copy-start | bytes 196
  18.7 49.5 %copy-start.26 = (bf16[32]{0:T(256)(128)(2,1)S(1)}, bf16[32]{0:T(256)(128)(2,1)}, u32[]{:S(2)}) copy-start(bf16[32]{0:T(256)(128)(2,1)} %param.26) | copy-start | bytes 196
  18.7 49.7 %copy-start.27 = (bf16[32]{0:T(256)(128)(2,1)S(1)}, bf16[32]{0:T(256)(128)(2,1)}, u32[]{:S(2)}) copy-start(bf16[32]{0:T(256)(128)(2,1)} %param.27) | copy-start | bytes 196
  18.8 49.9 %copy-start.28 = (bf16[32]{0:T(256)(128)(2,1)S(1)}, bf16[32]{0:T(256)(128)(2,1)}, u32[]{:S(2)}) copy-start(bf16[32]{0:T(256)(128)(2,1)} %param.31) | copy-start | bytes 196
  18.8 109.2 %copy-start.19 = (bf16[128]{0:T(256)(128)(2,1)S(1)}, bf16[128]{0:T(256)(128)(2,1)}, u32[]{:S(2)}) copy-start(bf16[128]{0:T(256)(128)(2,1)} %param.29) | copy-start | bytes 772
  20.0 42.7 %all-to-all-start.2 = ((bf16[32,9,1024]{2,1,0:T(8,128)(2,1)}), bf16[32,9,1024]{2,1,0:T(8,128)(2,1)S(1)}, u32[]{:S(2)}, u32[]{:S(2)}) async-start(bf16[32,9,1024]{2,1,0:T(8,128)(2,1)} %all_to_all.38), calls=%async_computation.2 | async-start | bytes 2097152 | tf_op jit(solution)/shard_map/all_to_all | solution.py:118
  62.6 135.2 %all-to-all-start = ((bf16[32,9,1024]{2,1,0:T(8,128)(2,1)}), bf16[32,9,1024]{2,1,0:T(8,128)(2,1)S(1)}, u32[]{:S(2)}, u32[]{:S(2)}) async-start(bf16[32,9,1024]{2,1,0:T(8,128)(2,1)} %all_to_all.32), calls=%async_computation | async-start | bytes 2097152 | tf_op jit(solution)/shard_map/all_to_all | solution.py:111
  67.0 468.4 %reduce-scatter.7.cloned.1.call-start = ((), (), s32[]{:S(2)}) async-start(), calls=%async_computation.13 | async-start | bytes 4325376 | tf_op jit(solution)/shard_map/reduce_scatter | solution.py:289
  211.2 40.3 %copy-start.10 = (bf16[16,64,256]{2,1,0:T(8,128)(2,1)}, bf16[16,64,256]{2,1,0:T(8,128)(2,1)S(1)}, u32[]{:S(2)}) copy-start(bf16[16,64,256]{2,1,0:T(8,128)(2,1)S(1)} %fusion.24) | copy-start | bytes 1572868
  345.7 322.4 %reduce-scatter.5.cloned.1.call-start = ((), (), s32[]{:S(2)}) async-start(), calls=%async_computation.12 | async-start | bytes 12976128 | tf_op jit(solution)/shard_map/reduce_scatter | solution.py:286
  366.0 668.3 %reduce-scatter.9.cloned.1.call-start = ((), (), s32[]{:S(2)}) async-start(), calls=%async_computation.14 | async-start | bytes 17301504 | tf_op jit(solution)/shard_map/reduce_scatter | solution.py:224
  375.9 1023.6 %reduce-scatter.11.cloned.1.call-start = ((), (), s32[]{:S(2)}) async-start(), calls=%async_computation.15 | async-start | bytes 17301504 | tf_op jit(solution)/shard_map/reduce_scatter | solution.py:212
  400.6 46.9 %all-to-all-start.1 = ((bf16[32,9,1024]{2,1,0:T(8,128)(2,1)}), bf16[32,9,1024]{2,1,0:T(8,128)(2,1)}, u32[]{:S(2)}, u32[]{:S(2)}) async-start(bf16[32,9,1024]{2,1,0:T(8,128)(2,1)} %all_to_all.35), calls=%async_computation.1 | async-start | bytes 2097152 | tf_op jit(solution)/shard_map/all_to_all | solution.py:190
  447.4 85.7 %all-to-all-start.3 = ((bf16[32,9,1024]{2,1,0:T(8,128)(2,1)}), bf16[32,9,1024]{2,1,0:T(8,128)(2,1)S(1)}, u32[]{:S(2)}, u32[]{:S(2)}) async-start(bf16[32,9,1024]{2,1,0:T(8,128)(2,1)} %all_to_all.41), calls=%async_computation.3 | async-start | bytes 2097152 | tf_op jit(solution)/shard_map/all_to_all | solution.py:295
  531.2 868.3 %copy-start.1 = (bf16[256,1,1024]{2,0,1:T(8,128)(2,1)S(1)}, bf16[256,1,1024]{2,0,1:T(8,128)(2,1)}, u32[]{:S(2)}) copy-start(bf16[256,1,1024]{2,0,1:T(8,128)(2,1)} %param.18) | copy-start | bytes 1572868
  (17 other events, 52.8 us)
Sparse Core Ops, SparseCore 0:
  10.9 94.6 all-gather.5
  108.5 55.6 all-gather.7
  167.2 76.4 all-gather.9
  246.4 75.9 all-gather.11
  345.8 161.0 reduce-scatter.6
  513.4 154.5 reduce-scatter.4
  671.0 363.2 reduce-scatter.8
  1037.3 362.1 reduce-scatter.10
where the time goes:
time: 1410 us
  waiting for transfers between devices  1030 us (73%)
  blocking collectives  195 us (14%)
  matrix products  84.6 us (6%)
  local copies, waits for them, and re-layouts  38.8 us (3%)
  starting transfers between devices  22.7 us (2%)
  other arithmetic  18.2 us (1%)
  between operations  15.1 us (1%)
    reduce_scatter x1, waiting for transfers between devices, on_device(): lax.psum_scatter(term_w_up, ('dp', 'fsdp'), scatter_dimension=0, tiled=True)  366 us
    reduce_scatter x1, waiting for transfers between devices, on_device(): lax.psum_scatter(term_w_down, ('dp', 'fsdp'), scatter_dimension=0, tiled=...  365 us
    reduce_scatter x1, waiting for transfers between devices, on_device(): lax.psum_scatter(term_w_qkv, ('dp', 'fsdp'), scatter_dimension=0, tiled=T...  133 us
    unnamed x2, blocking collectives  129 us
    all_gather x1, waiting for transfers between devices, on_device(): lax.all_gather(w_down, ('dp', 'fsdp'), axis=0, tiled=True)  71 us
    all_gather x1, blocking collectives, on_device(): lax.all_gather(b_up, ('dp', 'fsdp'), axis=0, tiled=True)  66 us
    all_to_all x1, waiting for transfers between devices, on_device(): lax.all_to_all(blank_rows.at[take_at].set(result_rows.astype(jnp.bfloat16...  32.5 us
    all_to_all x1, waiting for transfers between devices, on_device(): lax.all_to_all(blank_rows.at[send_at].set(flat_cot), ('dp', 'fsdp'), spli...  32.2 us
  transfers between devices with their start and end apart: 12, of which 7 were waited for; matrix products, arithmetic and copies ran while one was open for 8% of the time, Pallas kernels for 0%

commit v1 on v0

v1 whole, which is shorter than its diff:
```python
import jax
import jax.numpy as jnp
from jax import lax
from jax.experimental import pallas as pl
from jax.experimental.pallas import tpu as pltpu
from jax.sharding import PartitionSpec as P

HEADS = 16
HEAD_DIM = 64
EPSILON = 1e-05
AXES = ("dp", "fsdp")
BF16 = jnp.bfloat16
F32 = jnp.float32


class Grid:
    def __init__(self, n_dp, n_z):
        self.n_dp, self.n_z = n_dp, n_z
        side = 1
        while side * side * 2 < n_dp:
            side *= 2
        self.nx, self.ny = side, n_dp // (2 * side)
        self.x_masks = [2 * k for k in range(1, self.nx)]
        self.y_masks = [2 * side * k for k in range(1, self.ny)]
        self.z_masks = list(range(1, n_z))

    def bind(self):
        dp = lax.axis_index("dp")
        self.my_z = lax.axis_index("fsdp")
        self.my_core = dp % 2
        self.my_x = (dp // 2) % self.nx
        self.my_y = dp // (2 * self.nx)
        self.me = lax.axis_index(AXES)

    def over_dp(self, value, mask):
        return lax.ppermute(value, "dp", [(i, i ^ mask) for i in range(self.n_dp)])

    def over_z(self, value, mask):
        return lax.ppermute(value, "fsdp", [(i, i ^ mask) for i in range(self.n_z)])


def after(value, *deps):
    return lax.optimization_barrier((value,) + deps)[0]


def spread(grid, blocks, first, second):
    base = jnp.concatenate(blocks, 0)
    group = jnp.concatenate([base] + [grid.over_dp(base, m) for m in first], 0)
    masks = [0] + list(first)
    found = [(group, masks)]
    for m in second:
        found.append((grid.over_dp(group, m), [m ^ f for f in masks]))
    return found


def assemble(grid, pieces, rows, col_cuts):
    block = rows // (grid.n_dp * grid.n_z)
    half = grid.n_z // 2
    spans = list(zip([0] + col_cuts[:-1], col_cuts))
    copies = sum(len(masks) * half for _, masks, _ in pieces) * len(spans)

    def kernel(me_ref, *refs):
        sources = refs[: len(pieces)]
        outs = refs[len(pieces) : len(pieces) + len(spans)]
        sems = refs[-1]
        me = me_ref[0]
        started = []
        for source, (_, masks, z_from) in zip(sources, pieces):
            at = 0
            for m in masks:
                for z in range(half):
                    owner = lax.bitwise_xor(me, jnp.int32(m * grid.n_z + z_from + z))
                    to = pl.ds(pl.multiple_of(owner * block, block), block)
                    for out, (lo, hi) in zip(outs, spans):
                        copy = pltpu.make_async_copy(
                            source.at[pl.ds(at * block, block), pl.ds(lo, hi - lo)],
                            out.at[to],
                            sems.at[len(started)],
                        )
                        copy.start()
                        started.append(copy)
                    at += 1
        for copy in started:
            copy.wait()

    return pl.pallas_call(
        kernel,
        out_shape=[jax.ShapeDtypeStruct((rows, hi - lo), BF16) for lo, hi in spans],
        grid_spec=pltpu.PrefetchScalarGridSpec(
            num_scalar_prefetch=1,
            grid=(),
            in_specs=[pl.BlockSpec(memory_space=pl.ANY)] * len(pieces),
            out_specs=[pl.BlockSpec(memory_space=pltpu.VMEM)] * len(spans),
            scratch_shapes=[pltpu.SemaphoreType.DMA((copies,))],
        ),
        compiler_params=pltpu.CompilerParams(vmem_limit_bytes=20 << 20),
        name="assemble",
    )(grid.me.reshape(1).astype(jnp.int32), *[piece for piece, _, _ in pieces])


def gather(grid, shard, col_cuts, ready=()):
    rows = shard.shape[0] * grid.n_dp * grid.n_z
    if shard.shape[0] % 16:
        full = lax.all_gather(shard, AXES, axis=0, tiled=True)
        return [full[:, lo:hi] for lo, hi in zip([0] + col_cuts[:-1], col_cuts)], ()
    if ready:
        shard = after(shard, *ready)
    line = [shard] + [grid.over_z(shard, m) for m in grid.z_masks]
    half = grid.n_z // 2
    pieces = [(v, m, 0) for v, m in spread(grid, line[:half], grid.x_masks, grid.y_masks)]
    pieces += [(v, m, half) for v, m in spread(grid, line[half:], grid.y_masks, grid.x_masks)]
    pieces += [(grid.over_dp(v, 1), [k ^ 1 for k in m], z) for v, m, z in pieces]
    return assemble(grid, pieces, rows, col_cuts), tuple(line[1:])


def outer_sum(left, right):
    return lax.dot_general(left, right, (((0,), (0,)), ((), ())), preferred_element_type=F32)


def back_dot(grad_rows, weight):
    return lax.dot_general(grad_rows, weight, (((1,), (1,)), ((), ())), preferred_element_type=F32)


def pick(array, index, axis):
    return lax.dynamic_index_in_dim(array, index, axis, keepdims=False)


def exchange_sum(grid, array, axis, mine, base):
    count = array.shape[axis]
    total = pick(array, mine, axis)
    got = []
    for k in range(1, count):
        part = pick(array, mine ^ k, axis).astype(BF16)
        if base == 0:
            got.append(grid.over_z(part, k))
        else:
            got.append(grid.over_dp(part, base * k))
    for part in got:
        total = total + part.astype(F32)
    return total


def scatter_outer(grid, left, right):
    tokens, width = left.shape
    places = grid.ny * grid.nx
    block = width // (places * 2 * grid.n_z)
    cols = right.shape[1]
    parts = left.reshape(tokens, places, 2, grid.n_z * block)
    theirs = pick(parts, 1 - grid.my_core, 2).reshape(tokens, width // 2)
    mine = pick(parts, grid.my_core, 2).reshape(tokens, width // 2)
    got = grid.over_dp(outer_sum(theirs, right).astype(BF16), 1)
    held = outer_sum(mine, right) + got.astype(F32)
    held = held.reshape(grid.ny, grid.nx, grid.n_z, block, cols)
    half = grid.n_z // 2
    one = exchange_sum(grid, held[:, :, :half], 0, grid.my_y, 2 * grid.nx)
    two = exchange_sum(grid, held[:, :, half:], 1, grid.my_x, 2)
    one = exchange_sum(grid, one, 0, grid.my_x, 2)
    two = exchange_sum(grid, two, 0, grid.my_y, 2 * grid.nx)
    return exchange_sum(grid, jnp.concatenate([one, two], 0), 0, grid.my_z, 0)


def lookup(small_table, index_rows):
    matches = index_rows[:, None] == jnp.arange(small_table.shape[0], dtype=jnp.int32)[None, :]
    return jnp.sum(jnp.where(matches, small_table[None, :], 0), axis=1)


def rank_among(group_label, order_key):
    earlier = (group_label[None, :] == group_label[:, None]) & (
        order_key[None, :] < order_key[:, None]
    )
    return jnp.sum(earlier.astype(jnp.int32), axis=1)


def routing(lengths, deal_order, devices, row_count, device):
    slot_count = deal_order.shape[0]
    slot_ids = jnp.arange(slot_count, dtype=jnp.int32)
    starts = jnp.cumsum(lengths) - lengths
    slot_of = jnp.sum(
        jnp.where(deal_order[None, :] == slot_ids[:, None], slot_ids[None, :], 0), axis=1
    )
    slot_lengths = lookup(lengths, deal_order)
    slot_rows = row_count // devices + 1
    local_rows = jnp.arange(row_count, dtype=jnp.int32)
    token_index = local_rows * devices + device
    sequence = jnp.sum((starts[None, :] <= token_index[:, None]).astype(jnp.int32), axis=1) - 1
    slot_index = lookup(slot_of, sequence)
    target = slot_index // 2
    send_at = target * slot_rows + rank_among(target, local_rows)
    first_len = lax.dynamic_index_in_dim(slot_lengths, 2 * device, 0, False)
    second = local_rows >= first_len
    first_seq = lax.dynamic_index_in_dim(deal_order, 2 * device, 0, False)
    second_seq = lax.dynamic_index_in_dim(deal_order, 2 * device + 1, 0, False)
    sequence_here = jnp.where(second, second_seq, first_seq)
    position = local_rows - jnp.where(second, first_len, 0)
    source_token = lookup(starts, sequence_here) + position
    source = source_token % devices
    take_at = source * slot_rows + rank_among(source, source_token)
    return (send_at, take_at, second.astype(jnp.int32), position, slot_rows)


def standardize(values):
    centered = values - jnp.mean(values, axis=-1, keepdims=True)
    scale = lax.rsqrt(jnp.mean(centered * centered, axis=-1, keepdims=True) + EPSILON)
    return centered * scale, scale


def standardize_back(grad, unit, scale):
    return scale * (
        grad
        - jnp.mean(grad, axis=-1, keepdims=True)
        - unit * jnp.mean(grad * unit, axis=-1, keepdims=True)
    )


def col_sum(values):
    return jnp.sum(values.astype(F32), axis=0)


def on_device(
    n_dp,
    n_z,
    rows_in,
    cotangent,
    lengths,
    deal_order,
    w_qkv,
    b_query,
    b_value,
    w_out,
    b_out,
    gain_one,
    shift_one,
    w_up,
    b_up,
    w_down,
    b_down,
    gain_two,
    shift_two,
):
    grid = Grid(n_dp, n_z)
    grid.bind()
    devices = n_dp * n_z
    row_count, _, width = rows_in.shape
    hidden = w_up.shape[1]
    share = width // devices

    (full_qkv, full_out), ready = gather(
        grid, jnp.concatenate([w_qkv, w_out], axis=1), [3 * width, 4 * width]
    )
    (full_up,), ready = gather(grid, w_up, [hidden], ready)
    (full_down,), ready = gather(grid, w_down, [width], ready)

    send_at, take_at, segment, position, slot_rows = routing(
        lengths, deal_order, devices, row_count, grid.me
    )
    slots = devices * slot_rows
    slot_ids = jnp.arange(slots, dtype=jnp.int32)
    to_slots = (slot_ids[:, None] == send_at[None, :]).astype(BF16)
    from_slots = (take_at[:, None] == slot_ids[None, :]).astype(BF16)

    def pack(selector, contract, rows):
        return lax.dot_general(
            selector, rows, (((contract,), (0,)), ((), ())), preferred_element_type=F32
        ).astype(BF16)

    def swap(*parts):
        joined = jnp.concatenate([p.reshape(devices, -1, width) for p in parts], axis=1)
        return lax.all_to_all(joined, AXES, split_axis=0, concat_axis=0, tiled=True)

    small = jnp.concatenate(
        [b_query, b_value, b_out, gain_one, shift_one, b_down, gain_two, shift_two, b_up]
    )
    small = jnp.pad(small, (0, width - small.shape[0]))
    arrived = swap(
        pack(to_slots, 1, rows_in.reshape(row_count, width)),
        pack(to_slots, 1, cotangent.reshape(row_count, width)),
        jnp.broadcast_to(small, (devices, 1, width)),
    )
    token_rows = arrived[:, :slot_rows].reshape(slots, width)
    cot_rows = arrived[:, slot_rows : 2 * slot_rows].reshape(slots, width)
    inputs = pack(from_slots, 1, token_rows).astype(F32)
    grad_m_b = pack(from_slots, 1, cot_rows)
    small_all = arrived[:, 2 * slot_rows].astype(F32)
    vectors = [small_all[:, k * share : (k + 1) * share].reshape(width) for k in range(8)]
    bq, bv, bo, g1, s1, bd, g2, s2 = vectors
    bu = small_all[:, 8 * share : 8 * share + hidden // devices].reshape(hidden)

    unit_one, scale_one = standardize(inputs)
    normed_one_b = (unit_one * g1 + s1).astype(BF16)
    mixed = jnp.dot(normed_one_b, full_qkv, preferred_element_type=F32)
    head_shape = (row_count, HEADS, HEAD_DIM)
    query_b = (mixed[:, :width] + bq).astype(BF16).reshape(head_shape)
    key_b = mixed[:, width : 2 * width].astype(BF16).reshape(head_shape)
    value_b = (mixed[:, 2 * width :] + bv).astype(BF16).reshape(head_shape)
    allowed = (segment[:, None] == segment[None, :]) & (position[None, :] <= position[:, None])
    scale_factor = HEAD_DIM ** (-0.5)
    scores = jnp.einsum("qhd,khd->hqk", query_b, key_b, preferred_element_type=F32)
    masked = jnp.where(allowed[None], scores * scale_factor, -1000000000.0)
    exps = jnp.exp(masked - jnp.max(masked, axis=-1, keepdims=True))
    softmax_f = exps / jnp.sum(exps, axis=-1, keepdims=True)
    softmax_b = softmax_f.astype(BF16)
    attended_b = jnp.einsum("hqk,khd->qhd", softmax_b, value_b, preferred_element_type=F32)
    attended_b = attended_b.reshape(row_count, width).astype(BF16)
    hidden_one = inputs + jnp.dot(attended_b, full_out, preferred_element_type=F32) + bo

    unit_two, scale_two = standardize(hidden_one)
    normed_two_b = (unit_two * g2 + s2).astype(BF16)
    pre_act = jnp.dot(normed_two_b, full_up, preferred_element_type=F32) + bu
    half_cdf = 0.5 * (1.0 + lax.erf(pre_act * (0.5**0.5)))
    activation_b = (pre_act * half_cdf).astype(BF16)
    density = jnp.exp(-0.5 * pre_act * pre_act) * ((2.0 * jnp.pi) ** -0.5)
    slope = half_cdf + pre_act * density

    grad_w_down = scatter_outer(grid, activation_b, grad_m_b)
    term_b_down = col_sum(grad_m_b)

    result_rows = hidden_one + jnp.dot(activation_b, full_down, preferred_element_type=F32) + bd

    grad_pre_b = (back_dot(grad_m_b, full_down) * slope).astype(BF16)
    grad_w_up = scatter_outer(grid, normed_two_b, grad_pre_b)
    term_b_up = col_sum(grad_pre_b)
    grad_normed_two = back_dot(grad_pre_b, full_up)
    term_g2 = col_sum(grad_normed_two * unit_two)
    term_s2 = col_sum(grad_normed_two)
    grad_hidden = grad_m_b.astype(F32) + standardize_back(grad_normed_two * g2, unit_two, scale_two)
    grad_branch_b = grad_hidden.astype(BF16)
    term_b_out = col_sum(grad_branch_b)

    grad_w_out = scatter_outer(grid, attended_b, grad_branch_b)
    grad_att_b = back_dot(grad_branch_b, full_out).astype(BF16).reshape(head_shape)
    grad_probs = jnp.einsum("qhd,khd->hqk", grad_att_b, value_b, preferred_element_type=F32)
    grad_scores_b = (
        softmax_f * (grad_probs - jnp.sum(softmax_f * grad_probs, axis=-1, keepdims=True))
    ).astype(BF16)
    grad_query = jnp.einsum("hqk,khd->qhd", grad_scores_b, key_b, preferred_element_type=F32)
    grad_key = jnp.einsum("hqk,qhd->khd", grad_scores_b, query_b, preferred_element_type=F32)
    grad_value = jnp.einsum("hqk,qhd->khd", softmax_b, grad_att_b, preferred_element_type=F32)
    grad_mixed_b = jnp.concatenate(
        [
            (grad_query * scale_factor).astype(BF16).reshape(row_count, width),
            (grad_key * scale_factor).astype(BF16).reshape(row_count, width),
            grad_value.astype(BF16).reshape(row_count, width),
        ],
        axis=1,
    )
    grad_w_qkv = scatter_outer(grid, normed_one_b, grad_mixed_b)
    term_mixed = col_sum(grad_mixed_b)
    grad_normed_one = back_dot(grad_mixed_b, full_qkv)
    term_g1 = col_sum(grad_normed_one * unit_one)
    term_s1 = col_sum(grad_normed_one)
    grad_inputs = grad_hidden + standardize_back(grad_normed_one * g1, unit_one, scale_one)

    terms = [term_mixed[:width], term_mixed[2 * width :], term_b_out, term_g1, term_s1]
    terms += [term_b_down, term_g2, term_s2, term_b_up]
    terms = jnp.concatenate([v.reshape(devices, -1) for v in terms], axis=1)
    count = terms.shape[1]
    high = lax.reduce_precision(terms, 8, 7)
    low = terms - high
    small_back = jnp.concatenate([high, low], axis=1).astype(BF16)
    small_back = jnp.pad(small_back, ((0, 0), (0, width - 2 * count)))
    returned = swap(
        pack(from_slots, 0, result_rows.astype(BF16)),
        pack(from_slots, 0, grad_inputs.astype(BF16)),
        small_back[:, None],
    )
    rows_out = pack(to_slots, 0, returned[:, :slot_rows].reshape(slots, width))
    grad_rows = pack(to_slots, 0, returned[:, slot_rows : 2 * slot_rows].reshape(slots, width))
    sums = jnp.sum(returned[:, 2 * slot_rows].astype(F32), axis=0)
    sums = sums[:count] + sums[count : 2 * count]
    cut = [sums[k * share : (k + 1) * share] for k in range(8)]
    grad_bq, grad_bv, grad_bo, grad_g1, grad_s1, grad_bd, grad_g2, grad_s2 = cut
    grad_bu = sums[8 * share :]
    return (
        rows_out.reshape(row_count, 1, width),
        grad_rows.reshape(row_count, 1, width),
        grad_w_qkv,
        grad_bq,
        grad_bv,
        grad_w_out,
        grad_bo,
        grad_g1,
        grad_s1,
        grad_w_up,
        grad_bu,
        grad_w_down,
        grad_bd,
        grad_g2,
        grad_s2,
    )


def solution(mesh):
    n_dp, n_z = mesh.shape["dp"], mesh.shape["fsdp"]
    rows, vec, mat = P(None, AXES, None), P(AXES), P(AXES, None)

    def run(*args):
        return on_device(n_dp, n_z, *args)

    return jax.shard_map(
        run,
        mesh=mesh,
        in_specs=(rows, rows, P(), P())
        + (mat, vec, vec, mat, vec, vec, vec, mat, vec, mat, vec, vec, vec),
        out_specs=(rows, rows, mat, vec, vec, mat, vec, vec, vec, mat, vec, mat, vec, vec, vec),
        check_vma=False,
    )
```

time: 1410 us -> 536 us (0.38)
  waiting for transfers between devices: 1030 us -> 205 us
  blocking collectives: 195 us -> 0 us
  starting transfers between devices: 22.7 us -> 90 us
  local copies, waits for them, and re-layouts: 38.8 us -> 98.4 us
  other arithmetic: 18.2 us -> 36.1 us
    reduce_scatter x4 -> x0, waiting for transfers between devices: 864 us -> none  [the longest x1 366 us: on_device(): lax.psum_scatter(term_w_up, ('dp', 'fsdp'), scatter_dimension=0, tiled=True)]
    ppermute x0 -> x65, waiting for transfers between devices: none -> 205 us  [the longest x44 120 us: over_dp(): return lax.ppermute(value, 'dp', [(i, i ^ mask) for i in range(self.n_dp)])]
    unnamed x2 -> x0, blocking collectives: 129 us -> none
    all_gather x4 -> x0, waiting for transfers between devices: 101 us -> none  [the longest x1 71 us: on_device(): lax.all_gather(w_down, ('dp', 'fsdp'), axis=0, tiled=True)]
    ppermute x0 -> x65, starting transfers between devices: none -> 79.5 us  [the longest x21 41.2 us: over_z(): return lax.ppermute(value, 'fsdp', [(i, i ^ mask) for i in range(self.n_z)])]
    all_gather x1 -> x0, blocking collectives: 66 us -> none  [on_device(): lax.all_gather(b_up, ('dp', 'fsdp'), axis=0, tiled=True)]
    all_to_all x4 -> x2, waiting for transfers between devices: 64.7 us -> 0.01 us  [swap(): return lax.all_to_all(joined, AXES, split_axis=0, concat_axis=0, tiled=True)]
    unnamed x83 -> x150, local copies, waits for them, and re-layouts: 11.5 us -> 33.4 us
  transfers between devices with their start and end apart: 12 -> 67, of which waited for: 7 -> 27; matrix products, arithmetic and copies ran while one was open for 8% -> 32% of each run, Pallas kernels for 0% -> 1%
where the time goes in v1:
time: 536 us; the launch traced here: 526 us
  waiting for transfers between devices  205 us (38%)
  local copies, waits for them, and re-layouts  98.4 us (18%)
  starting transfers between devices  90 us (17%)
  matrix products  82.1 us (15%)
  other arithmetic  36.1 us (7%)
  Pallas kernels  11.2 us (2%)
    ppermute x44, waiting for transfers between devices, over_dp(): return lax.ppermute(value, 'dp', [(i, i ^ mask) for i in range(self.n_dp)])  120 us
    ppermute x21, waiting for transfers between devices, over_z(): return lax.ppermute(value, 'fsdp', [(i, i ^ mask) for i in range(self.n_z)])  84.9 us
    ppermute x21, starting transfers between devices, over_z(): return lax.ppermute(value, 'fsdp', [(i, i ^ mask) for i in range(self.n_z)])  41.2 us
    ppermute x44, starting transfers between devices, over_dp(): return lax.ppermute(value, 'dp', [(i, i ^ mask) for i in range(self.n_dp)])  38.3 us
    unnamed x150, local copies, waits for them, and re-layouts  33.4 us
    dot_general x8, matrix products, outer_sum(): lax.dot_general(left, right, (((0,), (0,)), ((), ())), preferred_element_...  24.9 us
    dot_general x4, matrix products, back_dot(): lax.dot_general(grad_rows, weight, (((1,), (1,)), ((), ())), preferred_el...  20.1 us
    dot_general x8, matrix products, pack(): lax.dot_general(selector, rows, (((contract,), (0,)), ((), ())), preferre...  17.6 us
  transfers between devices with their start and end apart: 67, of which 27 were waited for; matrix products, arithmetic and copies ran while one was open for 32% of the time, Pallas kernels for 1%

profile of v1, /device:TPU:0, one launch (start us, length us, event | category | flops | bytes accessed | tf_op | source)
XLA Modules:
  0.0 525.8 jit_solution(141043060095487900)
XLA Ops:
  20.0 6.2 %all-to-all-start = ((bf16[32,19,1024]{2,1,0:T(8,128)(2,1)}), bf16[32,19,1024]{2,1,0:T(8,128)(2,1)}, u32[]{:S(2)}, u32[]{:S(2)}) async-start(bf16[32,19,1024]{2,1,0:T(8,128)(2,1)} %pad_maximum_fusion), calls=%async_computation | async-start | bytes 3145728 | tf_op jit(solution)/shard_map/all_to_all | solution.py:268
  30.2 8.6 %collective-permute-start.15 = (bf16[32,4096]{1,0:T(8,128)(2,1)S(1)}, bf16[32,4096]{1,0:T(8,128)(2,1)S(1)}, u32[]{:S(2)}, u32[]{:S(2)}) collective-permute-start(bf16[32,4096]{1,0:T(8,128)(2,1)S(1)} %copy-done.46), channel_id=1, source_target_pairs={{0,3},{1,2},{2,1},{3,0},{4,7},{5,6},{6,5},{7,4},{8,11},{9,10},{10,... | collective-permute-start | bytes 786440 | tf_op jit(solution)/shard_map/ppermute | solution.py:39
  47.2 15.0 %collective-permute-done.15 = bf16[32,4096]{1,0:T(8,128)(2,1)S(1)} collective-permute-done((bf16[32,4096]{1,0:T(8,128)(2,1)S(1)}, bf16[32,4096]{1,0:T(8,128)(2,1)S(1)}, u32[]{:S(2)}, u32[]{:S(2)}) %collective-permute-start.15) | collective-permute-done | bytes 262176 | tf_op jit(solution)/shard_map/ppermute | solution.py:39
  62.2 24.0 %collective-permute-done.14 = bf16[32,4096]{1,0:T(8,128)(2,1)S(1)} collective-permute-done((bf16[32,4096]{1,0:T(8,128)(2,1)S(1)}, bf16[32,4096]{1,0:T(8,128)(2,1)S(1)}, u32[]{:S(2)}, u32[]{:S(2)}) %collective-permute-start.14) | collective-permute-done | bytes 262176 | tf_op jit(solution)/shard_map/ppermute | solution.py:39
  93.7 15.7 %collective-permute-done.25 = bf16[128,1024]{1,0:T(8,128)(2,1)S(1)} collective-permute-done((bf16[128,1024]{1,0:T(8,128)(2,1)S(1)}, bf16[128,1024]{1,0:T(8,128)(2,1)S(1)}, u32[]{:S(2)}, u32[]{:S(2)}) %collective-permute-start.25) | collective-permute-done | bytes 262176 | tf_op jit(solution)/shard_map/ppermute | solution.py:39
  116.9 7.3 %collective-permute-done.12 = bf16[64,4096]{1,0:T(8,128)(2,1)S(1)} collective-permute-done((bf16[64,4096]{1,0:T(8,128)(2,1)S(1)}, bf16[64,4096]{1,0:T(8,128)(2,1)S(1)}, u32[]{:S(2)}, u32[]{:S(2)}) %collective-permute-start.12) | collective-permute-done | bytes 524320 | tf_op jit(solution)/shard_map/ppermute | solution.py:36
  128.7 26.4 %collective-permute-done.23 = bf16[256,1024]{1,0:T(8,128)(2,1)S(1)} collective-permute-done((bf16[256,1024]{1,0:T(8,128)(2,1)S(1)}, bf16[256,1024]{1,0:T(8,128)(2,1)S(1)}, u32[]{:S(2)}, u32[]{:S(2)}) %collective-permute-start.23) | collective-permute-done | bytes 524320 | tf_op jit(solution)/shard_map/ppermute | solution.py:36
  198.8 5.5 %collective-permute-done.13.refs_1_ = bf16[128,4096]{1,0:T(8,128)(2,1)} collective-permute-done((bf16[128,4096]{1,0:T(8,128)(2,1)}, bf16[128,4096]{1,0:T(8,128)(2,1)}, u32[]{:S(2)}, u32[]{:S(2)}) %collective-permute-start.13) | collective-permute-done | bytes 1048608 | tf_op jit(solution)/shard_map/ppermute | solution.py:36
  216.2 10.0 %collective-permute-done.24.refs_1_ = bf16[512,1024]{1,0:T(8,128)(2,1)} collective-permute-done((bf16[512,1024]{1,0:T(8,128)(2,1)}, bf16[512,1024]{1,0:T(8,128)(2,1)}, u32[]{:S(2)}, u32[]{:S(2)}) %collective-permute-start.24) | collective-permute-done | bytes 1048608 | tf_op jit(solution)/shard_map/ppermute | solution.py:36
  232.9 5.2 multiply_convert_fusion.1
  242.5 8.6 %constant_dynamic-slice_fusion = (bf16[256,4,1,512]{3,2,1,0:T(2,128)(2,1)}, bf16[256,4,1,512]{3,2,1,0:T(2,128)(2,1)}) fusion(bf16[256,4,2,512]{3,2,1,0:T(2,128)(2,1)} %reshape.527, s32[]{:T(128)S(6)} %select_n.219, s32[]{:T(128)S(6)} %select_n.218), kind=kLoop, calls=%fused_computation.294 | loop fusion | bytes 4194312 | tf_op jit(solution)/shard_map/jit(dynamic_index_in_dim)/dynamic_slice | solution.py:125
  251.1 5.8 %copy.108 = bf16[256,4,1,512]{0,3,1,2:T(8,128)(2,1)} copy(bf16[256,4,1,512]{3,2,1,0:T(2,128)(2,1)} %get-tuple-element.51) | data formatting | bytes 2097152
  261.6 12.8 %convert_reduce_fusion = (f32[4096]{0:T(1024)S(1)}, bf16[256,4096]{1,0:T(8,128)(2,1)S(1)}) fusion(f32[256,4096]{1,0:T(8,128)S(1)} %copy-done.61, bf16[256,1024]{1,0:T(8,128)(2,1)S(1)} %convolution_convert_fusion.10, bf16[4096,1024]{1,0:T(8,128)(2,1)S(1)} %assemble.5), kind=kOutput, calls=%fused_computation.14 | convolution fusion | flops 2160062464 | bytes 15220736 | tf_op jit(solution)/shard_map/dot_general | solution.py:121
  292.7 7.5 %convolution_convert_fusion.5 = bf16[288,1024]{1,0:T(8,128)(2,1)} fusion(f32[256,1024]{1,0:T(8,128)S(1)} %copy-done.11, bf16[256,4096]{1,0:T(8,128)(2,1)} %get-tuple-element.109, bf16[4096,1024]{1,0:T(8,128)(2,1)} %copy-done.2, f32[1024]{0:T(1024)S(1)} %add.442, s32[256]{0:T(256)S(1)} %multiply_add_fusion), kind=kOutput, calls=%fused_computation.76 | convolution fusion | flops 2299633664 | bytes 12129280 | tf_op jit(solution)/shard_map/dot_general | solution.py:262
  331.3 5.8 %copy.107 = bf16[256,4,1,512]{0,3,1,2:T(8,128)(2,1)} copy(bf16[256,4,1,512]{3,2,1,0:T(2,128)(2,1)} %get-tuple-element.52) | data formatting | bytes 2097152
  343.4 6.1 %collective-permute-done.44 = bf16[2,2,32,1024]{3,2,1,0:T(8,128)(2,1)S(1)} collective-permute-done((bf16[2,2,32,1024]{3,2,1,0:T(8,128)(2,1)S(1)}, bf16[2,2,32,1024]{3,2,1,0:T(8,128)(2,1)S(1)}, u32[]{:S(2)}, u32[]{:S(2)}) %collective-permute-start.44) | collective-permute-done | bytes 262176 | tf_op jit(solution)/shard_map/ppermute | solution.py:36
  386.6 11.2 %collective-permute-done.34 = bf16[2,2,32,3072]{3,2,1,0:T(8,128)(2,1)} collective-permute-done((bf16[2,2,32,3072]{3,2,1,0:T(8,128)(2,1)}, bf16[2,2,32,3072]{3,2,1,0:T(8,128)(2,1)}, u32[]{:S(2)}, u32[]{:S(2)}) %collective-permute-start.34) | collective-permute-done | bytes 786464 | tf_op jit(solution)/shard_map/ppermute | solution.py:36
  426.9 13.9 %collective-permute-done.58 = bf16[2,2,128,1024]{3,2,1,0:T(8,128)(2,1)} collective-permute-done((bf16[2,2,128,1024]{3,2,1,0:T(8,128)(2,1)}, bf16[2,2,128,1024]{3,2,1,0:T(8,128)(2,1)}, u32[]{:S(2)}, u32[]{:S(2)}) %collective-permute-start.58) | collective-permute-done | bytes 1048608 | tf_op jit(solution)/shard_map/ppermute | solution.py:36
  447.5 12.1 %collective-permute-done.50 = bf16[2,2,32,4096]{3,2,1,0:T(8,128)(2,1)S(1)} collective-permute-done((bf16[2,2,32,4096]{3,2,1,0:T(8,128)(2,1)S(1)}, bf16[2,2,32,4096]{3,2,1,0:T(8,128)(2,1)S(1)}, u32[]{:S(2)}, u32[]{:S(2)}) %collective-permute-start.50) | collective-permute-done | bytes 1048608 | tf_op jit(solution)/shard_map/ppermute | solution.py:36
  463.4 8.3 %collective-permute-done.59 = bf16[2,128,1024]{2,1,0:T(8,128)(2,1)S(1)} collective-permute-done((bf16[2,128,1024]{2,1,0:T(8,128)(2,1)S(1)}, bf16[2,128,1024]{2,1,0:T(8,128)(2,1)S(1)}, u32[]{:S(2)}, u32[]{:S(2)}) %collective-permute-start.59) | collective-permute-done | bytes 524320 | tf_op jit(solution)/shard_map/ppermute | solution.py:36
  475.3 6.6 %collective-permute-done.51 = bf16[2,32,4096]{2,1,0:T(8,128)(2,1)S(1)} collective-permute-done((bf16[2,32,4096]{2,1,0:T(8,128)(2,1)S(1)}, bf16[2,32,4096]{2,1,0:T(8,128)(2,1)S(1)}, u32[]{:S(2)}, u32[]{:S(2)}) %collective-permute-start.51) | collective-permute-done | bytes 524320 | tf_op jit(solution)/shard_map/ppermute | solution.py:36
  490.4 5.4 %collective-permute-done.62 = bf16[128,1024]{1,0:T(8,128)(2,1)S(1)} collective-permute-done((bf16[128,1024]{1,0:T(8,128)(2,1)S(1)}, bf16[128,1024]{1,0:T(8,128)(2,1)S(1)}, u32[]{:S(2)}, u32[]{:S(2)}) %collective-permute-start.62) | collective-permute-done | bytes 262176 | tf_op jit(solution)/shard_map/ppermute | solution.py:39
  495.8 5.3 %collective-permute-start.56 = (bf16[32,4096]{1,0:T(8,128)(2,1)S(1)}, bf16[32,4096]{1,0:T(8,128)(2,1)S(1)}, u32[]{:S(2)}, u32[]{:S(2)}) collective-permute-start(bf16[32,4096]{1,0:T(8,128)(2,1)S(1)} %get-tuple-element.55), channel_id=1, source_target_pairs={{0,3},{1,2},{2,1},{3,0},{4,7},{5,6},{6,5},{7,4},{8,11},{9,10},{10,... | collective-permute-start | bytes 786440 | tf_op jit(solution)/shard_map/ppermute | solution.py:39
  506.4 17.9 %collective-permute-done.55 = bf16[32,4096]{1,0:T(8,128)(2,1)S(1)} collective-permute-done((bf16[32,4096]{1,0:T(8,128)(2,1)S(1)}, bf16[32,4096]{1,0:T(8,128)(2,1)S(1)}, u32[]{:S(2)}, u32[]{:S(2)}) %collective-permute-start.55) | collective-permute-done | bytes 262176 | tf_op jit(solution)/shard_map/ppermute | solution.py:39
  (442 shorter events, 272.0 us)
Async XLA Ops:
  20.0 136.5 %all-to-all-start = ((bf16[32,19,1024]{2,1,0:T(8,128)(2,1)}), bf16[32,19,1024]{2,1,0:T(8,128)(2,1)}, u32[]{:S(2)}, u32[]{:S(2)}) async-start(bf16[32,19,1024]{2,1,0:T(8,128)(2,1)} %pad_maximum_fusion), calls=%async_computation | async-start | bytes 3145728 | tf_op jit(solution)/shard_map/all_to_all | solution.py:268
  30.2 32.0 %collective-permute-start.15 = (bf16[32,4096]{1,0:T(8,128)(2,1)S(1)}, bf16[32,4096]{1,0:T(8,128)(2,1)S(1)}, u32[]{:S(2)}, u32[]{:S(2)}) collective-permute-start(bf16[32,4096]{1,0:T(8,128)(2,1)S(1)} %copy-done.46), channel_id=1, source_target_pairs={{0,3},{1,2},{2,1},{3,0},{4,7},{5,6},{6,5},{7,4},{8,11},{9,10},{10,... | collective-permute-start | bytes 786440 | tf_op jit(solution)/shard_map/ppermute | solution.py:39
  38.8 47.4 %collective-permute-start.14 = (bf16[32,4096]{1,0:T(8,128)(2,1)S(1)}, bf16[32,4096]{1,0:T(8,128)(2,1)S(1)}, u32[]{:S(2)}, u32[]{:S(2)}) collective-permute-start(bf16[32,4096]{1,0:T(8,128)(2,1)S(1)} %copy-done.46), channel_id=1, source_target_pairs={{0,2},{1,3},{2,0},{3,1},{4,6},{5,7},{6,4},{7,5},{8,10},{9,11},{10,... | collective-permute-start | bytes 786440 | tf_op jit(solution)/shard_map/ppermute | solution.py:39
  38.8 47.4 %collective-permute-start.11 = (bf16[32,4096]{1,0:T(8,128)(2,1)S(1)}, bf16[32,4096]{1,0:T(8,128)(2,1)S(1)}, u32[]{:S(2)}, u32[]{:S(2)}) collective-permute-start(bf16[32,4096]{1,0:T(8,128)(2,1)S(1)} %copy-done.46), channel_id=1, source_target_pairs={{0,1},{1,0},{2,3},{3,2},{4,5},{5,4},{6,7},{7,6},{8,9},{9,8},{10,11... | collective-permute-start | bytes 786440 | tf_op jit(solution)/shard_map/ppermute | solution.py:39
  41.2 50.9 %collective-permute-start.5 = (bf16[64,4096]{1,0:T(8,128)(2,1)S(1)}, bf16[64,4096]{1,0:T(8,128)(2,1)S(1)}, u32[]{:S(2)}, u32[]{:S(2)}) collective-permute-start(bf16[64,4096]{1,0:T(8,128)(2,1)S(1)} %pad_maximum_fusion.5), channel_id=1, source_target_pairs={{0,16},{4,20},{8,24},{12,28},{16,0},{20,4},{24,8},{28,12},{1,17},{... | collective-permute-start | bytes 1572872 | tf_op jit(solution)/shard_map/ppermute | solution.py:36
  43.7 69.3 %collective-permute-start.1 = (bf16[64,4096]{1,0:T(8,128)(2,1)S(1)}, bf16[64,4096]{1,0:T(8,128)(2,1)S(1)}, u32[]{:S(2)}, u32[]{:S(2)}) collective-permute-start(bf16[64,4096]{1,0:T(8,128)(2,1)S(1)} %pad_maximum_fusion.4), channel_id=1, source_target_pairs={{0,8},{4,12},{8,0},{12,4},{16,24},{20,28},{24,16},{28,20},{1,9},{5... | collective-permute-start | bytes 1572872 | tf_op jit(solution)/shard_map/ppermute | solution.py:36
  111.6 66.3 %collective-permute-start.9 = (bf16[128,4096]{1,0:T(8,128)(2,1)S(1)}, bf16[128,4096]{1,0:T(8,128)(2,1)}, u32[]{:S(2)}, u32[]{:S(2)}) collective-permute-start(bf16[128,4096]{1,0:T(8,128)(2,1)S(1)} %constant_dynamic-update-slice_fusion.2.refs_2_), channel_id=1, source_target_pairs={{0,4},{4,0},{8,12},{12,8},{16,20},{20,16},{24,28},{28,24},{1,5},{5... | collective-permute-start | bytes 3145736 | tf_op jit(solution)/shard_map/ppermute | solution.py:36
  112.4 43.6 %collective-permute-start.6 = (bf16[128,4096]{1,0:T(8,128)(2,1)S(1)}, bf16[128,4096]{1,0:T(8,128)(2,1)}, u32[]{:S(2)}, u32[]{:S(2)}) collective-permute-start(bf16[128,4096]{1,0:T(8,128)(2,1)S(1)} %constant_dynamic-update-slice_fusion.2.refs_2_), channel_id=1, source_target_pairs={{0,8},{4,12},{8,0},{12,4},{16,24},{20,28},{24,16},{28,20},{1,9},{5... | collective-permute-start | bytes 3145736 | tf_op jit(solution)/shard_map/ppermute | solution.py:36
  116.3 40.2 %collective-permute-start.2 = (bf16[128,4096]{1,0:T(8,128)(2,1)S(1)}, bf16[128,4096]{1,0:T(8,128)(2,1)}, u32[]{:S(2)}, u32[]{:S(2)}) collective-permute-start(bf16[128,4096]{1,0:T(8,128)(2,1)S(1)} %pad_maximum_fusion.3.refs_0_), channel_id=1, source_target_pairs={{0,16},{4,20},{8,24},{12,28},{16,0},{20,4},{24,8},{28,12},{1,17},{... | collective-permute-start | bytes 3145736 | tf_op jit(solution)/shard_map/ppermute | solution.py:36
  127.9 51.5 %collective-permute-start.7 = (bf16[128,4096]{1,0:T(8,128)(2,1)S(1)}, bf16[128,4096]{1,0:T(8,128)(2,1)}, u32[]{:S(2)}, u32[]{:S(2)}) collective-permute-start(bf16[128,4096]{1,0:T(8,128)(2,1)S(1)} %pad_maximum_fusion.3.refs_0_), channel_id=1, source_target_pairs={{0,4},{4,0},{8,12},{12,8},{16,20},{20,16},{24,28},{28,24},{1,5},{5... | collective-permute-start | bytes 3145736 | tf_op jit(solution)/shard_map/ppermute | solution.py:36
  155.1 43.0 %collective-permute-start.18 = (bf16[128,4096]{1,0:T(8,128)(2,1)}, bf16[128,4096]{1,0:T(8,128)(2,1)}, u32[]{:S(2)}, u32[]{:S(2)}) collective-permute-start(bf16[128,4096]{1,0:T(8,128)(2,1)} %constant_dynamic-update-slice_fusion.5.refs_0_), channel_id=1, source_target_pairs={{0,4},{4,0},{8,12},{12,8},{16,20},{20,16},{24,28},{28,24},{1,5},{5... | collective-permute-start | bytes 3145736 | tf_op jit(solution)/shard_map/ppermute | solution.py:36
  179.4 36.3 %collective-permute-start.20 = (bf16[128,4096]{1,0:T(8,128)(2,1)}, bf16[128,4096]{1,0:T(8,128)(2,1)}, u32[]{:S(2)}, u32[]{:S(2)}) collective-permute-start(bf16[128,4096]{1,0:T(8,128)(2,1)} %copy-done.6), channel_id=1, source_target_pairs={{0,4},{4,0},{8,12},{12,8},{16,20},{20,16},{24,28},{28,24},{1,5},{5... | collective-permute-start | bytes 3145736 | tf_op jit(solution)/shard_map/ppermute | solution.py:36
  181.0 45.2 %collective-permute-start.24 = (bf16[512,1024]{1,0:T(8,128)(2,1)}, bf16[512,1024]{1,0:T(8,128)(2,1)}, u32[]{:S(2)}, u32[]{:S(2)}) collective-permute-start(bf16[512,1024]{1,0:T(8,128)(2,1)} %constant_dynamic-update-slice_fusion.11.refs_0_), channel_id=1, source_target_pairs={{0,16},{4,20},{8,24},{12,28},{16,0},{20,4},{24,8},{28,12},{1,17},{... | collective-permute-start | bytes 3145736 | tf_op jit(solution)/shard_map/ppermute | solution.py:36
  215.7 41.2 %collective-permute-start.29 = (bf16[512,1024]{1,0:T(8,128)(2,1)}, bf16[512,1024]{1,0:T(8,128)(2,1)}, u32[]{:S(2)}, u32[]{:S(2)}) collective-permute-start(bf16[512,1024]{1,0:T(8,128)(2,1)} %constant_dynamic-update-slice_fusion.11.refs_0_), channel_id=1, source_target_pairs={{0,4},{4,0},{8,12},{12,8},{16,20},{20,16},{24,28},{28,24},{1,5},{5... | collective-permute-start | bytes 3145736 | tf_op jit(solution)/shard_map/ppermute | solution.py:36
  313.1 53.3 %all-to-all-start.1 = ((bf16[32,19,1024]{2,1,0:T(8,128)(2,1)}), bf16[32,19,1024]{2,1,0:T(8,128)(2,1)S(1)}, u32[]{:S(2)}, u32[]{:S(2)}) async-start(bf16[32,19,1024]{2,1,0:T(8,128)(2,1)} %pad_maximum_fusion.2), calls=%async_computation.1 | async-start | bytes 3145728 | tf_op jit(solution)/shard_map/all_to_all | solution.py:268
  321.3 49.5 %collective-permute-start.33 = (bf16[512,3072]{1,0:T(8,128)(2,1)}, bf16[512,3072]{1,0:T(8,128)(2,1)}, u32[]{:S(2)}, u32[]{:S(2)}) collective-permute-start(bf16[512,3072]{1,0:T(8,128)(2,1)} %convolution_convert_fusion.1), channel_id=1, source_target_pairs={{0,4},{4,0},{8,12},{12,8},{16,20},{20,16},{24,28},{28,24},{1,5},{5... | collective-permute-start | bytes 9437192 | tf_op jit(solution)/shard_map/ppermute | solution.py:36
  337.1 71.0 %collective-permute-start.57 = (bf16[2048,1024]{1,0:T(8,128)(2,1)}, bf16[2048,1024]{1,0:T(8,128)(2,1)}, u32[]{:S(2)}, u32[]{:S(2)}) collective-permute-start(bf16[2048,1024]{1,0:T(8,128)(2,1)} %convolution_convert_fusion.2), channel_id=1, source_target_pairs={{0,4},{4,0},{8,12},{12,8},{16,20},{20,16},{24,28},{28,24},{1,5},{5... | collective-permute-start | bytes 12582920 | tf_op jit(solution)/shard_map/ppermute | solution.py:36
  364.4 53.3 %collective-permute-start.49 = (bf16[512,4096]{1,0:T(8,128)(2,1)}, bf16[512,4096]{1,0:T(8,128)(2,1)}, u32[]{:S(2)}, u32[]{:S(2)}) collective-permute-start(bf16[512,4096]{1,0:T(8,128)(2,1)} %convolution_convert_fusion), channel_id=1, source_target_pairs={{0,4},{4,0},{8,12},{12,8},{16,20},{20,16},{24,28},{28,24},{1,5},{5... | collective-permute-start | bytes 12582920 | tf_op jit(solution)/shard_map/ppermute | solution.py:36
  422.3 37.3 %collective-permute-start.50 = (bf16[2,2,32,4096]{3,2,1,0:T(8,128)(2,1)S(1)}, bf16[2,2,32,4096]{3,2,1,0:T(8,128)(2,1)S(1)}, u32[]{:S(2)}, u32[]{:S(2)}) collective-permute-start(bf16[2,2,32,4096]{3,2,1,0:T(8,128)(2,1)S(1)} %fusion.32), channel_id=1, source_target_pairs={{0,16},{4,20},{8,24},{12,28},{16,0},{20,4},{24,8},{28,12},{1,17},{... | collective-permute-start | bytes 3145736 | tf_op jit(solution)/shard_map/ppermute | solution.py:36
  424.0 37.3 %collective-permute-start.52 = (bf16[2,2,32,4096]{3,2,1,0:T(8,128)(2,1)S(1)}, bf16[2,2,32,4096]{3,2,1,0:T(8,128)(2,1)S(1)}, u32[]{:S(2)}, u32[]{:S(2)}) collective-permute-start(bf16[2,2,32,4096]{3,2,1,0:T(8,128)(2,1)S(1)} %fusion.34), channel_id=1, source_target_pairs={{0,8},{4,12},{8,0},{12,4},{16,24},{20,28},{24,16},{28,20},{1,9},{5... | collective-permute-start | bytes 3145736 | tf_op jit(solution)/shard_map/ppermute | solution.py:36
  426.2 59.7 %collective-permute-start.38 = (bf16[32,3072]{1,0:T(8,128)(2,1)S(1)}, bf16[32,3072]{1,0:T(8,128)(2,1)S(1)}, u32[]{:S(2)}, u32[]{:S(2)}) collective-permute-start(bf16[32,3072]{1,0:T(8,128)(2,1)S(1)} %get-tuple-element.58), channel_id=1, source_target_pairs={{0,1},{1,0},{2,3},{3,2},{4,5},{5,4},{6,7},{7,6},{8,9},{9,8},{10,11... | collective-permute-start | bytes 589832 | tf_op jit(solution)/shard_map/ppermute | solution.py:39
  440.8 46.4 %collective-permute-start.39 = (bf16[32,3072]{1,0:T(8,128)(2,1)S(1)}, bf16[32,3072]{1,0:T(8,128)(2,1)S(1)}, u32[]{:S(2)}, u32[]{:S(2)}) collective-permute-start(bf16[32,3072]{1,0:T(8,128)(2,1)S(1)} %get-tuple-element.59), channel_id=1, source_target_pairs={{0,2},{1,3},{2,0},{3,1},{4,6},{5,7},{6,4},{7,5},{8,10},{9,11},{10,... | collective-permute-start | bytes 589832 | tf_op jit(solution)/shard_map/ppermute | solution.py:39
  444.0 43.3 %collective-permute-start.40 = (bf16[32,3072]{1,0:T(8,128)(2,1)S(1)}, bf16[32,3072]{1,0:T(8,128)(2,1)S(1)}, u32[]{:S(2)}, u32[]{:S(2)}) collective-permute-start(bf16[32,3072]{1,0:T(8,128)(2,1)S(1)} %get-tuple-element.60), channel_id=1, source_target_pairs={{0,3},{1,2},{2,1},{3,0},{4,7},{5,6},{6,5},{7,4},{8,11},{9,10},{10,... | collective-permute-start | bytes 589832 | tf_op jit(solution)/shard_map/ppermute | solution.py:39
  487.3 37.1 %collective-permute-start.55 = (bf16[32,4096]{1,0:T(8,128)(2,1)S(1)}, bf16[32,4096]{1,0:T(8,128)(2,1)S(1)}, u32[]{:S(2)}, u32[]{:S(2)}) collective-permute-start(bf16[32,4096]{1,0:T(8,128)(2,1)S(1)} %get-tuple-element.54), channel_id=1, source_target_pairs={{0,2},{1,3},{2,0},{3,1},{4,6},{5,7},{6,4},{7,5},{8,10},{9,11},{10,... | collective-permute-start | bytes 786440 | tf_op jit(solution)/shard_map/ppermute | solution.py:39
  (109 other events, 1667.8 us)

commit v2 on v1

v2 whole, which is shorter than its diff:
```python
import jax
import jax.numpy as jnp
from jax import lax
from jax.experimental import pallas as pl
from jax.experimental.pallas import tpu as pltpu
from jax.sharding import PartitionSpec as P

HEADS = 16
HEAD_DIM = 64
EPSILON = 1e-05
AXES = ("dp", "fsdp")
BF16 = jnp.bfloat16
F32 = jnp.float32


class Grid:
    def __init__(self, n_dp, n_z):
        self.n_dp, self.n_z = n_dp, n_z
        side = 1
        while side * side * 2 < n_dp:
            side *= 2
        self.nx, self.ny = side, n_dp // (2 * side)
        self.x_masks = [2 * k for k in range(1, self.nx)]
        self.y_masks = [2 * side * k for k in range(1, self.ny)]
        self.z_masks = list(range(1, n_z))

    def bind(self):
        self.my_dp = lax.axis_index("dp").astype(jnp.int32)
        self.my_z = lax.axis_index("fsdp").astype(jnp.int32)
        self.me = lax.axis_index(AXES).astype(jnp.int32)

    def over_dp(self, value, mask):
        return lax.ppermute(value, "dp", [(i, i ^ mask) for i in range(self.n_dp)])

    def over_z(self, value, mask):
        return lax.ppermute(value, "fsdp", [(i, i ^ mask) for i in range(self.n_z)])


class Clock:
    def __init__(self):
        self.last = ()

    def gate(self, *values):
        held = lax.optimization_barrier(tuple(values) + self.last)[: len(values)]
        return held if len(values) > 1 else held[0]

    def tick(self, *values):
        self.last = values


class Gather:
    def __init__(self, grid, clock, shard, col_cuts):
        self.grid, self.clock, self.cuts = grid, clock, col_cuts
        self.shard = shard

    def step0(self):
        shard = self.clock.gate(self.shard)
        far = [m for m in self.grid.z_masks if m % 2 == 0]
        self.near = [(shard, 0)]
        self.coming = [(self.grid.over_z(shard, m), m) for m in far]

    def step1(self):
        grid = self.grid
        got = self.clock.gate(*[v for v, _ in self.coming], self.shard)[:-1]
        got = [(v, m) for v, (_, m) in zip(got, self.coming)]
        parts = self.near + got
        low = jnp.concatenate([v for v, _ in parts], 0)
        self.clock.tick(low)
        self.low = (low, [m for _, m in parts])
        self.high = (grid.over_z(low, 1), [m ^ 1 for m in self.low[1]])
        self.low_got = [(grid.over_dp(low, m), m) for m in grid.x_masks]

    def step2(self):
        high = self.clock.gate(self.high[0], self.shard)[0]
        self.clock.tick(high)
        self.high = (high, self.high[1])
        self.high_got = [(self.grid.over_dp(high, m), m) for m in self.grid.y_masks]

    def join(self, have, coming):
        got = self.clock.gate(*[v for v, _ in coming], have[0])[:-1]
        rows = jnp.concatenate([have[0], *got], 0)
        marks = list(have[1])
        for _, m in coming:
            marks += [(d ^ m, z) for d, z in have[1]]
        self.clock.tick(rows)
        return rows, marks

    def step3(self):
        low = (self.low[0], [(0, z) for z in self.low[1]])
        self.low = self.join(low, self.low_got)
        self.low_got = [(self.grid.over_dp(self.low[0], m), m) for m in self.grid.y_masks]

    def step4(self):
        high = (self.high[0], [(0, z) for z in self.high[1]])
        self.high = self.join(high, self.high_got)
        self.high_got = [(self.grid.over_dp(self.high[0], m), m) for m in self.grid.x_masks]

    def step5(self):
        self.low = self.join(self.low, self.low_got)
        self.low_got = self.grid.over_dp(self.low[0], 1)

    def step6(self):
        self.high = self.join(self.high, self.high_got)
        self.high_got = self.grid.over_dp(self.high[0], 1)

    def step7(self):
        grid = self.grid
        block = self.shard.shape[0]
        rows = block * grid.n_dp * grid.n_z
        spans = list(zip([0] + self.cuts[:-1], self.cuts))
        pieces = []
        for (mine, marks), theirs in ((self.low, self.low_got), (self.high, self.high_got)):
            pieces.append((mine, [d * grid.n_z + z for d, z in marks]))
            pieces.append((theirs, [(d ^ 1) * grid.n_z + z for d, z in marks]))
        copies = sum(len(marks) for _, marks in pieces) * len(spans)

        def kernel(me_ref, *refs):
            sources = refs[: len(pieces)]
            outs = refs[len(pieces) : len(pieces) + len(spans)]
            sems = refs[-1]
            started = []
            for source, (_, marks) in zip(sources, pieces):
                for at, mark in enumerate(marks):
                    owner = lax.bitwise_xor(me_ref[0], jnp.int32(mark))
                    to = pl.ds(pl.multiple_of(owner * block, block), block)
                    for out, (lo, hi) in zip(outs, spans):
                        copy = pltpu.make_async_copy(
                            source.at[pl.ds(at * block, block), pl.ds(lo, hi - lo)],
                            out.at[to],
                            sems.at[len(started)],
                        )
                        copy.start()
                        started.append(copy)
            for copy in started:
                copy.wait()

        arrays = self.clock.gate(*[v for v, _ in pieces])
        full = pl.pallas_call(
            kernel,
            out_shape=[jax.ShapeDtypeStruct((rows, hi - lo), BF16) for lo, hi in spans],
            grid_spec=pltpu.PrefetchScalarGridSpec(
                num_scalar_prefetch=1,
                grid=(),
                in_specs=[pl.BlockSpec(memory_space=pl.ANY)] * len(pieces),
                out_specs=[pl.BlockSpec(memory_space=pltpu.VMEM)] * len(spans),
                scratch_shapes=[pltpu.SemaphoreType.DMA((copies,))],
            ),
            compiler_params=pltpu.CompilerParams(vmem_limit_bytes=20 << 20),
            cost_estimate=pl.CostEstimate(flops=0, bytes_accessed=0, transcendentals=0),
            name="assemble",
        )(grid.me.reshape(1), *arrays)
        self.clock.tick(*full)
        return full


class PlainGather:
    def __init__(self, grid, clock, shard, col_cuts):
        self.clock, self.shard, self.cuts = clock, shard, col_cuts

    def step0(self):
        self.full = lax.all_gather(self.shard, AXES, axis=0, tiled=True)

    def step1(self):
        pass

    step2 = step3 = step4 = step5 = step6 = step1

    def step7(self):
        return [self.full[:, lo:hi] for lo, hi in zip([0] + self.cuts[:-1], self.cuts)]


def make_gather(grid, clock, shard, col_cuts):
    kind = PlainGather if shard.shape[0] % 16 else Gather
    return kind(grid, clock, shard, col_cuts)


def contract_rows(left, right):
    return lax.dot_general(left, right, (((0,), (0,)), ((), ())), preferred_element_type=F32)


def back_dot(grad_rows, weight):
    return lax.dot_general(grad_rows, weight, (((1,), (1,)), ((), ())), preferred_element_type=F32)


def pick(array, index):
    return lax.dynamic_index_in_dim(array, index, 0, keepdims=False)


def total_of(base, parts):
    for part in parts:
        base = base + part.astype(F32)
    return base


class Scatter:
    def __init__(self, grid, clock, left, right):
        self.grid, self.clock, self.left, self.right = grid, clock, left, right
        self.places = grid.ny * grid.nx
        self.chunk = left.shape[1] // grid.n_dp
        self.cols = right.shape[1]

    def call(self, kernel, mask, ins, in_specs, out_shape, out_specs):
        tokens = self.left.shape[0]
        left, right, *ins = self.clock.gate(self.left, self.right, *ins)
        return pl.pallas_call(
            kernel,
            out_shape=out_shape,
            grid_spec=pltpu.PrefetchScalarGridSpec(
                num_scalar_prefetch=1,
                grid=(self.places,),
                in_specs=[
                    pl.BlockSpec(
                        (tokens, self.chunk),
                        lambda j, dp: (0, lax.bitwise_xor(dp[0], 2 * j + mask)),
                    ),
                    pl.BlockSpec((tokens, self.cols), lambda j, dp: (0, 0)),
                    *in_specs,
                ],
                out_specs=out_specs,
            ),
            compiler_params=pltpu.CompilerParams(vmem_limit_bytes=20 << 20),
            cost_estimate=pl.CostEstimate(
                flops=2 * tokens * self.chunk * self.places * self.cols,
                bytes_accessed=4 * self.chunk * self.places * self.cols,
                transcendentals=0,
            ),
            name="outer",
        )(self.grid.my_dp.reshape(1), left, right, *ins)

    def across(self):
        def kernel(dp_ref, left, right, out):
            out[...] = contract_rows(left[...], right[...]).astype(BF16)

        spec = pl.BlockSpec((self.chunk, self.cols), lambda j, dp: (j, 0))
        shape = jax.ShapeDtypeStruct((self.chunk * self.places, self.cols), BF16)
        send = self.call(kernel, 1, (), (), shape, spec)
        self.clock.tick(send)
        self.got = self.grid.over_dp(send, 1)

    def first(self):
        grid = self.grid
        nx, ny, cols = grid.nx, grid.ny, self.cols
        half = self.chunk // 2

        def kernel(dp_ref, left, right, got, low_keep, low_send, high_keep, high_send):
            j = pl.program_id(0)
            py, px = j // nx, j % nx
            held = contract_rows(left[...], right[...]) + got[...].astype(F32)

            @pl.when(py == 0)
            def _():
                low_keep[0] = held[:half]

            @pl.when(py != 0)
            def _():
                low_send[0] = held[:half].astype(BF16)

            @pl.when(px == 0)
            def _():
                high_keep[0] = held[half:]

            @pl.when(px != 0)
            def _():
                high_send[0] = held[half:].astype(BF16)

        def block(index):
            return pl.BlockSpec((1, half, cols), lambda j, dp: (index(j // nx, j % nx), 0, 0))

        def low_send_at(y, x):
            return jnp.where(y == 0, 0, (y - 1) * nx + x)

        def high_send_at(y, x):
            return (jnp.maximum(x, 1) - 1) * ny + y

        low_keep, low_send, high_keep, high_send = self.call(
            kernel,
            0,
            (self.got,),
            [pl.BlockSpec((self.chunk, cols), lambda j, dp: (j, 0))],
            [
                jax.ShapeDtypeStruct((nx, half, cols), F32),
                jax.ShapeDtypeStruct(((ny - 1) * nx, half, cols), BF16),
                jax.ShapeDtypeStruct((ny, half, cols), F32),
                jax.ShapeDtypeStruct(((nx - 1) * ny, half, cols), BF16),
            ],
            [
                block(lambda y, x: jnp.where(y == 0, x, nx - 1)),
                block(low_send_at),
                block(lambda y, x: y),
                block(high_send_at),
            ],
        )
        self.clock.tick(low_send, high_send)
        self.keep = (low_keep, high_keep)
        self.low_got = [
            grid.over_dp(low_send[k * nx : (k + 1) * nx], m) for k, m in enumerate(grid.y_masks)
        ]
        self.high_got = [
            grid.over_dp(high_send[k * ny : (k + 1) * ny], m) for k, m in enumerate(grid.x_masks)
        ]

    def second(self):
        grid = self.grid
        got = self.clock.gate(*self.low_got, *self.high_got)
        count = len(self.low_got)
        low_keep, high_keep = self.keep
        low_got, high_got = got[:count], got[count:]
        low_send = total_of(low_keep[1:], [g[1:] for g in low_got]).astype(BF16)
        high_send = total_of(high_keep[1:], [g[1:] for g in high_got]).astype(BF16)
        self.clock.tick(low_send, high_send)
        self.keep = (
            total_of(low_keep[0], [g[0] for g in low_got]),
            total_of(high_keep[0], [g[0] for g in high_got]),
        )
        self.low_got = [grid.over_dp(low_send[k], m) for k, m in enumerate(grid.x_masks)]
        self.high_got = [grid.over_dp(high_send[k], m) for k, m in enumerate(grid.y_masks)]

    def third(self):
        grid = self.grid
        got = self.clock.gate(*self.low_got, *self.high_got)
        count = len(self.low_got)
        low = total_of(self.keep[0], got[:count])
        high = total_of(self.keep[1], got[count:])
        lines = jnp.concatenate([low, high], 0).reshape(grid.n_z // 2, 2, -1, self.cols)
        odd = grid.my_z % 2
        send = lax.dynamic_index_in_dim(lines, 1 - odd, 1, keepdims=False).astype(BF16)
        self.keep = lax.dynamic_index_in_dim(lines, odd, 1, keepdims=False)
        self.clock.tick(send)
        self.line = grid.over_z(send, 1)

    def fourth(self):
        grid = self.grid
        held = self.keep + self.clock.gate(self.line).astype(F32)
        pair = grid.my_z // 2
        sends = [pick(held, pair ^ (m // 2)).astype(BF16) for m in grid.z_masks if m % 2 == 0]
        self.keep = pick(held, pair)
        self.clock.tick(*sends)
        far = [m for m in grid.z_masks if m % 2 == 0]
        self.line = [grid.over_z(v, m) for v, m in zip(sends, far)]

    def done(self):
        got = self.clock.gate(*self.line, self.keep)[:-1]
        out = total_of(self.keep, got)
        self.clock.tick(out)
        return out


class PlainScatter:
    def __init__(self, grid, clock, left, right):
        self.left, self.right = left, right

    def across(self):
        term = contract_rows(self.left, self.right)
        self.out = lax.psum_scatter(term, AXES, scatter_dimension=0, tiled=True)

    def first(self):
        pass

    second = third = fourth = first

    def done(self):
        return self.out


def make_scatter(grid, clock, left, right):
    kind = PlainScatter if (left.shape[1] // grid.n_dp) % 128 else Scatter
    return kind(grid, clock, left, right)


def lookup(small_table, index_rows):
    matches = index_rows[:, None] == jnp.arange(small_table.shape[0], dtype=jnp.int32)[None, :]
    return jnp.sum(jnp.where(matches, small_table[None, :], 0), axis=1)


def rank_among(group_label, order_key):
    earlier = (group_label[None, :] == group_label[:, None]) & (
        order_key[None, :] < order_key[:, None]
    )
    return jnp.sum(earlier.astype(jnp.int32), axis=1)


def routing(lengths, deal_order, devices, row_count, device):
    slot_count = deal_order.shape[0]
    slot_ids = jnp.arange(slot_count, dtype=jnp.int32)
    starts = jnp.cumsum(lengths) - lengths
    slot_of = jnp.sum(
        jnp.where(deal_order[None, :] == slot_ids[:, None], slot_ids[None, :], 0), axis=1
    )
    slot_lengths = lookup(lengths, deal_order)
    local_rows = jnp.arange(row_count, dtype=jnp.int32)
    token_index = local_rows * devices + device
    sequence = jnp.sum((starts[None, :] <= token_index[:, None]).astype(jnp.int32), axis=1) - 1
    slot_index = lookup(slot_of, sequence)
    target = slot_index // 2
    send_rank = rank_among(target, local_rows)
    first_len = lax.dynamic_index_in_dim(slot_lengths, 2 * device, 0, False)
    second = local_rows >= first_len
    first_seq = lax.dynamic_index_in_dim(deal_order, 2 * device, 0, False)
    second_seq = lax.dynamic_index_in_dim(deal_order, 2 * device + 1, 0, False)
    sequence_here = jnp.where(second, second_seq, first_seq)
    position = local_rows - jnp.where(second, first_len, 0)
    source_token = lookup(starts, sequence_here) + position
    source = source_token % devices
    take_rank = rank_among(source, source_token)
    return target, send_rank, source, take_rank, second.astype(jnp.int32), position


def standardize(values):
    centered = values - jnp.mean(values, axis=-1, keepdims=True)
    scale = lax.rsqrt(jnp.mean(centered * centered, axis=-1, keepdims=True) + EPSILON)
    return centered * scale, scale


def standardize_back(grad, unit, scale):
    return scale * (
        grad
        - jnp.mean(grad, axis=-1, keepdims=True)
        - unit * jnp.mean(grad * unit, axis=-1, keepdims=True)
    )


def col_sum(values):
    return jnp.sum(values.astype(F32), axis=0)


def on_device(
    n_dp,
    n_z,
    rows_in,
    cotangent,
    lengths,
    deal_order,
    w_qkv,
    b_query,
    b_value,
    w_out,
    b_out,
    gain_one,
    shift_one,
    w_up,
    b_up,
    w_down,
    b_down,
    gain_two,
    shift_two,
):
    grid = Grid(n_dp, n_z)
    grid.bind()
    clock = Clock()
    devices = n_dp * n_z
    row_count, _, width = rows_in.shape
    hidden = w_up.shape[1]
    share = width // devices

    attn = make_gather(
        grid, clock, jnp.concatenate([w_qkv, w_out], axis=1), [3 * width, 4 * width]
    )
    up = make_gather(grid, clock, w_up, [hidden])
    down = make_gather(grid, clock, w_down, [width])

    attn.step0()

    target, send_rank, source, take_rank, segment, position = routing(
        lengths, deal_order, devices, row_count, grid.me
    )
    slot_rows = row_count // devices + 1
    block_rows = -(-(2 * slot_rows + 1) // 8) * 8
    slots = devices * block_rows
    slot_ids = jnp.arange(slots, dtype=jnp.int32)
    send_at = target * block_rows + send_rank
    take_at = source * block_rows + take_rank
    send_both = jnp.concatenate([send_at, send_at + slot_rows])
    take_both = jnp.concatenate([take_at, take_at + slot_rows])
    to_slots = (slot_ids[:, None] == send_both[None, :]).astype(BF16)
    from_slots = (take_both[:, None] == slot_ids[None, :]).astype(BF16)
    last_row = (slot_ids % block_rows == 2 * slot_rows)[:, None]

    def all_swap(block):
        block = block.reshape(devices, block_rows, width)
        return lax.all_to_all(block, AXES, split_axis=0, concat_axis=0, tiled=True)

    small = jnp.concatenate(
        [b_query, b_value, b_out, gain_one, shift_one, b_down, gain_two, shift_two, b_up]
    )
    small = jnp.pad(small, (0, width - small.shape[0]))
    block = jnp.dot(
        to_slots[:, :row_count], rows_in.reshape(row_count, width), preferred_element_type=F32
    )
    block += jnp.dot(
        to_slots[:, row_count:], cotangent.reshape(row_count, width), preferred_element_type=F32
    )
    block = block.astype(BF16)
    block = jnp.where(last_row, small[None, :], block)
    clock.tick(block)
    attn.step1()
    up.step0()
    arrived = all_swap(clock.gate(block))
    attn.step2()
    attn.step3()
    up.step1()
    attn.step4()
    down.step0()
    up.step2()
    up.step3()

    arrived = clock.gate(arrived)
    taken = jnp.dot(from_slots, arrived.reshape(slots, width), preferred_element_type=F32)
    grad_m_b = taken[row_count:].astype(BF16)
    inputs = taken[:row_count]
    small_all = arrived[:, 2 * slot_rows].astype(F32)
    vectors = [small_all[:, k * share : (k + 1) * share].reshape(width) for k in range(8)]
    bq, bv, bo, g1, s1, bd, g2, s2 = vectors
    bu = small_all[:, 8 * share : 8 * share + hidden // devices].reshape(hidden)
    unit_one, scale_one = standardize(inputs)
    normed_one_b = (unit_one * g1 + s1).astype(BF16)
    clock.tick(normed_one_b, grad_m_b)
    term_b_down = col_sum(grad_m_b)

    attn.step5()
    down.step1()
    up.step4()
    attn.step6()
    down.step2()
    down.step3()
    full_qkv, full_out = attn.step7()

    mixed = jnp.dot(clock.gate(normed_one_b), full_qkv, preferred_element_type=F32)
    head_shape = (row_count, HEADS, HEAD_DIM)
    query_b = (mixed[:, :width] + bq).astype(BF16).reshape(head_shape)
    key_b = mixed[:, width : 2 * width].astype(BF16).reshape(head_shape)
    value_b = (mixed[:, 2 * width :] + bv).astype(BF16).reshape(head_shape)
    allowed = (segment[:, None] == segment[None, :]) & (position[None, :] <= position[:, None])
    scale_factor = HEAD_DIM ** (-0.5)
    scores = jnp.einsum("qhd,khd->hqk", query_b, key_b, preferred_element_type=F32)
    masked = jnp.where(allowed[None], scores * scale_factor, -1000000000.0)
    exps = jnp.exp(masked - jnp.max(masked, axis=-1, keepdims=True))
    softmax_f = exps / jnp.sum(exps, axis=-1, keepdims=True)
    softmax_b = softmax_f.astype(BF16)
    attended_b = jnp.einsum("hqk,khd->qhd", softmax_b, value_b, preferred_element_type=F32)
    attended_b = attended_b.reshape(row_count, width).astype(BF16)
    hidden_one = inputs + jnp.dot(attended_b, full_out, preferred_element_type=F32) + bo
    unit_two, scale_two = standardize(hidden_one)
    normed_two_b = (unit_two * g2 + s2).astype(BF16)
    clock.tick(normed_two_b)

    up.step5()
    down.step4()
    up.step6()
    (full_up,) = up.step7()
    pre_act = jnp.dot(clock.gate(normed_two_b), full_up, preferred_element_type=F32) + bu
    half_cdf = 0.5 * (1.0 + lax.erf(pre_act * (0.5**0.5)))
    activation_b = (pre_act * half_cdf).astype(BF16)
    density = jnp.exp(-0.5 * pre_act * pre_act) * ((2.0 * jnp.pi) ** -0.5)
    slope = half_cdf + pre_act * density
    clock.tick(activation_b, slope)

    for_down = make_scatter(grid, clock, activation_b, grad_m_b)
    for_down.across()
    down.step5()
    down.step6()
    for_down.first()
    (full_down,) = down.step7()

    grad_pre_b = (back_dot(clock.gate(grad_m_b), full_down) * slope).astype(BF16)
    clock.tick(grad_pre_b)
    term_b_up = col_sum(grad_pre_b)
    for_up = make_scatter(grid, clock, normed_two_b, grad_pre_b)
    for_up.across()

    grad_normed_two = back_dot(clock.gate(grad_pre_b), full_up)
    term_g2 = col_sum(grad_normed_two * unit_two)
    term_s2 = col_sum(grad_normed_two)
    grad_hidden = grad_m_b.astype(F32) + standardize_back(grad_normed_two * g2, unit_two, scale_two)
    grad_branch_b = grad_hidden.astype(BF16)
    clock.tick(grad_branch_b)
    term_b_out = col_sum(grad_branch_b)
    for_down.second()
    for_up.first()

    for_out = make_scatter(grid, clock, attended_b, grad_branch_b)
    for_out.across()
    grad_att_b = back_dot(clock.gate(grad_branch_b), full_out).astype(BF16)
    clock.tick(grad_att_b)
    for_down.third()
    for_out.first()

    grad_att_b = clock.gate(grad_att_b).reshape(head_shape)
    grad_probs = jnp.einsum("qhd,khd->hqk", grad_att_b, value_b, preferred_element_type=F32)
    grad_scores_b = (
        softmax_f * (grad_probs - jnp.sum(softmax_f * grad_probs, axis=-1, keepdims=True))
    ).astype(BF16)
    grad_query = jnp.einsum("hqk,khd->qhd", grad_scores_b, key_b, preferred_element_type=F32)
    grad_key = jnp.einsum("hqk,qhd->khd", grad_scores_b, query_b, preferred_element_type=F32)
    grad_value = jnp.einsum("hqk,qhd->khd", softmax_b, grad_att_b, preferred_element_type=F32)
    grad_mixed_b = jnp.concatenate(
        [
            (grad_query * scale_factor).astype(BF16).reshape(row_count, width),
            (grad_key * scale_factor).astype(BF16).reshape(row_count, width),
            grad_value.astype(BF16).reshape(row_count, width),
        ],
        axis=1,
    )
    clock.tick(grad_mixed_b)
    term_mixed = col_sum(grad_mixed_b)
    for_up.second()
    for_qkv = make_scatter(grid, clock, normed_one_b, grad_mixed_b)
    for_qkv.across()

    grad_normed_one = back_dot(clock.gate(grad_mixed_b), full_qkv)
    term_g1 = col_sum(grad_normed_one * unit_one)
    term_s1 = col_sum(grad_normed_one)
    grad_inputs = grad_hidden + standardize_back(grad_normed_one * g1, unit_one, scale_one)
    grad_inputs_b = grad_inputs.astype(BF16)
    clock.tick(grad_inputs_b)
    for_qkv.first()
    for_out.second()
    for_up.third()
    for_down.fourth()

    result = jnp.dot(clock.gate(activation_b), full_down, preferred_element_type=F32)
    result_b = (hidden_one + result + bd).astype(BF16)
    terms = [term_mixed[:width], term_mixed[2 * width :], term_b_out, term_g1, term_s1]
    terms += [term_b_down, term_g2, term_s2, term_b_up]
    terms = jnp.concatenate([v.reshape(devices, -1) for v in terms], axis=1)
    count = terms.shape[1]
    top = lax.reduce_precision(terms, 8, 7)
    small_back = jnp.concatenate([top, terms - top], axis=1).astype(BF16)
    small_back = jnp.pad(small_back, ((0, 0), (0, width - 2 * count)))
    small_back = jnp.broadcast_to(small_back[:, None], (devices, block_rows, width))
    both = jnp.concatenate([result_b, grad_inputs_b], axis=0)
    block = contract_rows(from_slots, both).astype(BF16)
    block = jnp.where(last_row, small_back.reshape(slots, width), block)
    clock.tick(block)
    returned = all_swap(block)

    for_qkv.second()
    for_out.third()
    for_up.fourth()
    for_qkv.third()
    for_out.fourth()
    grad_w_down = for_down.done()
    for_qkv.fourth()
    grad_w_up = for_up.done()
    grad_w_out = for_out.done()
    returned = clock.gate(returned)
    placed = contract_rows(to_slots, returned.reshape(slots, width)).astype(BF16)
    sums = jnp.sum(returned[:, 2 * slot_rows].astype(F32), axis=0)
    clock.tick(placed)
    grad_w_qkv = for_qkv.done()

    sums = sums[:count] + sums[count : 2 * count]
    cut = [sums[k * share : (k + 1) * share] for k in range(8)]
    grad_bq, grad_bv, grad_bo, grad_g1, grad_s1, grad_bd, grad_g2, grad_s2 = cut
    grad_bu = sums[8 * share :]
    return (
        placed[:row_count].reshape(row_count, 1, width),
        placed[row_count:].reshape(row_count, 1, width),
        grad_w_qkv,
        grad_bq,
        grad_bv,
        grad_w_out,
        grad_bo,
        grad_g1,
        grad_s1,
        grad_w_up,
        grad_bu,
        grad_w_down,
        grad_bd,
        grad_g2,
        grad_s2,
    )


def solution(mesh):
    n_dp, n_z = mesh.shape["dp"], mesh.shape["fsdp"]
    rows, vec, mat = P(None, AXES, None), P(AXES), P(AXES, None)

    def run(*args):
        return on_device(n_dp, n_z, *args)

    return jax.shard_map(
        run,
        mesh=mesh,
        in_specs=(rows, rows, P(), P())
        + (mat, vec, vec, mat, vec, vec, vec, mat, vec, mat, vec, vec, vec),
        out_specs=(rows, rows, mat, vec, vec, mat, vec, vec, vec, mat, vec, mat, vec, vec, vec),
        check_vma=False,
    )
```

time: 536 us -> 418 us (0.78); the launches traced: 526 us -> 413 us
  waiting for transfers between devices: 205 us -> 140 us
  local copies, waits for them, and re-layouts: 98.4 us -> 66.1 us
  starting transfers between devices: 90 us -> 64.1 us
  matrix products: 82.1 us -> 60.2 us
  Pallas kernels: 11.2 us -> 31.8 us
  other arithmetic: 36.1 us -> 49.1 us
    ppermute x21 -> x14, waiting for transfers between devices: 84.9 us -> 46.8 us  [over_z(): return lax.ppermute(value, 'fsdp', [(i, i ^ mask) for i in range(self.n_z)])]
    ppermute x44 -> x38, waiting for transfers between devices: 120 us -> 92.8 us  [over_dp(): return lax.ppermute(value, 'dp', [(i, i ^ mask) for i in range(self.n_dp)])]
    dot_general x18 -> x8, matrix products: 49.6 us -> 23.2 us  [the longest x1 5.79 us: on_device(): jnp.dot(clock.gate(normed_two_b), full_up, preferred_element_type=F32) + bu]
    ppermute x21 -> x14, starting transfers between devices: 41.2 us -> 19.9 us  [over_z(): return lax.ppermute(value, 'fsdp', [(i, i ^ mask) for i in range(self.n_z)])]
    pallas_call x3 -> x11, Pallas kernels: 11.2 us -> 31.8 us  [the longest x8 24.7 us: call(): pl.pallas_call(kernel, out_shape=out_shape, grid_spec=pltpu.PrefetchScala...]
    dynamic_slice x4 -> x0, local copies, waits for them, and re-layouts: 14.7 us -> none  [pick(): return lax.dynamic_index_in_dim(array, index, axis, keepdims=False)]
    reshape x11 -> x4, local copies, waits for them, and re-layouts: 18.3 us -> 4.05 us  [the longest x1 1.03 us: on_device(): placed[row_count:].reshape(row_count, 1, width)]
    convert_element_type x5 -> x10, other arithmetic: 1.5 us -> 13 us  [the longest x4 5.11 us: second(): high_send = total_of(high_keep[1:], [g[1:] for g in high_got]).astype(BF16)]
  transfers between devices with their start and end apart: 67 -> 54, of which waited for: 27 -> 18; matrix products, arithmetic and copies ran while one was open for 32% -> 32% of each run, Pallas kernels for 1% -> 5%
where the time goes in v2:
time: 418 us; the launch traced here: 413 us
  waiting for transfers between devices  140 us (33%)
  local copies, waits for them, and re-layouts  66.1 us (16%)
  starting transfers between devices  64.1 us (15%)
  matrix products  60.2 us (14%)
  other arithmetic  49.1 us (12%)
  Pallas kernels  31.8 us (8%)
    ppermute x38, waiting for transfers between devices, over_dp(): return lax.ppermute(value, 'dp', [(i, i ^ mask) for i in range(self.n_dp)])  92.8 us
    ppermute x14, waiting for transfers between devices, over_z(): return lax.ppermute(value, 'fsdp', [(i, i ^ mask) for i in range(self.n_z)])  46.8 us
    unnamed x232, local copies, waits for them, and re-layouts  37.9 us
    ppermute x38, starting transfers between devices, over_dp(): return lax.ppermute(value, 'dp', [(i, i ^ mask) for i in range(self.n_dp)])  35.7 us
    pallas_call x8, Pallas kernels, call(): pl.pallas_call(kernel, out_shape=out_shape, grid_spec=pltpu.PrefetchScala...  24.7 us
    ppermute x14, starting transfers between devices, over_z(): return lax.ppermute(value, 'fsdp', [(i, i ^ mask) for i in range(self.n_z)])  19.9 us
    dot_general x4, matrix products, back_dot(): lax.dot_general(grad_rows, weight, (((1,), (1,)), ((), ())), preferred_el...  19.2 us
    add x12, other arithmetic, total_of(): base = base + part.astype(F32)  12.7 us
  transfers between devices with their start and end apart: 54, of which 18 were waited for; matrix products, arithmetic and copies ran while one was open for 32% of the time, Pallas kernels for 5%

profile of v2, /device:TPU:0, one launch (start us, length us, event | category | flops | bytes accessed | tf_op | source)
XLA Modules:
  0.0 413.2 jit_solution(14114947770465534013)
XLA Ops:
  2.5 4.0 collective-permute-start
  17.7 3.7 broadcast_select_fusion
  25.7 4.4 %all-to-all-start = ((bf16[32,24,1024]{2,1,0:T(8,128)(2,1)}), bf16[32,24,1024]{2,1,0:T(8,128)(2,1)S(1)}, u32[]{:S(2)}, u32[]{:S(2)}) async-start(bf16[32,24,1024]{2,1,0:T(8,128)(2,1)} %bitcast.6), calls=%async_computation | async-start | bytes 3145728 | tf_op jit(solution)/shard_map/all_to_all | solution.py:480
  30.9 15.1 %collective-permute-done.3 = bf16[64,4096]{1,0:T(8,128)(2,1)S(1)} collective-permute-done((bf16[64,4096]{1,0:T(8,128)(2,1)}, bf16[64,4096]{1,0:T(8,128)(2,1)S(1)}, u32[]{:S(2)}, u32[]{:S(2)}) %collective-permute-start.3) | collective-permute-done | bytes 524320 | tf_op jit(solution)/shard_map/ppermute | solution.py:36
  53.5 14.6 %collective-permute-done.6 = bf16[64,4096]{1,0:T(8,128)(2,1)S(1)} collective-permute-done((bf16[64,4096]{1,0:T(8,128)(2,1)S(1)}, bf16[64,4096]{1,0:T(8,128)(2,1)S(1)}, u32[]{:S(2)}, u32[]{:S(2)}) %collective-permute-start.6) | collective-permute-done | bytes 524320 | tf_op jit(solution)/shard_map/ppermute | solution.py:33
  71.7 6.3 %collective-permute-done.5 = bf16[64,4096]{1,0:T(8,128)(2,1)} collective-permute-done((bf16[64,4096]{1,0:T(8,128)(2,1)S(1)}, bf16[64,4096]{1,0:T(8,128)(2,1)}, u32[]{:S(2)}, u32[]{:S(2)}) %collective-permute-start.5) | collective-permute-done | bytes 524320 | tf_op jit(solution)/shard_map/ppermute | solution.py:36
  95.6 4.4 %collective-permute-done.10 = bf16[64,4096]{1,0:T(8,128)(2,1)} collective-permute-done((bf16[64,4096]{1,0:T(8,128)(2,1)}, bf16[64,4096]{1,0:T(8,128)(2,1)}, u32[]{:S(2)}, u32[]{:S(2)}) %collective-permute-start.10) | collective-permute-done | bytes 524320 | tf_op jit(solution)/shard_map/ppermute | solution.py:33
  110.7 8.5 %collective-permute-done.14 = bf16[256,1024]{1,0:T(8,128)(2,1)} collective-permute-done((bf16[256,1024]{1,0:T(8,128)(2,1)}, bf16[256,1024]{1,0:T(8,128)(2,1)}, u32[]{:S(2)}, u32[]{:S(2)}) %collective-permute-start.14) | collective-permute-done | bytes 524320 | tf_op jit(solution)/shard_map/ppermute | solution.py:36
  127.5 4.2 %assemble.3 = (bf16[1024,3072]{1,0:T(8,128)(2,1)S(1)}, bf16[1024,1024]{1,0:T(8,128)(2,1)S(1)}) custom-call(s32[1]{0:T(128)} %bitcast.8.me_ref, bf16[256,4096]{1,0:T(8,128)(2,1)S(1)} %pad_maximum_fusion.refs_0_, bf16[256,4096]{1,0:T(8,128)(2,1)} %collective-permute-done.8.refs_1_, bf16[256,4096]{1,0:T(8,128)(2,1)} %constant_dynamic-update-slice_fusion.13.refs_2_, ...), custom_call_target="tpu_custom_call" | custom-call | tf_op jit(solution)/shard_map/assemble/pallas_call | solution.py:138
  135.9 3.4 fusion.61
  150.1 5.9 %collective-permute-done.20.refs_3_ = bf16[256,4096]{1,0:T(8,128)(2,1)S(1)} collective-permute-done((bf16[256,4096]{1,0:T(8,128)(2,1)S(1)}, bf16[256,4096]{1,0:T(8,128)(2,1)S(1)}, u32[]{:S(2)}, u32[]{:S(2)}) %collective-permute-start.20) | collective-permute-done | bytes 2097184 | tf_op jit(solution)/shard_map/ppermute | solution.py:33
  158.8 5.8 %multiply_convert_fusion.1 = (bf16[256,4096]{1,0:T(8,128)(2,1)S(1)}, f32[256,4096]{1,0:T(8,128)}) fusion(f32[4096]{0:T(1024)S(1)} %slice_bitcast_fusion.2, bf16[256,1024]{1,0:T(8,128)(2,1)S(1)} %add_convert_fusion.6.left, bf16[1024,4096]{1,0:T(8,128)(2,1)S(1)} %assemble.4), kind=kOutput, calls=%fused_computation.12 | convolution fusion | flops 2159017984 | bytes 15220736 | tf_op jit(solution)/shard_map/dot_general | solution.py:550
  167.6 24.6 %collective-permute-done.15 = bf16[512,1024]{1,0:T(8,128)(2,1)S(1)} collective-permute-done((bf16[512,1024]{1,0:T(8,128)(2,1)S(1)}, bf16[512,1024]{1,0:T(8,128)(2,1)S(1)}, u32[]{:S(2)}, u32[]{:S(2)}) %collective-permute-start.15) | collective-permute-done | bytes 1048608 | tf_op jit(solution)/shard_map/ppermute | solution.py:33
  201.6 8.3 %convert_reduce_fusion = (f32[4096]{0:T(1024)}, bf16[256,4096]{1,0:T(8,128)(2,1)S(1)}) fusion(f32[256,4096]{1,0:T(8,128)} %get-tuple-element.251, bf16[256,1024]{1,0:T(8,128)(2,1)S(1)} %get-tuple-element.165.right, bf16[4096,1024]{1,0:T(8,128)(2,1)S(1)} %assemble.5), kind=kOutput, calls=%fused_computation.9 | convolution fusion | flops 2151673856 | bytes 15220736 | tf_op jit(solution)/shard_map/dot_general | solution.py:182
  209.9 3.5 outer.10
  219.2 19.8 %collective-permute-done.26 = bf16[2,256,1024]{2,1,0:T(8,128)(2,1)S(1)} collective-permute-done((bf16[2,256,1024]{2,1,0:T(8,128)(2,1)S(1)}, bf16[2,256,1024]{2,1,0:T(8,128)(2,1)S(1)}, u32[]{:S(2)}, u32[]{:S(2)}) %collective-permute-start.26) | collective-permute-done | bytes 1048608 | tf_op jit(solution)/shard_map/ppermute | solution.py:33
  243.0 5.6 %outer.11 = (f32[2,64,4096]{2,1,0:T(8,128)S(1)}, bf16[2,64,4096]{2,1,0:T(8,128)(2,1)}, f32[2,64,4096]{2,1,0:T(8,128)S(1)}, bf16[2,64,4096]{2,1,0:T(8,128)(2,1)}) custom-call(s32[1]{0:T(128)} %bitcast.14.dp_ref, bf16[256,1024]{1,0:T(8,128)(2,1)S(1)} %copy-done.8, bf16[256,4096]{1,0:T(8,128)(2,1)S(1)} %get-tuple-element.174.right, ...), custom_call_target="tpu_custom_call" | custom-call | flops 1073741824 | bytes 8388608 | tf_op jit(solution)/shard_map/outer/pallas_call | solution.py:205
  297.9 6.6 %multiply_reduce_fusion.3 = (f32[1024]{0:T(1024)S(1)}, f32[256]{0:T(256)}, f32[256]{0:T(256)}, f32[1024]{0:T(1024)S(1)}, f32[256,1024]{1,0:T(8,128)}) fusion(f32[256]{0:T(256)S(1)} %copy-done.90, f32[256]{0:T(256)S(1)} %copy-done.84, f32[512,1024]{1,0:T(8,128)} %copy-done.42, f32[1024]{0:T(1024)S(1)} %copy-done.82, ...), kind=kOutput, calls=%fused_computation.70 | convolution fusion | flops 1612969472 | bytes 9977856 | tf_op jit(solution)/shard_map/dot_general | solution.py:182
  312.4 5.3 %outer.15 = (f32[2,64,3072]{2,1,0:T(8,128)S(1)}, bf16[2,64,3072]{2,1,0:T(8,128)(2,1)}, f32[2,64,3072]{2,1,0:T(8,128)S(1)}, bf16[2,64,3072]{2,1,0:T(8,128)(2,1)}) custom-call(s32[1]{0:T(128)} %bitcast.14.dp_ref, bf16[256,1024]{1,0:T(8,128)(2,1)S(1)} %copy-done.6, bf16[256,3072]{1,0:T(8,128)(2,1)S(1)} %get-tuple-element.198.right, ...), custom_call_target="tpu_custom_call" | custom-call | flops 805306368 | bytes 6291456 | tf_op jit(solution)/shard_map/outer/pallas_call | solution.py:205
  340.8 4.0 all-to-all-start.1
  349.0 11.8 %collective-permute-done.39 = bf16[64,1024]{1,0:T(8,128)(2,1)S(1)} collective-permute-done((bf16[64,1024]{1,0:T(8,128)(2,1)S(1)}, bf16[64,1024]{1,0:T(8,128)(2,1)S(1)}, u32[]{:S(2)}, u32[]{:S(2)}) %collective-permute-start.39) | collective-permute-done | bytes 131104 | tf_op jit(solution)/shard_map/ppermute | solution.py:33
  366.9 5.1 %collective-permute-start.48 = (bf16[32,4096]{1,0:T(8,128)(2,1)S(1)}, bf16[32,4096]{1,0:T(8,128)(2,1)S(1)}, u32[]{:S(2)}, u32[]{:S(2)}) collective-permute-start(bf16[32,4096]{1,0:T(8,128)(2,1)S(1)} %fusion.36), channel_id=1, source_target_pairs={{0,2},{1,3},{2,0},{3,1},{4,6},{5,7},{6,4},{7,5},{8,10},{9,11},{10,... | collective-permute-start | bytes 786440 | tf_op jit(solution)/shard_map/ppermute | solution.py:36
  372.0 5.4 %collective-permute-done.45 = bf16[64,3072]{1,0:T(8,128)(2,1)S(1)} collective-permute-done((bf16[64,3072]{1,0:T(8,128)(2,1)S(1)}, bf16[64,3072]{1,0:T(8,128)(2,1)S(1)}, u32[]{:S(2)}, u32[]{:S(2)}) %collective-permute-start.45) | collective-permute-done | bytes 393248 | tf_op jit(solution)/shard_map/ppermute | solution.py:33
  387.1 13.9 %collective-permute-done.49 = bf16[2,32,3072]{2,1,0:T(8,128)(2,1)S(1)} collective-permute-done((bf16[2,32,3072]{2,1,0:T(8,128)(2,1)S(1)}, bf16[2,32,3072]{2,1,0:T(8,128)(2,1)S(1)}, u32[]{:S(2)}, u32[]{:S(2)}) %collective-permute-start.49) | collective-permute-done | bytes 393248 | tf_op jit(solution)/shard_map/ppermute | solution.py:36
  (474 shorter events, 216.5 us)
Async XLA Ops:
  25.7 59.6 %all-to-all-start = ((bf16[32,24,1024]{2,1,0:T(8,128)(2,1)}), bf16[32,24,1024]{2,1,0:T(8,128)(2,1)S(1)}, u32[]{:S(2)}, u32[]{:S(2)}) async-start(bf16[32,24,1024]{2,1,0:T(8,128)(2,1)} %bitcast.6), calls=%async_computation | async-start | bytes 3145728 | tf_op jit(solution)/shard_map/all_to_all | solution.py:480
  50.4 27.7 %collective-permute-start.5 = (bf16[64,4096]{1,0:T(8,128)(2,1)S(1)}, bf16[64,4096]{1,0:T(8,128)(2,1)}, u32[]{:S(2)}, u32[]{:S(2)}) collective-permute-start(bf16[64,4096]{1,0:T(8,128)(2,1)S(1)} %get-tuple-element.281), channel_id=1, source_target_pairs={{0,1},{1,0},{2,3},{3,2},{4,5},{5,4},{6,7},{7,6},{8,9},{9,8},{10,11... | collective-permute-start | bytes 1572872 | tf_op jit(solution)/shard_map/ppermute | solution.py:36
  50.4 29.2 %collective-permute-start.4 = (bf16[64,4096]{1,0:T(8,128)(2,1)S(1)}, bf16[64,4096]{1,0:T(8,128)(2,1)S(1)}, u32[]{:S(2)}, u32[]{:S(2)}) collective-permute-start(bf16[64,4096]{1,0:T(8,128)(2,1)S(1)} %get-tuple-element.281), channel_id=1, source_target_pairs={{0,8},{4,12},{8,0},{12,4},{16,24},{20,28},{24,16},{28,20},{1,9},{5... | collective-permute-start | bytes 1572872 | tf_op jit(solution)/shard_map/ppermute | solution.py:33
  53.0 39.0 %collective-permute-start.7 = (bf16[128,4096]{1,0:T(8,128)(2,1)}, bf16[128,4096]{1,0:T(8,128)(2,1)}, u32[]{:S(2)}, u32[]{:S(2)}) collective-permute-start(bf16[128,4096]{1,0:T(8,128)(2,1)} %pad_maximum_fusion.5), channel_id=1, source_target_pairs={{0,16},{4,20},{8,24},{12,28},{16,0},{20,4},{24,8},{28,12},{1,17},{... | collective-permute-start | bytes 3145736 | tf_op jit(solution)/shard_map/ppermute | solution.py:33
  69.2 32.8 %collective-permute-start.9 = (bf16[128,4096]{1,0:T(8,128)(2,1)}, bf16[128,4096]{1,0:T(8,128)(2,1)}, u32[]{:S(2)}, u32[]{:S(2)}) collective-permute-start(bf16[128,4096]{1,0:T(8,128)(2,1)} %get-tuple-element.270), channel_id=1, source_target_pairs={{0,8},{4,12},{8,0},{12,4},{16,24},{20,28},{24,16},{28,20},{1,9},{5... | collective-permute-start | bytes 3145736 | tf_op jit(solution)/shard_map/ppermute | solution.py:33
  109.1 35.1 %collective-permute-start.16 = (bf16[128,4096]{1,0:T(8,128)(2,1)}, bf16[128,4096]{1,0:T(8,128)(2,1)}, u32[]{:S(2)}, u32[]{:S(2)}) collective-permute-start(bf16[128,4096]{1,0:T(8,128)(2,1)} %get-tuple-element.268), channel_id=1, source_target_pairs={{0,16},{4,20},{8,24},{12,28},{16,0},{20,4},{24,8},{28,12},{1,17},{... | collective-permute-start | bytes 3145736 | tf_op jit(solution)/shard_map/ppermute | solution.py:33
  119.3 28.9 %collective-permute-start.18 = (bf16[128,4096]{1,0:T(8,128)(2,1)}, bf16[128,4096]{1,0:T(8,128)(2,1)}, u32[]{:S(2)}, u32[]{:S(2)}) collective-permute-start(bf16[128,4096]{1,0:T(8,128)(2,1)} %copy-done.72), channel_id=1, source_target_pairs={{0,8},{4,12},{8,0},{12,4},{16,24},{20,28},{24,16},{28,20},{1,9},{5... | collective-permute-start | bytes 3145736 | tf_op jit(solution)/shard_map/ppermute | solution.py:33
  121.8 25.2 %collective-permute-start.19 = (bf16[256,1024]{1,0:T(8,128)(2,1)}, bf16[256,1024]{1,0:T(8,128)(2,1)}, u32[]{:S(2)}, u32[]{:S(2)}) collective-permute-start(bf16[256,1024]{1,0:T(8,128)(2,1)} %collective-permute-done.14), channel_id=1, source_target_pairs={{0,16},{4,20},{8,24},{12,28},{16,0},{20,4},{24,8},{28,12},{1,17},{... | collective-permute-start | bytes 1572872 | tf_op jit(solution)/shard_map/ppermute | solution.py:33
  166.5 26.8 %collective-permute-start.24 = (bf16[2048,1024]{1,0:T(8,128)(2,1)S(1)}, bf16[2048,1024]{1,0:T(8,128)(2,1)S(1)}, u32[]{:S(2)}, u32[]{:S(2)}) collective-permute-start(bf16[2048,1024]{1,0:T(8,128)(2,1)S(1)} %outer.8), channel_id=1, source_target_pairs={{0,4},{4,0},{8,12},{12,8},{16,20},{20,16},{24,28},{28,24},{1,5},{5... | collective-permute-start | bytes 12582920 | tf_op jit(solution)/shard_map/ppermute | solution.py:33
  166.8 25.4 %collective-permute-start.15 = (bf16[512,1024]{1,0:T(8,128)(2,1)S(1)}, bf16[512,1024]{1,0:T(8,128)(2,1)S(1)}, u32[]{:S(2)}, u32[]{:S(2)}) collective-permute-start(bf16[512,1024]{1,0:T(8,128)(2,1)S(1)} %copy-done.80), channel_id=1, source_target_pairs={{0,16},{4,20},{8,24},{12,28},{16,0},{20,4},{24,8},{28,12},{1,17},{... | collective-permute-start | bytes 3145736 | tf_op jit(solution)/shard_map/ppermute | solution.py:33
  167.6 25.1 %collective-permute-start.22 = (bf16[512,1024]{1,0:T(8,128)(2,1)S(1)}, bf16[512,1024]{1,0:T(8,128)(2,1)S(1)}, u32[]{:S(2)}, u32[]{:S(2)}) collective-permute-start(bf16[512,1024]{1,0:T(8,128)(2,1)S(1)} %get-tuple-element.258), channel_id=1, source_target_pairs={{0,8},{4,12},{8,0},{12,4},{16,24},{20,28},{24,16},{28,20},{1,9},{5... | collective-permute-start | bytes 3145736 | tf_op jit(solution)/shard_map/ppermute | solution.py:33
  213.4 29.5 %collective-permute-start.25 = (bf16[512,4096]{1,0:T(8,128)(2,1)}, bf16[512,4096]{1,0:T(8,128)(2,1)}, u32[]{:S(2)}, u32[]{:S(2)}) collective-permute-start(bf16[512,4096]{1,0:T(8,128)(2,1)} %outer.10), channel_id=1, source_target_pairs={{0,4},{4,0},{8,12},{12,8},{16,20},{20,16},{24,28},{28,24},{1,5},{5... | collective-permute-start | bytes 12582920 | tf_op jit(solution)/shard_map/ppermute | solution.py:33
  213.5 25.5 %collective-permute-start.26 = (bf16[2,256,1024]{2,1,0:T(8,128)(2,1)S(1)}, bf16[2,256,1024]{2,1,0:T(8,128)(2,1)S(1)}, u32[]{:S(2)}, u32[]{:S(2)}) collective-permute-start(bf16[2,256,1024]{2,1,0:T(8,128)(2,1)S(1)} %copy-done.37), channel_id=1, source_target_pairs={{0,16},{4,20},{8,24},{12,28},{16,0},{20,4},{24,8},{28,12},{1,17},{... | collective-permute-start | bytes 3145736 | tf_op jit(solution)/shard_map/ppermute | solution.py:33
  214.7 25.2 %collective-permute-start.27 = (bf16[2,256,1024]{2,1,0:T(8,128)(2,1)S(1)}, bf16[2,256,1024]{2,1,0:T(8,128)(2,1)S(1)}, u32[]{:S(2)}, u32[]{:S(2)}) collective-permute-start(bf16[2,256,1024]{2,1,0:T(8,128)(2,1)S(1)} %copy-done.35), channel_id=1, source_target_pairs={{0,8},{4,12},{8,0},{12,4},{16,24},{20,28},{24,16},{28,20},{1,9},{5... | collective-permute-start | bytes 3145736 | tf_op jit(solution)/shard_map/ppermute | solution.py:33
  254.2 32.8 %collective-permute-start.31 = (bf16[2,64,4096]{2,1,0:T(8,128)(2,1)}, bf16[2,64,4096]{2,1,0:T(8,128)(2,1)}, u32[]{:S(2)}, u32[]{:S(2)}) collective-permute-start(bf16[2,64,4096]{2,1,0:T(8,128)(2,1)} %get-tuple-element.176), channel_id=1, source_target_pairs={{0,16},{4,20},{8,24},{12,28},{16,0},{20,4},{24,8},{28,12},{1,17},{... | collective-permute-start | bytes 3145736 | tf_op jit(solution)/shard_map/ppermute | solution.py:33
  255.5 31.5 %collective-permute-start.32 = (bf16[2,64,4096]{2,1,0:T(8,128)(2,1)}, bf16[2,64,4096]{2,1,0:T(8,128)(2,1)}, u32[]{:S(2)}, u32[]{:S(2)}) collective-permute-start(bf16[2,64,4096]{2,1,0:T(8,128)(2,1)} %get-tuple-element.177), channel_id=1, source_target_pairs={{0,8},{4,12},{8,0},{12,4},{16,24},{20,28},{24,16},{28,20},{1,9},{5... | collective-permute-start | bytes 3145736 | tf_op jit(solution)/shard_map/ppermute | solution.py:33
  295.3 35.4 %collective-permute-start.33 = (bf16[2,128,1024]{2,1,0:T(8,128)(2,1)}, bf16[2,128,1024]{2,1,0:T(8,128)(2,1)}, u32[]{:S(2)}, u32[]{:S(2)}) collective-permute-start(bf16[2,128,1024]{2,1,0:T(8,128)(2,1)} %fusion.28), channel_id=1, source_target_pairs={{0,1},{1,0},{2,3},{3,2},{4,5},{5,4},{6,7},{7,6},{8,9},{9,8},{10,11... | collective-permute-start | bytes 1572872 | tf_op jit(solution)/shard_map/ppermute | solution.py:36
  296.8 24.5 %collective-permute-start.37 = (bf16[2,64,1024]{2,1,0:T(8,128)(2,1)S(1)}, bf16[2,64,1024]{2,1,0:T(8,128)(2,1)}, u32[]{:S(2)}, u32[]{:S(2)}) collective-permute-start(bf16[2,64,1024]{2,1,0:T(8,128)(2,1)S(1)} %get-tuple-element.187), channel_id=1, source_target_pairs={{0,8},{4,12},{8,0},{12,4},{16,24},{20,28},{24,16},{28,20},{1,9},{5... | collective-permute-start | bytes 786440 | tf_op jit(solution)/shard_map/ppermute | solution.py:33
  320.1 24.8 %collective-permute-start.41 = (bf16[2,64,3072]{2,1,0:T(8,128)(2,1)}, bf16[2,64,3072]{2,1,0:T(8,128)(2,1)}, u32[]{:S(2)}, u32[]{:S(2)}) collective-permute-start(bf16[2,64,3072]{2,1,0:T(8,128)(2,1)} %get-tuple-element.200), channel_id=1, source_target_pairs={{0,16},{4,20},{8,24},{12,28},{16,0},{20,4},{24,8},{28,12},{1,17},{... | collective-permute-start | bytes 2359304 | tf_op jit(solution)/shard_map/ppermute | solution.py:33
  321.3 25.3 %collective-permute-start.42 = (bf16[2,64,3072]{2,1,0:T(8,128)(2,1)}, bf16[2,64,3072]{2,1,0:T(8,128)(2,1)}, u32[]{:S(2)}, u32[]{:S(2)}) collective-permute-start(bf16[2,64,3072]{2,1,0:T(8,128)(2,1)} %get-tuple-element.201), channel_id=1, source_target_pairs={{0,8},{4,12},{8,0},{12,4},{16,24},{20,28},{24,16},{28,20},{1,9},{5... | collective-permute-start | bytes 2359304 | tf_op jit(solution)/shard_map/ppermute | solution.py:33
  330.5 33.1 %collective-permute-start.46 = (bf16[2,32,4096]{2,1,0:T(8,128)(2,1)}, bf16[2,32,4096]{2,1,0:T(8,128)(2,1)}, u32[]{:S(2)}, u32[]{:S(2)}) collective-permute-start(bf16[2,32,4096]{2,1,0:T(8,128)(2,1)} %fusion.29), channel_id=1, source_target_pairs={{0,1},{1,0},{2,3},{3,2},{4,5},{5,4},{6,7},{7,6},{8,9},{9,8},{10,11... | collective-permute-start | bytes 1572872 | tf_op jit(solution)/shard_map/ppermute | solution.py:36
  334.1 52.1 %collective-permute-start.50 = (bf16[128,1024]{1,0:T(8,128)(2,1)}, bf16[128,1024]{1,0:T(8,128)(2,1)S(1)}, u32[]{:S(2)}, u32[]{:S(2)}) collective-permute-start(bf16[128,1024]{1,0:T(8,128)(2,1)} %fusion.35), channel_id=1, source_target_pairs={{0,2},{1,3},{2,0},{3,1},{4,6},{5,7},{6,4},{7,5},{8,10},{9,11},{10,... | collective-permute-start | bytes 786440 | tf_op jit(solution)/shard_map/ppermute | solution.py:36
  340.8 62.5 %all-to-all-start.1 = ((bf16[32,24,1024]{2,1,0:T(8,128)(2,1)}), bf16[32,24,1024]{2,1,0:T(8,128)(2,1)}, u32[]{:S(2)}, u32[]{:S(2)}) async-start(bf16[32,24,1024]{2,1,0:T(8,128)(2,1)} %bitcast.178), calls=%async_computation.1 | async-start | bytes 3145728 | tf_op jit(solution)/shard_map/all_to_all | solution.py:480
  366.9 34.9 %collective-permute-start.48 = (bf16[32,4096]{1,0:T(8,128)(2,1)S(1)}, bf16[32,4096]{1,0:T(8,128)(2,1)S(1)}, u32[]{:S(2)}, u32[]{:S(2)}) collective-permute-start(bf16[32,4096]{1,0:T(8,128)(2,1)S(1)} %fusion.36), channel_id=1, source_target_pairs={{0,2},{1,3},{2,0},{3,1},{4,6},{5,7},{6,4},{7,5},{8,10},{9,11},{10,... | collective-permute-start | bytes 786440 | tf_op jit(solution)/shard_map/ppermute | solution.py:36
  (139 other events, 1218.1 us)

commit v3 on v2

v3 whole, which is shorter than its diff:
```python
import jax
import jax.numpy as jnp
from jax import lax
from jax.experimental import pallas as pl
from jax.experimental.pallas import tpu as pltpu
from jax.sharding import PartitionSpec as P

HEADS = 16
HEAD_DIM = 64
EPSILON = 1e-05
AXES = ("dp", "fsdp")
BF16 = jnp.bfloat16
F32 = jnp.float32


class Grid:
    def __init__(self, n_dp, n_z):
        self.n_dp, self.n_z = n_dp, n_z
        side = 1
        while side * side * 2 < n_dp:
            side *= 2
        self.nx, self.ny = side, n_dp // (2 * side)
        self.x_masks = [2 * k for k in range(1, self.nx)]
        self.y_masks = [2 * side * k for k in range(1, self.ny)]
        self.z_masks = list(range(1, n_z))
        self.square = self.nx == self.ny == 2 and n_z == 4

    def bind(self):
        self.my_dp = lax.axis_index("dp").astype(jnp.int32)
        self.my_z = lax.axis_index("fsdp").astype(jnp.int32)
        self.me = lax.axis_index(AXES).astype(jnp.int32)

    def over_dp(self, value, mask):
        return lax.ppermute(value, "dp", [(i, i ^ mask) for i in range(self.n_dp)])

    def crossed(self, value, even_mask, odd_mask):
        pairs = [(i, i ^ (odd_mask if i % 2 else even_mask)) for i in range(self.n_dp)]
        return lax.ppermute(value, "dp", pairs)

    def over_z(self, value, mask):
        return lax.ppermute(value, "fsdp", [(i, i ^ mask) for i in range(self.n_z)])


class Clock:
    def __init__(self):
        self.last = ()

    def gate(self, *values):
        held = lax.optimization_barrier(tuple(values) + self.last)[: len(values)]
        return held if len(values) > 1 else held[0]

    def tick(self, *values):
        self.last = values


class Lines:
    def __init__(self, grid, clock, shards):
        self.grid, self.clock = grid, clock
        self.block = shards[0].shape[0]
        self.parts, blocks = [], []
        at = 0
        for shard in shards:
            height, cols = shard.shape
            count = height // self.block
            blocks += [shard[k * self.block : (k + 1) * self.block] for k in range(count)]
            self.parts.append((at, count, cols))
            at += count * cols
        self.shard = jnp.concatenate(blocks, axis=1) if len(blocks) > 1 else blocks[0]

    def step0(self):
        self.held = self.clock.gate(self.shard)
        self.far = [m for m in self.grid.z_masks if m % 2 == 0]
        self.coming = [self.grid.over_z(self.held, m) for m in self.far]

    def step1(self):
        *got, held = self.clock.gate(*self.coming, self.held)
        self.held = jnp.concatenate([held, *got], 0)
        self.clock.tick(self.held)
        self.coming = self.grid.over_z(self.held, 1)

    def step2(self):
        got, held = self.clock.gate(self.coming, self.held)
        z_marks = [0] + self.far
        z_marks += [m ^ 1 for m in z_marks]
        joined = []
        for at, count, cols in self.parts:
            cut = slice(at, at + count * cols)
            joined.append(jnp.concatenate([held[:, cut], got[:, cut]], 0))
        self.clock.tick(*joined)
        return [
            Gather(self.grid, self.clock, rows, z_marks, self.block, count, cols)
            for rows, (_, count, cols) in zip(joined, self.parts)
        ]


class Gather:
    def __init__(self, grid, clock, rows, z_marks, block, count, cols):
        self.grid, self.clock, self.rows = grid, clock, rows
        self.z_marks, self.block, self.count, self.cols = z_marks, block, count, cols
        self.pieces = []

    def take(self, rows, even_mask, odd_mask):
        self.pieces.append((rows, even_mask, odd_mask))
        self.pieces.append((self.grid.over_dp(rows, 1), odd_mask ^ 1, even_mask ^ 1))

    def step0(self):
        grid = self.grid
        (x,), (y,) = grid.x_masks, grid.y_masks
        rows = self.clock.gate(self.rows)
        self.first = grid.crossed(rows, x, y)
        self.second = grid.crossed(rows, y, x)
        self.take(rows, 0, 0)

    def step1(self):
        grid = self.grid
        (x,), (y,) = grid.x_masks, grid.y_masks
        first = self.clock.gate(self.first)
        self.clock.tick(first)
        self.third = grid.crossed(first, y, x)
        self.take(first, x, y)

    def step2(self):
        (x,), (y,) = self.grid.x_masks, self.grid.y_masks
        second = self.clock.gate(self.second)
        self.clock.tick(second)
        self.take(second, y, x)

    def step3(self):
        (x,), (y,) = self.grid.x_masks, self.grid.y_masks
        third = self.clock.gate(self.third)
        self.clock.tick(third)
        self.take(third, x ^ y, x ^ y)

    def done(self, cuts=()):
        grid, block, count = self.grid, self.block, self.count
        pieces, z_marks = self.pieces, self.z_marks
        owners = grid.n_dp * grid.n_z
        edges = [0, *cuts, self.cols]
        spans = list(zip(edges[:-1], edges[1:]))
        copies = owners * count * len(spans)

        def kernel(me_ref, *refs):
            sources = refs[: len(pieces)]
            results = refs[len(pieces) : len(pieces) + len(spans)]
            sems = refs[-1]
            me = me_ref[0]
            odd = (me // grid.n_z) % 2 == 1
            started = []
            for source, (_, even_mask, odd_mask) in zip(sources, pieces):
                mask = jnp.where(odd, jnp.int32(odd_mask), jnp.int32(even_mask))
                for at, z in enumerate(z_marks):
                    owner = lax.bitwise_xor(me, mask * grid.n_z + z)
                    for k in range(count):
                        to = pl.multiple_of((owner * count + k) * block, block)
                        for result, (lo, hi) in zip(results, spans):
                            copy = pltpu.make_async_copy(
                                source.at[
                                    pl.ds(at * block, block), pl.ds(k * self.cols + lo, hi - lo)
                                ],
                                result.at[pl.ds(to, block)],
                                sems.at[len(started)],
                            )
                            copy.start()
                            started.append(copy)
            for copy in started:
                copy.wait()

        arrays = self.clock.gate(*[v for v, _, _ in pieces])
        rows = owners * count * block
        full = pl.pallas_call(
            kernel,
            out_shape=[jax.ShapeDtypeStruct((rows, hi - lo), BF16) for lo, hi in spans],
            grid_spec=pltpu.PrefetchScalarGridSpec(
                num_scalar_prefetch=1,
                grid=(),
                in_specs=[pl.BlockSpec(memory_space=pl.ANY)] * len(pieces),
                out_specs=[pl.BlockSpec(memory_space=pltpu.VMEM)] * len(spans),
                scratch_shapes=[pltpu.SemaphoreType.DMA((copies,))],
            ),
            compiler_params=pltpu.CompilerParams(vmem_limit_bytes=20 << 20),
            cost_estimate=pl.CostEstimate(flops=0, bytes_accessed=0, transcendentals=0),
            name="assemble",
        )(grid.me.reshape(1), *arrays)
        self.clock.tick(*full)
        return full


class PlainLines:
    def __init__(self, grid, clock, shards):
        self.shards = shards

    def step0(self):
        pass

    step1 = step0

    def step2(self):
        return [PlainGather(v) for v in self.shards]


class PlainGather:
    def __init__(self, shard):
        self.full = lax.all_gather(shard, AXES, axis=0, tiled=True)

    def step0(self):
        pass

    step1 = step2 = step3 = step0

    def done(self, cuts=()):
        edges = [0, *cuts, self.full.shape[1]]
        return [self.full[:, lo:hi] for lo, hi in zip(edges[:-1], edges[1:])]


def make_lines(grid, clock, *shards):
    plain = shards[0].shape[0] % 16 or not grid.square
    kind = PlainLines if plain else Lines
    return kind(grid, clock, shards)


def contract_rows(left, right):
    return lax.dot_general(left, right, (((0,), (0,)), ((), ())), preferred_element_type=F32)


def back_dot(grad_rows, weight):
    return lax.dot_general(grad_rows, weight, (((1,), (1,)), ((), ())), preferred_element_type=F32)


def pick(array, index):
    return lax.dynamic_index_in_dim(array, index, 0, keepdims=False)


def total_of(base, parts):
    for part in parts:
        base = base + part.astype(F32)
    return base


class Scatter:
    places = 4

    def __init__(self, grid, clock, left, right):
        self.grid, self.clock, self.left, self.right = grid, clock, left, right
        self.chunk = left.shape[1] // grid.n_dp
        self.cols = right.shape[1]
        once = pl.Buffered(1)
        self.whole = pl.BlockSpec(
            (self.chunk, self.cols), lambda j, dp: (0, 0), pipeline_mode=once
        )
        self.rows = pl.BlockSpec(right.shape, lambda j, dp: (0, 0), pipeline_mode=once)

    def shape(self, dtype):
        return jax.ShapeDtypeStruct((self.chunk, self.cols), dtype)

    def call(self, kernel, other, ins, dtypes):
        tokens = self.left.shape[0]

        def place(j, dp):
            a, b = j // 2, j % 2
            odd = (dp[0] + other) % 2
            mask = jnp.where(odd == 1, 2 * a + 4 * b, 4 * a + 2 * b)
            return 0, lax.bitwise_xor(dp[0], mask + other)

        left, right, *ins = self.clock.gate(self.left, self.right, *ins)
        return pl.pallas_call(
            kernel,
            out_shape=[self.shape(d) for d in dtypes],
            grid_spec=pltpu.PrefetchScalarGridSpec(
                num_scalar_prefetch=1,
                grid=(self.places,),
                in_specs=[
                    pl.BlockSpec((tokens, self.chunk), place),
                    self.rows,
                    *[self.whole for _ in ins],
                ],
                out_specs=[self.whole for _ in dtypes],
            ),
            compiler_params=pltpu.CompilerParams(vmem_limit_bytes=18 << 20),
            cost_estimate=pl.CostEstimate(flops=0, bytes_accessed=0, transcendentals=0),
            name="outer",
        )(self.grid.my_dp.reshape(1), left, right, *ins)

    def across(self):
        def kernel(dp_ref, left, right, *outs):
            term = contract_rows(left[...], right[...]).astype(BF16)
            for k, out in enumerate(outs):

                @pl.when(pl.program_id(0) == k)
                def _(out=out):
                    out[...] = term

        sends = self.call(kernel, 1, (), [BF16] * self.places)
        self.clock.tick(*sends)
        self.got = [self.grid.over_dp(v, 1) for v in sends]

    def first(self):
        grid, places = self.grid, self.places
        (x,), (y,) = grid.x_masks, grid.y_masks

        def kernel(dp_ref, left, right, *refs):
            term = contract_rows(left[...], right[...])
            for k, (got, out) in enumerate(zip(refs[:places], refs[places:])):

                @pl.when(pl.program_id(0) == k)
                def _(got=got, out=out):
                    out[...] = (term + got[...].astype(F32)).astype(out.dtype)

        keep, pass_on, aside, onward = self.call(kernel, 0, self.got, [F32, F32, BF16, BF16])
        self.clock.tick(aside, onward)
        self.keep, self.pass_on = keep, pass_on
        self.got = grid.crossed(onward, y, x)
        self.aside = grid.crossed(aside, y, x)

    def second(self):
        (x,), (y,) = self.grid.x_masks, self.grid.y_masks
        got, pass_on = self.clock.gate(self.got, self.pass_on)
        send = (pass_on + got.astype(F32)).astype(BF16)
        self.clock.tick(send)
        self.got = self.grid.crossed(send, x, y)

    def third(self):
        grid = self.grid
        got, aside, keep = self.clock.gate(self.got, self.aside, self.keep)
        lines = total_of(keep, [got, aside]).reshape(2, 2, -1, self.cols)
        odd = grid.my_z % 2
        send = lax.dynamic_index_in_dim(lines, 1 - odd, 1, keepdims=False).astype(BF16)
        self.keep = lax.dynamic_index_in_dim(lines, odd, 1, keepdims=False)
        self.clock.tick(send)
        self.got = grid.over_z(send, 1)

    def fourth(self):
        grid = self.grid
        got, keep = self.clock.gate(self.got, self.keep)
        held = keep + got.astype(F32)
        pair = grid.my_z // 2
        send = pick(held, 1 - pair).astype(BF16)
        self.keep = pick(held, pair)
        self.clock.tick(send)
        self.got = grid.over_z(send, 2)

    def done(self):
        got, keep = self.clock.gate(self.got, self.keep)
        out = keep + got.astype(F32)
        self.clock.tick(out)
        return out


class PlainScatter:
    def __init__(self, grid, clock, left, right):
        self.left, self.right = left, right

    def across(self):
        term = contract_rows(self.left, self.right)
        self.out = lax.psum_scatter(term, AXES, scatter_dimension=0, tiled=True)

    def first(self):
        pass

    second = third = fourth = first

    def done(self):
        return self.out


def make_scatter(grid, clock, left, right):
    plain = (left.shape[1] // grid.n_dp) % 128 or not grid.square
    kind = PlainScatter if plain else Scatter
    return kind(grid, clock, left, right)


def lookup(small_table, index_rows):
    matches = index_rows[:, None] == jnp.arange(small_table.shape[0], dtype=jnp.int32)[None, :]
    return jnp.sum(jnp.where(matches, small_table[None, :], 0), axis=1)


def rank_among(group_label, order_key):
    earlier = (group_label[None, :] == group_label[:, None]) & (
        order_key[None, :] < order_key[:, None]
    )
    return jnp.sum(earlier.astype(jnp.int32), axis=1)


def routing(lengths, deal_order, devices, row_count, device):
    slot_count = deal_order.shape[0]
    slot_ids = jnp.arange(slot_count, dtype=jnp.int32)
    starts = jnp.cumsum(lengths) - lengths
    slot_of = jnp.sum(
        jnp.where(deal_order[None, :] == slot_ids[:, None], slot_ids[None, :], 0), axis=1
    )
    slot_lengths = lookup(lengths, deal_order)
    local_rows = jnp.arange(row_count, dtype=jnp.int32)
    token_index = local_rows * devices + device
    sequence = jnp.sum((starts[None, :] <= token_index[:, None]).astype(jnp.int32), axis=1) - 1
    slot_index = lookup(slot_of, sequence)
    target = slot_index // 2
    send_rank = rank_among(target, local_rows)
    first_len = lax.dynamic_index_in_dim(slot_lengths, 2 * device, 0, False)
    second = local_rows >= first_len
    first_seq = lax.dynamic_index_in_dim(deal_order, 2 * device, 0, False)
    second_seq = lax.dynamic_index_in_dim(deal_order, 2 * device + 1, 0, False)
    sequence_here = jnp.where(second, second_seq, first_seq)
    position = local_rows - jnp.where(second, first_len, 0)
    source_token = lookup(starts, sequence_here) + position
    source = source_token % devices
    take_rank = rank_among(source, source_token)
    return target, send_rank, source, take_rank, first_len.reshape(1)


def head_probs(query, key, first_len):
    rows = query.shape[0]
    scores = back_dot(query, key) * (HEAD_DIM**-0.5)
    q_at = lax.broadcasted_iota(jnp.int32, (rows, rows), 0)
    k_at = lax.broadcasted_iota(jnp.int32, (rows, rows), 1)
    allowed = (k_at <= q_at) & ((q_at < first_len) | (k_at >= first_len))
    masked = jnp.where(allowed, scores, -1000000000.0)
    exps = jnp.exp(masked - jnp.max(masked, axis=-1, keepdims=True))
    return exps / jnp.sum(exps, axis=-1, keepdims=True)


def attend(first_len, mixed_b):
    rows, width = mixed_b.shape[0], mixed_b.shape[1] // 3
    pairs = width // (2 * HEAD_DIM)

    def kernel(first_ref, query, key, value, out):
        left = lax.broadcasted_iota(jnp.int32, (rows, 2 * HEAD_DIM), 1) < HEAD_DIM
        found = []
        for one in (left, ~left):
            q = jnp.where(one, query[...], jnp.zeros((), BF16))
            probs = head_probs(q, key[...], first_ref[0]).astype(BF16)
            found.append(jnp.dot(probs, value[...], preferred_element_type=F32))
        out[...] = jnp.where(left, *found).astype(BF16)

    def part(k):
        return pl.BlockSpec((rows, 2 * HEAD_DIM), lambda h, first: (0, k * pairs + h))

    return pl.pallas_call(
        kernel,
        out_shape=jax.ShapeDtypeStruct((rows, width), BF16),
        grid_spec=pltpu.PrefetchScalarGridSpec(
            num_scalar_prefetch=1,
            grid=(pairs,),
            in_specs=[part(0), part(1), part(2)],
            out_specs=part(0),
        ),
        compiler_params=pltpu.CompilerParams(vmem_limit_bytes=16 << 20),
        cost_estimate=pl.CostEstimate(flops=0, bytes_accessed=0, transcendentals=0),
        name="attend",
    )(first_len, mixed_b, mixed_b, mixed_b)


def attend_back(first_len, mixed_b, grad_att_b):
    rows, width = grad_att_b.shape
    pairs = width // (2 * HEAD_DIM)

    def kernel(first_ref, query, key, value, grad, out, sums):
        h = pl.program_id(0)
        scale = HEAD_DIM**-0.5
        left = lax.broadcasted_iota(jnp.int32, (rows, 2 * HEAD_DIM), 1) < HEAD_DIM
        none = jnp.zeros((), BF16)
        results = ([], [], [])
        for one in (left, ~left):
            q = jnp.where(one, query[...], none)
            g = jnp.where(one, grad[...], none)
            probs = head_probs(q, key[...], first_ref[0])
            grad_probs = back_dot(g, value[...])
            dots = jnp.sum(probs * grad_probs, axis=-1, keepdims=True)
            grad_scores = (probs * (grad_probs - dots)).astype(BF16)
            results[0].append(jnp.dot(grad_scores, key[...], preferred_element_type=F32) * scale)
            results[1].append(contract_rows(grad_scores, q) * scale)
            results[2].append(contract_rows(probs.astype(BF16), g))
        for k, both in enumerate(results):
            block = jnp.where(left, *both).astype(BF16)
            at = pl.multiple_of(k * width + h * 2 * HEAD_DIM, 2 * HEAD_DIM)
            out[:, pl.ds(at, 2 * HEAD_DIM)] = block
            total = jnp.sum(block.astype(F32), axis=0, keepdims=True)
            sums[:, pl.ds(at, 2 * HEAD_DIM)] = total

    def part(k):
        return pl.BlockSpec((rows, 2 * HEAD_DIM), lambda h, first: (0, k * pairs + h))

    return pl.pallas_call(
        kernel,
        out_shape=[
            jax.ShapeDtypeStruct((rows, 3 * width), BF16),
            jax.ShapeDtypeStruct((1, 3 * width), F32),
        ],
        grid_spec=pltpu.PrefetchScalarGridSpec(
            num_scalar_prefetch=1,
            grid=(pairs,),
            in_specs=[part(0), part(1), part(2), part(0)],
            out_specs=[
                pl.BlockSpec((rows, 3 * width), lambda h, first: (0, 0)),
                pl.BlockSpec((1, 3 * width), lambda h, first: (0, 0)),
            ],
        ),
        compiler_params=pltpu.CompilerParams(vmem_limit_bytes=16 << 20),
        cost_estimate=pl.CostEstimate(flops=0, bytes_accessed=0, transcendentals=0),
        name="attend_back",
    )(first_len, mixed_b, mixed_b, mixed_b, grad_att_b)


def standardize(values):
    centered = values - jnp.mean(values, axis=-1, keepdims=True)
    scale = lax.rsqrt(jnp.mean(centered * centered, axis=-1, keepdims=True) + EPSILON)
    return centered * scale, scale


def standardize_back(grad, unit, scale):
    return scale * (
        grad
        - jnp.mean(grad, axis=-1, keepdims=True)
        - unit * jnp.mean(grad * unit, axis=-1, keepdims=True)
    )


def col_sum(values):
    return jnp.sum(values.astype(F32), axis=0)


def on_device(
    n_dp,
    n_z,
    rows_in,
    cotangent,
    lengths,
    deal_order,
    w_qkv,
    b_query,
    b_value,
    w_out,
    b_out,
    gain_one,
    shift_one,
    w_up,
    b_up,
    w_down,
    b_down,
    gain_two,
    shift_two,
):
    grid = Grid(n_dp, n_z)
    grid.bind()
    clock = Clock()
    devices = n_dp * n_z
    row_count, _, width = rows_in.shape
    hidden = w_up.shape[1]
    share = width // devices

    early = make_lines(grid, clock, jnp.concatenate([w_qkv, w_out], axis=1))
    late = make_lines(grid, clock, w_up, w_down)
    early.step0()

    target, send_rank, source, take_rank, first_len = routing(
        lengths, deal_order, devices, row_count, grid.me
    )
    slot_rows = row_count // devices + 1
    in_rows = -(-(slot_rows + 1) // 8) * 8
    out_rows = -(-(2 * slot_rows + 1) // 8) * 8

    def selector(owner, rank, block_rows):
        at = (owner * block_rows + rank)[:, None]
        slot_ids = jnp.arange(devices * block_rows, dtype=jnp.int32)[None, :]
        return (at == slot_ids).astype(BF16)

    def is_row(block_rows, row):
        slot_ids = jnp.arange(devices * block_rows, dtype=jnp.int32)
        return (slot_ids % block_rows == row)[:, None]

    to_slots = selector(target, send_rank, in_rows)
    from_slots = selector(source, take_rank, in_rows)
    first_half = selector(source, take_rank, out_rows)
    second_half = selector(source, take_rank + slot_rows, out_rows)
    take_both = jnp.concatenate(
        [selector(target, send_rank, out_rows), selector(target, send_rank + slot_rows, out_rows)]
    )

    def swap(block):
        shape = block.shape
        block = block.reshape(devices, -1, width)
        block = lax.all_to_all(block, AXES, split_axis=0, concat_axis=0, tiled=True)
        return block.reshape(shape)

    small = jnp.concatenate(
        [b_query, b_value, b_out, gain_one, shift_one, b_down, gain_two, shift_two, b_up]
    )
    small = jnp.pad(small, (0, width - small.shape[0]))
    block = contract_rows(to_slots, rows_in.reshape(row_count, width))
    block = jnp.where(is_row(in_rows, slot_rows), small[None, :], block.astype(BF16))
    clock.tick(block)
    early.step1()
    late.step0()
    (attn,) = early.step2()
    arrived = swap(clock.gate(block))
    attn.step0()
    late.step1()
    attn.step1()
    attn.step2()
    up, down = late.step2()
    up.step0()
    attn.step3()
    arrived = clock.gate(arrived)
    inputs = jnp.dot(from_slots, arrived, preferred_element_type=F32)
    small_all = arrived.reshape(devices, in_rows, width)[:, slot_rows].astype(F32)
    vectors = [small_all[:, k * share : (k + 1) * share].reshape(width) for k in range(8)]
    bq, bv, bo, g1, s1, bd, g2, s2 = vectors
    bu = small_all[:, 8 * share : 8 * share + hidden // devices].reshape(hidden)
    unit_one, scale_one = standardize(inputs)
    normed_one_b = (unit_one * g1 + s1).astype(BF16)
    clock.tick(normed_one_b)
    full_qkv, full_out = attn.done((3 * width,))
    mixed = jnp.dot(clock.gate(normed_one_b), full_qkv, preferred_element_type=F32)
    mixed_b = (mixed + jnp.concatenate([bq, jnp.zeros_like(bq), bv])).astype(BF16)
    attended_b = attend(first_len, mixed_b)
    clock.tick(attended_b)
    up.step1()
    up.step2()
    down.step0()
    attended_b, cot_rows = clock.gate(attended_b, cotangent)
    cot_block = contract_rows(to_slots, cot_rows.reshape(row_count, width)).astype(BF16)
    clock.tick(cot_block)
    arrived_cot = swap(cot_block)
    hidden_one = inputs + jnp.dot(attended_b, full_out, preferred_element_type=F32) + bo
    unit_two, scale_two = standardize(hidden_one)
    normed_two_b = (unit_two * g2 + s2).astype(BF16)
    clock.tick(normed_two_b)

    up.step3()
    (full_up,) = up.done()
    pre_act = jnp.dot(clock.gate(normed_two_b), full_up, preferred_element_type=F32) + bu
    half_cdf = 0.5 * (1.0 + lax.erf(pre_act * (0.5**0.5)))
    activation_b = (pre_act * half_cdf).astype(BF16)
    density = jnp.exp(-0.5 * pre_act * pre_act) * ((2.0 * jnp.pi) ** -0.5)
    slope = half_cdf + pre_act * density
    clock.tick(activation_b, slope)

    arrived_cot = clock.gate(arrived_cot)
    grad_m_b = jnp.dot(from_slots, arrived_cot, preferred_element_type=F32).astype(BF16)
    clock.tick(grad_m_b)
    term_b_down = col_sum(grad_m_b)
    for_down = make_scatter(grid, clock, activation_b, grad_m_b)
    for_down.across()
    down.step1()
    down.step2()
    for_down.first()
    down.step3()
    (full_down,) = down.done()
    grad_pre_b = (back_dot(clock.gate(grad_m_b), full_down) * slope).astype(BF16)
    clock.tick(grad_pre_b)
    term_b_up = col_sum(grad_pre_b)
    for_up = make_scatter(grid, clock, normed_two_b, grad_pre_b)
    for_up.across()
    for_down.second()

    grad_normed_two = back_dot(clock.gate(grad_pre_b), full_up)
    term_g2 = col_sum(grad_normed_two * unit_two)
    term_s2 = col_sum(grad_normed_two)
    grad_hidden = grad_m_b.astype(F32) + standardize_back(grad_normed_two * g2, unit_two, scale_two)
    grad_branch_b = grad_hidden.astype(BF16)
    clock.tick(grad_branch_b)
    term_b_out = col_sum(grad_branch_b)
    for_out = make_scatter(grid, clock, attended_b, grad_branch_b)
    for_out.across()
    for_up.first()
    grad_att_b = back_dot(clock.gate(grad_branch_b), full_out).astype(BF16)
    clock.tick(grad_att_b)
    for_out.first()
    grad_mixed_b, term_mixed = attend_back(first_len, mixed_b, clock.gate(grad_att_b))
    clock.tick(grad_mixed_b)
    term_mixed = term_mixed[0]
    for_qkv = make_scatter(grid, clock, normed_one_b, grad_mixed_b)
    for_qkv.across()
    for_down.third()
    for_up.second()
    for_out.second()

    grad_normed_one = back_dot(clock.gate(grad_mixed_b), full_qkv)
    term_g1 = col_sum(grad_normed_one * unit_one)
    term_s1 = col_sum(grad_normed_one)
    grad_inputs = grad_hidden + standardize_back(grad_normed_one * g1, unit_one, scale_one)
    grad_inputs_b = grad_inputs.astype(BF16)
    clock.tick(grad_inputs_b)
    for_qkv.first()

    result = jnp.dot(clock.gate(activation_b), full_down, preferred_element_type=F32)
    result_b = (hidden_one + result + bd).astype(BF16)
    terms = [term_mixed[:width], term_mixed[2 * width :], term_b_out, term_g1, term_s1]
    terms += [term_b_down, term_g2, term_s2, term_b_up]
    terms = jnp.concatenate([v.reshape(devices, -1) for v in terms], axis=1)
    count = terms.shape[1]
    top = lax.reduce_precision(terms, 8, 7)
    small_back = jnp.concatenate([top, terms - top], axis=1).astype(BF16)
    small_back = jnp.pad(small_back, ((0, 0), (0, width - 2 * count)))
    small_back = jnp.broadcast_to(small_back[:, None], (devices, out_rows, width))
    block = contract_rows(first_half, result_b) + contract_rows(second_half, grad_inputs_b)
    last_row = is_row(out_rows, 2 * slot_rows)
    block = jnp.where(last_row, small_back.reshape(-1, width), block.astype(BF16))
    clock.tick(block)
    returned = swap(block)

    for_up.third()
    for_qkv.second()
    for_down.fourth()
    for_out.third()
    for_up.fourth()
    for_qkv.third()
    for_out.fourth()
    for_qkv.fourth()
    grad_w_down = for_down.done()
    grad_w_up = for_up.done()
    grad_w_out = for_out.done()
    returned = clock.gate(returned)
    placed = jnp.dot(take_both, returned, preferred_element_type=F32).astype(BF16)
    rows_out, grad_rows = placed[:row_count], placed[row_count:]
    sums = jnp.sum(
        returned.reshape(devices, out_rows, width)[:, 2 * slot_rows].astype(F32), axis=0
    )
    clock.tick(placed)
    grad_w_qkv = for_qkv.done()

    sums = sums[:count] + sums[count : 2 * count]
    cut = [sums[k * share : (k + 1) * share] for k in range(8)]
    grad_bq, grad_bv, grad_bo, grad_g1, grad_s1, grad_bd, grad_g2, grad_s2 = cut
    grad_bu = sums[8 * share :]
    return (
        rows_out.reshape(row_count, 1, width),
        grad_rows.reshape(row_count, 1, width),
        grad_w_qkv,
        grad_bq,
        grad_bv,
        grad_w_out,
        grad_bo,
        grad_g1,
        grad_s1,
        grad_w_up,
        grad_bu,
        grad_w_down,
        grad_bd,
        grad_g2,
        grad_s2,
    )


def solution(mesh):
    n_dp, n_z = mesh.shape["dp"], mesh.shape["fsdp"]
    rows, vec, mat = P(None, AXES, None), P(AXES), P(AXES, None)

    def run(*args):
        return on_device(n_dp, n_z, *args)

    return jax.shard_map(
        run,
        mesh=mesh,
        in_specs=(rows, rows, P(), P())
        + (mat, vec, vec, mat, vec, vec, vec, mat, vec, mat, vec, vec, vec),
        out_specs=(rows, rows, mat, vec, vec, mat, vec, vec, vec, mat, vec, mat, vec, vec, vec),
        check_vma=False,
    )
```

time: 418 us -> 407 us (0.974)
  Pallas kernels: 31.8 us -> 61.7 us
  waiting for transfers between devices: 140 us -> 112 us
  starting transfers between devices: 64.1 us -> 81.3 us
  local copies, waits for them, and re-layouts: 66.1 us -> 51.1 us
  other arithmetic: 49.1 us -> 40.5 us
  matrix products: 60.2 us -> 51.7 us
    ppermute x38 -> x28, waiting for transfers between devices: 92.8 us -> 0.82 us  [over_dp(): return lax.ppermute(value, 'dp', [(i, i ^ mask) for i in range(self.n_dp)])]
    ppermute x0 -> x21, waiting for transfers between devices: none -> 41.1 us  [crossed(): return lax.ppermute(value, 'dp', pairs)]
    pallas_call x11 -> x13, Pallas kernels: 31.8 us -> 61.7 us  [the longest x8 30.5 us: call(): pl.pallas_call(kernel, out_shape=[self.shape(d) for d in dtypes], grid_sp...]
    ppermute x38 -> x28, starting transfers between devices: 35.7 us -> 8.49 us  [over_dp(): return lax.ppermute(value, 'dp', [(i, i ^ mask) for i in range(self.n_dp)])]
    ppermute x0 -> x21, starting transfers between devices: none -> 27.2 us  [crossed(): return lax.ppermute(value, 'dp', pairs)]
    dot_general x9 -> x3, matrix products: 24.4 us -> 6.83 us  [the longest x1 2.68 us: on_device(): inputs = jnp.dot(from_slots, arrived, preferred_element_type=F32)]
    ppermute x14 -> x12, waiting for transfers between devices: 46.8 us -> 63.8 us  [over_z(): return lax.ppermute(value, 'fsdp', [(i, i ^ mask) for i in range(self.n_z)])]
    all_to_all x2 -> x3, starting transfers between devices: 8.46 us -> 23.6 us  [swap(): block = lax.all_to_all(block, AXES, split_axis=0, concat_axis=0, tiled=True)]
  transfers between devices with their start and end apart: 54 -> 64, of which waited for: 18 -> 15; matrix products, arithmetic and copies ran while one was open for 32% -> 28% of each run, Pallas kernels for 5% -> 15%
where the time goes in v3:
time: 407 us; the launch traced here: 400 us
  waiting for transfers between devices  112 us (28%)
  starting transfers between devices  81.3 us (20%)
  Pallas kernels  61.7 us (15%)
  matrix products  51.7 us (13%)
  local copies, waits for them, and re-layouts  51.1 us (13%)
  other arithmetic  40.5 us (10%)
    ppermute x12, waiting for transfers between devices, over_z(): return lax.ppermute(value, 'fsdp', [(i, i ^ mask) for i in range(self.n_z)])  63.8 us
    ppermute x21, waiting for transfers between devices, crossed(): return lax.ppermute(value, 'dp', pairs)  41.1 us
    pallas_call x8, Pallas kernels, call(): pl.pallas_call(kernel, out_shape=[self.shape(d) for d in dtypes], grid_sp...  30.5 us
    unnamed x142, local copies, waits for them, and re-layouts  30.3 us
    ppermute x21, starting transfers between devices, crossed(): return lax.ppermute(value, 'dp', pairs)  27.2 us
    all_to_all x3, starting transfers between devices, swap(): block = lax.all_to_all(block, AXES, split_axis=0, concat_axis=0, tiled=True)  23.6 us
    ppermute x12, starting transfers between devices, over_z(): return lax.ppermute(value, 'fsdp', [(i, i ^ mask) for i in range(self.n_z)])  22.1 us
    dot_general x4, matrix products, back_dot(): lax.dot_general(grad_rows, weight, (((1,), (1,)), ((), ())), preferred_el...  19.6 us
  transfers between devices with their start and end apart: 64, of which 15 were waited for; matrix products, arithmetic and copies ran while one was open for 28% of the time, Pallas kernels for 15%

profile of v3, /device:TPU:0, one launch (start us, length us, event | category | flops | bytes accessed | tf_op | source)
XLA Modules:
  0.0 399.7 jit_solution(16288380594795930417)
XLA Ops:
  1.7 4.1 %collective-permute-start = (bf16[32,4096]{1,0:T(8,128)(2,1)S(1)}, bf16[32,4096]{1,0:T(8,128)(2,1)S(1)}, u32[]{:S(2)}, u32[]{:S(2)}) collective-permute-start(bf16[32,4096]{1,0:T(8,128)(2,1)S(1)} %pad_maximum_fusion.2), channel_id=1, source_target_pairs={{0,2},{1,3},{2,0},{3,1},{4,6},{5,7},{6,4},{7,5},{8,10},{9,11},{10,... | collective-permute-start | bytes 786440 | tf_op jit(solution)/shard_map/ppermute | solution.py:41
  14.3 6.1 %concatenate.42 = bf16[384]{0:T(512)(128)(2,1)S(1)} concatenate(bf16[32]{0:T(256)(128)(2,1)} %param.22, bf16[32]{0:T(256)(128)(2,1)} %param.23, bf16[32]{0:T(256)(128)(2,1)} %param.25, bf16[32]{0:T(256)(128)(2,1)} %param.26, bf16[32]{0:T(256)(128)(2,1)} %param.27, bf16[32]{0:T(256)(128)(2,1)} %param.31, bf16[32]{0:T(256)(128)(2,1)} %param.32, bf16[32]{0:T(256)(128)(2,1)} %param.33, ...), dimensions={0} | concatenate | bytes 1536 | tf_op jit(solution)/shard_map/concatenate | solution.py:583
  24.9 20.1 %collective-permute-done.1 = bf16[64,4096]{1,0:T(8,128)(2,1)S(1)} collective-permute-done((bf16[64,4096]{1,0:T(8,128)(2,1)S(1)}, bf16[64,4096]{1,0:T(8,128)(2,1)S(1)}, u32[]{:S(2)}, u32[]{:S(2)}) %collective-permute-start.1) | collective-permute-done | bytes 524320 | tf_op jit(solution)/shard_map/ppermute | solution.py:41
  52.4 4.5 %all-to-all-start = ((bf16[32,16,1024]{2,1,0:T(8,128)(2,1)}), bf16[32,16,1024]{2,1,0:T(8,128)(2,1)}, u32[]{:S(2)}, u32[]{:S(2)}) async-start(bf16[32,16,1024]{2,1,0:T(8,128)(2,1)} %bitcast.116), calls=%async_computation | async-start | bytes 2097152 | tf_op jit(solution)/shard_map/all_to_all | solution.py:580
  56.9 17.1 %collective-permute-done.2.refs_2_ = bf16[128,4096]{1,0:T(8,128)(2,1)S(1)} collective-permute-done((bf16[128,4096]{1,0:T(8,128)(2,1)S(1)}, bf16[128,4096]{1,0:T(8,128)(2,1)S(1)}, u32[]{:S(2)}, u32[]{:S(2)}) %collective-permute-start.2) | collective-permute-done | bytes 1048608 | tf_op jit(solution)/shard_map/ppermute | solution.py:38
  76.2 11.7 %collective-permute-done.5 = bf16[64,8192]{1,0:T(8,128)(2,1)} collective-permute-done((bf16[64,8192]{1,0:T(8,128)(2,1)}, bf16[64,8192]{1,0:T(8,128)(2,1)}, u32[]{:S(2)}, u32[]{:S(2)}) %collective-permute-start.5) | collective-permute-done | bytes 1048608 | tf_op jit(solution)/shard_map/ppermute | solution.py:41
  94.1 4.5 %collective-permute-done.4.refs_6_ = bf16[128,4096]{1,0:T(8,128)(2,1)} collective-permute-done((bf16[128,4096]{1,0:T(8,128)(2,1)S(1)}, bf16[128,4096]{1,0:T(8,128)(2,1)}, u32[]{:S(2)}, u32[]{:S(2)}) %collective-permute-start.4) | collective-permute-done | bytes 1048608 | tf_op jit(solution)/shard_map/ppermute | solution.py:38
  114.9 8.7 %attend.1.left = bf16[256,1024]{1,0:T(8,128)(2,1)S(1)} custom-call(s32[1]{0:T(128)} %dynamic_slice.66.first_ref, bf16[256,3072]{1,0:T(8,128)(2,1)S(1)} %fusion.5.query.key.value, bf16[256,3072]{1,0:T(8,128)(2,1)S(1)} %fusion.5.query.key.value, bf16[256,3072]{1,0:T(8,128)(2,1)S(1)} %fusion.5.query.key.value), custom_call_target="tpu_custom_call" | custom-call | tf_op jit(solution)/shard_map/attend/pallas_call | solution.py:436
  127.7 9.4 %all-to-all-start.1 = ((bf16[32,16,1024]{2,1,0:T(8,128)(2,1)}), bf16[32,16,1024]{2,1,0:T(8,128)(2,1)}, u32[]{:S(2)}, u32[]{:S(2)}) async-start(bf16[32,16,1024]{2,1,0:T(8,128)(2,1)} %bitcast.113), calls=%async_computation.1 | async-start | bytes 2097152 | tf_op jit(solution)/shard_map/all_to_all | solution.py:580
  150.6 5.8 %fusion.4 = (f32[256,4096]{1,0:T(8,128)}, bf16[256,4096]{1,0:T(8,128)(2,1)}) fusion(f32[4096]{0:T(1024)S(1)} %slice_bitcast_fusion.2, bf16[256,1024]{1,0:T(8,128)(2,1)S(1)} %add_convert_fusion.5.left, bf16[1024,4096]{1,0:T(8,128)(2,1)S(1)} %assemble.4), kind=kOutput, calls=%fused_computation.7 | convolution fusion | flops 2159017984 | bytes 15220736 | tf_op jit(solution)/shard_map/dot_general | solution.py:629
  156.4 5.7 %all-to-all-done.1 = bf16[32,16,1024]{2,1,0:T(8,128)(2,1)} async-done(((bf16[32,16,1024]{2,1,0:T(8,128)(2,1)}), bf16[32,16,1024]{2,1,0:T(8,128)(2,1)}, u32[]{:S(2)}, u32[]{:S(2)}) %all-to-all-start.1) | async-done | bytes 1048608 | tf_op jit(solution)/shard_map/all_to_all | solution.py:580
  176.5 4.3 %outer.9 = (f32[512,1024]{1,0:T(8,128)S(1)}, f32[512,1024]{1,0:T(8,128)S(1)}, bf16[512,1024]{1,0:T(8,128)(2,1)}, bf16[512,1024]{1,0:T(8,128)(2,1)}) custom-call(s32[1]{0:T(128)} %bitcast.13.dp_ref, bf16[256,4096]{1,0:T(8,128)(2,1)S(1)} %copy-done.4, bf16[256,1024]{1,0:T(8,128)(2,1)S(1)} %convolution_convert_fusion.2.right, ...), custom_call_target="tpu_custom_call" | custom-call | tf_op jit(solution)/shard_map/outer/pallas_call | solution.py:265
  183.4 5.5 %collective-permute-done.23.refs_6_ = bf16[128,4096]{1,0:T(8,128)(2,1)S(1)} collective-permute-done((bf16[128,4096]{1,0:T(8,128)(2,1)}, bf16[128,4096]{1,0:T(8,128)(2,1)S(1)}, u32[]{:S(2)}, u32[]{:S(2)}) %collective-permute-start.23) | collective-permute-done | bytes 1048608 | tf_op jit(solution)/shard_map/ppermute | solution.py:38
  195.4 9.6 %convert_reduce_fusion = (f32[4096]{0:T(1024)}, bf16[256,4096]{1,0:T(8,128)(2,1)}) fusion(f32[256,4096]{1,0:T(8,128)} %get-tuple-element.360, bf16[256,1024]{1,0:T(8,128)(2,1)S(1)} %convolution_convert_fusion.2.right, bf16[4096,1024]{1,0:T(8,128)(2,1)S(1)} %assemble.5), kind=kOutput, calls=%fused_computation.8 | convolution fusion | flops 2151673856 | bytes 15220736 | tf_op jit(solution)/shard_map/dot_general | solution.py:226
  234.9 5.7 %outer.12 = (f32[128,4096]{1,0:T(8,128)S(1)}, f32[128,4096]{1,0:T(8,128)S(1)}, bf16[128,4096]{1,0:T(8,128)(2,1)}, bf16[128,4096]{1,0:T(8,128)(2,1)}) custom-call(s32[1]{0:T(128)} %bitcast.13.dp_ref, bf16[256,1024]{1,0:T(8,128)(2,1)S(1)} %copy-done.16, bf16[256,4096]{1,0:T(8,128)(2,1)S(1)} %copy-done.8, bf16[128,4096]{1,0:T(8,128)(2,1)S(1)} %copy-done.32, ...), custom_call_target="tpu_custom_call" | custom-call | tf_op jit(solution)/shard_map/outer/pallas_call | solution.py:265
  248.6 11.7 %attend_back.1 = (bf16[256,3072]{1,0:T(8,128)(2,1)S(1)}, f32[1,3072]{1,0:T(1,128)S(1)}) custom-call(s32[1]{0:T(128)} %dynamic_slice.66.first_ref, bf16[256,3072]{1,0:T(8,128)(2,1)S(1)} %fusion.5.query.key.value, bf16[256,3072]{1,0:T(8,128)(2,1)S(1)} %fusion.5.query.key.value, bf16[256,3072]{1,0:T(8,128)(2,1)S(1)} %fusion.5.query.key.value, ...), custom_call_target="tpu_custom_call" | custom-call | tf_op jit(solution)/shard_map/attend_back/pallas_call | solution.py:481
  276.1 6.5 %multiply_reduce_fusion.2 = (f32[1024]{0:T(1024)S(1)}, f32[256]{0:T(256)S(1)}, f32[256]{0:T(256)}, f32[1024]{0:T(1024)S(1)}, f32[256,1024]{1,0:T(8,128)}) fusion(f32[256,1024]{1,0:T(8,128)S(1)} %copy-done.48, f32[256]{0:T(256)S(1)} %add_rsqrt_fusion.1, f32[256]{0:T(256)S(1)} %broadcast_multiply_fusion.5, f32[1024]{0:T(1024)S(1)} %mul.194, ...), kind=kOutput, calls=%fused_computation.50 | convolution fusion | flops 1612969472 | bytes 9977856 | tf_op jit(solution)/shard_map/dot_general | solution.py:226
  293.7 4.8 %outer.15 = (f32[128,3072]{1,0:T(8,128)S(1)}, f32[128,3072]{1,0:T(8,128)S(1)}, bf16[128,3072]{1,0:T(8,128)(2,1)S(1)}, bf16[128,3072]{1,0:T(8,128)(2,1)}) custom-call(s32[1]{0:T(128)} %bitcast.13.dp_ref, bf16[256,1024]{1,0:T(8,128)(2,1)S(1)} %add_convert_fusion.6.left, bf16[256,3072]{1,0:T(8,128)(2,1)S(1)} %copy-done.11, ...), custom_call_target="tpu_custom_call" | custom-call | tf_op jit(solution)/shard_map/outer/pallas_call | solution.py:265
  302.7 8.1 %fusion.17 = f32[768,1024]{1,0:T(8,128)} fusion(f32[256,1024]{1,0:T(8,128)} %copy-done.49, bf16[256,4096]{1,0:T(8,128)(2,1)S(1)} %copy-done.5, bf16[4096,1024]{1,0:T(8,128)(2,1)} %copy-done.2, f32[1024]{0:T(1024)S(1)} %copy-done.62, s32[256]{0:T(256)S(1)} %copy-done.64), kind=kOutput, calls=%fused_computation.36 | convolution fusion | flops 2551119872 | bytes 14685184 | tf_op jit(solution)/shard_map/dot_general | solution.py:222
  314.6 9.7 %all-to-all-start.2 = ((bf16[32,24,1024]{2,1,0:T(8,128)(2,1)}), bf16[32,24,1024]{2,1,0:T(8,128)(2,1)}, u32[]{:S(2)}, u32[]{:S(2)}) async-start(bf16[32,24,1024]{2,1,0:T(8,128)(2,1)} %bitcast.110), calls=%async_computation.2 | async-start | bytes 3145728 | tf_op jit(solution)/shard_map/all_to_all | solution.py:580
  334.6 10.7 %collective-permute-done.46 = bf16[128,1024]{1,0:T(8,128)(2,1)S(1)} collective-permute-done((bf16[128,1024]{1,0:T(8,128)(2,1)}, bf16[128,1024]{1,0:T(8,128)(2,1)S(1)}, u32[]{:S(2)}, u32[]{:S(2)}) %collective-permute-start.46) | collective-permute-done | bytes 262176 | tf_op jit(solution)/shard_map/ppermute | solution.py:38
  352.0 16.2 %collective-permute-done.55 = bf16[2,32,4096]{2,1,0:T(8,128)(2,1)S(1)} collective-permute-done((bf16[2,32,4096]{2,1,0:T(8,128)(2,1)S(1)}, bf16[2,32,4096]{2,1,0:T(8,128)(2,1)S(1)}, u32[]{:S(2)}, u32[]{:S(2)}) %collective-permute-start.55) | collective-permute-done | bytes 524320 | tf_op jit(solution)/shard_map/ppermute | solution.py:41
  370.6 4.4 %collective-permute-start.56 = (bf16[32,1024]{1,0:T(8,128)(2,1)S(1)}, bf16[32,1024]{1,0:T(8,128)(2,1)S(1)}, u32[]{:S(2)}, u32[]{:S(2)}) collective-permute-start(bf16[32,1024]{1,0:T(8,128)(2,1)S(1)} %fusion.39), channel_id=1, source_target_pairs={{0,2},{1,3},{2,0},{3,1},{4,6},{5,7},{6,4},{7,5},{8,10},{9,11},{10,... | collective-permute-start | bytes 196616 | tf_op jit(solution)/shard_map/ppermute | solution.py:41
  375.0 12.9 %collective-permute-done.59 = bf16[2,32,3072]{2,1,0:T(8,128)(2,1)S(1)} collective-permute-done((bf16[2,32,3072]{2,1,0:T(8,128)(2,1)S(1)}, bf16[2,32,3072]{2,1,0:T(8,128)(2,1)S(1)}, u32[]{:S(2)}, u32[]{:S(2)}) %collective-permute-start.59) | collective-permute-done | bytes 393248 | tf_op jit(solution)/shard_map/ppermute | solution.py:41
  (382 shorter events, 189.8 us)
Async XLA Ops:
  45.1 28.9 %collective-permute-start.2 = (bf16[128,4096]{1,0:T(8,128)(2,1)S(1)}, bf16[128,4096]{1,0:T(8,128)(2,1)S(1)}, u32[]{:S(2)}, u32[]{:S(2)}) collective-permute-start(bf16[128,4096]{1,0:T(8,128)(2,1)S(1)} %constant_dynamic-update-slice_fusion.2.refs_0_), channel_id=1, source_target_pairs={{0,8},{4,20},{8,0},{12,28},{16,24},{20,4},{24,16},{28,12},{1,9},{5... | collective-permute-start | bytes 3145736 | tf_op jit(solution)/shard_map/ppermute | solution.py:38
  46.7 28.9 %collective-permute-start.6 = (bf16[128,4096]{1,0:T(8,128)(2,1)S(1)}, bf16[128,4096]{1,0:T(8,128)(2,1)}, u32[]{:S(2)}, u32[]{:S(2)}) collective-permute-start(bf16[128,4096]{1,0:T(8,128)(2,1)S(1)} %constant_dynamic-update-slice_fusion.2.refs_0_), channel_id=1, source_target_pairs={{0,16},{4,12},{8,24},{12,4},{16,0},{20,28},{24,8},{28,20},{1,17},{... | collective-permute-start | bytes 3145736 | tf_op jit(solution)/shard_map/ppermute | solution.py:38
  51.6 36.2 %collective-permute-start.5 = (bf16[64,8192]{1,0:T(8,128)(2,1)}, bf16[64,8192]{1,0:T(8,128)(2,1)}, u32[]{:S(2)}, u32[]{:S(2)}) collective-permute-start(bf16[64,8192]{1,0:T(8,128)(2,1)} %constant_dynamic-update-slice_fusion.5), channel_id=1, source_target_pairs={{0,1},{1,0},{2,3},{3,2},{4,5},{5,4},{6,7},{7,6},{8,9},{9,8},{10,11... | collective-permute-start | bytes 3145736 | tf_op jit(solution)/shard_map/ppermute | solution.py:41
  52.4 52.2 %collective-permute-start.7 = (bf16[128,4096]{1,0:T(8,128)(2,1)S(1)}, bf16[128,4096]{1,0:T(8,128)(2,1)}, u32[]{:S(2)}, u32[]{:S(2)}) collective-permute-start(bf16[128,4096]{1,0:T(8,128)(2,1)S(1)} %constant_dynamic-update-slice_fusion.2.refs_0_), channel_id=1, source_target_pairs={{0,4},{4,0},{8,12},{12,8},{16,20},{20,16},{24,28},{28,24},{1,5},{5... | collective-permute-start | bytes 3145736 | tf_op jit(solution)/shard_map/ppermute | solution.py:34
  52.4 46.2 %all-to-all-start = ((bf16[32,16,1024]{2,1,0:T(8,128)(2,1)}), bf16[32,16,1024]{2,1,0:T(8,128)(2,1)}, u32[]{:S(2)}, u32[]{:S(2)}) async-start(bf16[32,16,1024]{2,1,0:T(8,128)(2,1)} %bitcast.116), calls=%async_computation | async-start | bytes 2097152 | tf_op jit(solution)/shard_map/all_to_all | solution.py:580
  75.6 32.2 %collective-permute-start.8 = (bf16[128,4096]{1,0:T(8,128)(2,1)S(1)}, bf16[128,4096]{1,0:T(8,128)(2,1)}, u32[]{:S(2)}, u32[]{:S(2)}) collective-permute-start(bf16[128,4096]{1,0:T(8,128)(2,1)S(1)} %collective-permute-done.2.refs_2_), channel_id=1, source_target_pairs={{0,4},{4,0},{8,12},{12,8},{16,20},{20,16},{24,28},{28,24},{1,5},{5... | collective-permute-start | bytes 3145736 | tf_op jit(solution)/shard_map/ppermute | solution.py:34
  75.6 31.6 %collective-permute-start.9 = (bf16[128,4096]{1,0:T(8,128)(2,1)}, bf16[128,4096]{1,0:T(8,128)(2,1)}, u32[]{:S(2)}, u32[]{:S(2)}) collective-permute-start(bf16[128,4096]{1,0:T(8,128)(2,1)} %collective-permute-done.6.refs_4_), channel_id=1, source_target_pairs={{0,4},{4,0},{8,12},{12,8},{16,20},{20,16},{24,28},{28,24},{1,5},{5... | collective-permute-start | bytes 3145736 | tf_op jit(solution)/shard_map/ppermute | solution.py:34
  92.6 31.1 %collective-permute-start.12 = (bf16[128,4096]{1,0:T(8,128)(2,1)}, bf16[128,4096]{1,0:T(8,128)(2,1)}, u32[]{:S(2)}, u32[]{:S(2)}) collective-permute-start(bf16[128,4096]{1,0:T(8,128)(2,1)} %pad_maximum_fusion.refs_0_), channel_id=1, source_target_pairs={{0,8},{4,20},{8,0},{12,28},{16,24},{20,4},{24,16},{28,12},{1,9},{5... | collective-permute-start | bytes 3145736 | tf_op jit(solution)/shard_map/ppermute | solution.py:38
  107.3 35.1 %collective-permute-start.13 = (bf16[128,4096]{1,0:T(8,128)(2,1)}, bf16[128,4096]{1,0:T(8,128)(2,1)}, u32[]{:S(2)}, u32[]{:S(2)}) collective-permute-start(bf16[128,4096]{1,0:T(8,128)(2,1)} %pad_maximum_fusion.refs_0_), channel_id=1, source_target_pairs={{0,4},{4,0},{8,12},{12,8},{16,20},{20,16},{24,28},{28,24},{1,5},{5... | collective-permute-start | bytes 3145736 | tf_op jit(solution)/shard_map/ppermute | solution.py:34
  127.7 34.4 %all-to-all-start.1 = ((bf16[32,16,1024]{2,1,0:T(8,128)(2,1)}), bf16[32,16,1024]{2,1,0:T(8,128)(2,1)}, u32[]{:S(2)}, u32[]{:S(2)}) async-start(bf16[32,16,1024]{2,1,0:T(8,128)(2,1)} %bitcast.113), calls=%async_computation.1 | async-start | bytes 2097152 | tf_op jit(solution)/shard_map/all_to_all | solution.py:580
  140.7 32.5 %collective-permute-start.19 = (bf16[128,4096]{1,0:T(8,128)(2,1)}, bf16[128,4096]{1,0:T(8,128)(2,1)}, u32[]{:S(2)}, u32[]{:S(2)}) collective-permute-start(bf16[128,4096]{1,0:T(8,128)(2,1)} %pad_maximum_fusion.1.refs_0_), channel_id=1, source_target_pairs={{0,8},{4,20},{8,0},{12,28},{16,24},{20,4},{24,16},{28,12},{1,9},{5... | collective-permute-start | bytes 3145736 | tf_op jit(solution)/shard_map/ppermute | solution.py:38
  142.4 31.5 %collective-permute-start.21 = (bf16[128,4096]{1,0:T(8,128)(2,1)}, bf16[128,4096]{1,0:T(8,128)(2,1)}, u32[]{:S(2)}, u32[]{:S(2)}) collective-permute-start(bf16[128,4096]{1,0:T(8,128)(2,1)} %pad_maximum_fusion.1.refs_0_), channel_id=1, source_target_pairs={{0,16},{4,12},{8,24},{12,4},{16,0},{20,28},{24,8},{28,20},{1,17},{... | collective-permute-start | bytes 3145736 | tf_op jit(solution)/shard_map/ppermute | solution.py:38
  191.0 74.7 %collective-permute-start.41 = (bf16[512,1024]{1,0:T(8,128)(2,1)}, bf16[512,1024]{1,0:T(8,128)(2,1)}, u32[]{:S(2)}, u32[]{:S(2)}) collective-permute-start(bf16[512,1024]{1,0:T(8,128)(2,1)} %get-tuple-element.235), channel_id=1, source_target_pairs={{0,16},{4,12},{8,24},{12,4},{16,0},{20,28},{24,8},{28,20},{1,17},{... | collective-permute-start | bytes 3145736 | tf_op jit(solution)/shard_map/ppermute | solution.py:38
  217.0 49.1 %collective-permute-start.40 = (bf16[512,1024]{1,0:T(8,128)(2,1)}, bf16[512,1024]{1,0:T(8,128)(2,1)}, u32[]{:S(2)}, u32[]{:S(2)}) collective-permute-start(bf16[512,1024]{1,0:T(8,128)(2,1)} %add_convert_fusion.2), channel_id=1, source_target_pairs={{0,8},{4,20},{8,0},{12,28},{16,24},{20,4},{24,16},{28,12},{1,9},{5... | collective-permute-start | bytes 3145736 | tf_op jit(solution)/shard_map/ppermute | solution.py:38
  273.5 50.8 %collective-permute-start.51 = (bf16[128,4096]{1,0:T(8,128)(2,1)}, bf16[128,4096]{1,0:T(8,128)(2,1)}, u32[]{:S(2)}, u32[]{:S(2)}) collective-permute-start(bf16[128,4096]{1,0:T(8,128)(2,1)} %get-tuple-element.269), channel_id=1, source_target_pairs={{0,16},{4,12},{8,24},{12,4},{16,0},{20,28},{24,8},{28,20},{1,17},{... | collective-permute-start | bytes 3145736 | tf_op jit(solution)/shard_map/ppermute | solution.py:38
  288.5 44.2 %collective-permute-start.48 = (bf16[2,128,1024]{2,1,0:T(8,128)(2,1)}, bf16[2,128,1024]{2,1,0:T(8,128)(2,1)}, u32[]{:S(2)}, u32[]{:S(2)}) collective-permute-start(bf16[2,128,1024]{2,1,0:T(8,128)(2,1)} %fusion.18), channel_id=1, source_target_pairs={{0,1},{1,0},{2,3},{3,2},{4,5},{5,4},{6,7},{7,6},{8,9},{9,8},{10,11... | collective-permute-start | bytes 1572872 | tf_op jit(solution)/shard_map/ppermute | solution.py:41
  290.3 44.3 %collective-permute-start.47 = (bf16[128,1024]{1,0:T(8,128)(2,1)}, bf16[128,1024]{1,0:T(8,128)(2,1)}, u32[]{:S(2)}, u32[]{:S(2)}) collective-permute-start(bf16[128,1024]{1,0:T(8,128)(2,1)} %copy-done.44), channel_id=1, source_target_pairs={{0,16},{4,12},{8,24},{12,4},{16,0},{20,28},{24,8},{28,20},{1,17},{... | collective-permute-start | bytes 786440 | tf_op jit(solution)/shard_map/ppermute | solution.py:38
  291.2 35.0 %collective-permute-start.50 = (bf16[128,4096]{1,0:T(8,128)(2,1)}, bf16[128,4096]{1,0:T(8,128)(2,1)}, u32[]{:S(2)}, u32[]{:S(2)}) collective-permute-start(bf16[128,4096]{1,0:T(8,128)(2,1)} %add_convert_fusion.1), channel_id=1, source_target_pairs={{0,8},{4,20},{8,0},{12,28},{16,24},{20,4},{24,16},{28,12},{1,9},{5... | collective-permute-start | bytes 3145736 | tf_op jit(solution)/shard_map/ppermute | solution.py:38
  301.7 28.0 %collective-permute-start.49 = (bf16[128,3072]{1,0:T(8,128)(2,1)}, bf16[128,3072]{1,0:T(8,128)(2,1)}, u32[]{:S(2)}, u32[]{:S(2)}) collective-permute-start(bf16[128,3072]{1,0:T(8,128)(2,1)} %get-tuple-element.307), channel_id=1, source_target_pairs={{0,16},{4,12},{8,24},{12,4},{16,0},{20,28},{24,8},{28,20},{1,17},{... | collective-permute-start | bytes 2359304 | tf_op jit(solution)/shard_map/ppermute | solution.py:38
  314.6 77.0 %all-to-all-start.2 = ((bf16[32,24,1024]{2,1,0:T(8,128)(2,1)}), bf16[32,24,1024]{2,1,0:T(8,128)(2,1)}, u32[]{:S(2)}, u32[]{:S(2)}) async-start(bf16[32,24,1024]{2,1,0:T(8,128)(2,1)} %bitcast.110), calls=%async_computation.2 | async-start | bytes 3145728 | tf_op jit(solution)/shard_map/all_to_all | solution.py:580
  326.2 42.2 %collective-permute-start.54 = (bf16[128,3072]{1,0:T(8,128)(2,1)S(1)}, bf16[128,3072]{1,0:T(8,128)(2,1)S(1)}, u32[]{:S(2)}, u32[]{:S(2)}) collective-permute-start(bf16[128,3072]{1,0:T(8,128)(2,1)S(1)} %copy-done.43), channel_id=1, source_target_pairs={{0,16},{4,12},{8,24},{12,4},{16,0},{20,28},{24,8},{28,20},{1,17},{... | collective-permute-start | bytes 2359304 | tf_op jit(solution)/shard_map/ppermute | solution.py:38
  329.8 38.4 %collective-permute-start.55 = (bf16[2,32,4096]{2,1,0:T(8,128)(2,1)S(1)}, bf16[2,32,4096]{2,1,0:T(8,128)(2,1)S(1)}, u32[]{:S(2)}, u32[]{:S(2)}) collective-permute-start(bf16[2,32,4096]{2,1,0:T(8,128)(2,1)S(1)} %fusion.19), channel_id=1, source_target_pairs={{0,1},{1,0},{2,3},{3,2},{4,5},{5,4},{6,7},{7,6},{8,9},{9,8},{10,11... | collective-permute-start | bytes 1572872 | tf_op jit(solution)/shard_map/ppermute | solution.py:41
  332.7 35.8 %collective-permute-start.53 = (bf16[128,3072]{1,0:T(8,128)(2,1)S(1)}, bf16[128,3072]{1,0:T(8,128)(2,1)S(1)}, u32[]{:S(2)}, u32[]{:S(2)}) collective-permute-start(bf16[128,3072]{1,0:T(8,128)(2,1)S(1)} %add_convert_fusion.3), channel_id=1, source_target_pairs={{0,8},{4,20},{8,0},{12,28},{16,24},{20,4},{24,16},{28,12},{1,9},{5... | collective-permute-start | bytes 2359304 | tf_op jit(solution)/shard_map/ppermute | solution.py:38
  346.4 42.8 %collective-permute-start.58 = (bf16[128,1024]{1,0:T(8,128)(2,1)S(1)}, bf16[128,1024]{1,0:T(8,128)(2,1)S(1)}, u32[]{:S(2)}, u32[]{:S(2)}) collective-permute-start(bf16[128,1024]{1,0:T(8,128)(2,1)S(1)} %fusion.27), channel_id=1, source_target_pairs={{0,2},{1,3},{2,0},{3,1},{4,6},{5,7},{6,4},{7,5},{8,10},{9,11},{10,... | collective-permute-start | bytes 786440 | tf_op jit(solution)/shard_map/ppermute | solution.py:41
  (107 other events, 1605.6 us)
